TPU v7x, 128 devices: a whole 4x4x4 slice. The times are simulated.
128 devices in a mesh: gx: 8 (over y, core), gy: 16 (over z, x).
Axes of the slice: x: 4, y: 4, z: 4, core: 2. Of those that a mesh axis runs over, the one named last changes fastest.
Arguments:
- raw_window: float32 [8192, 16384], P('gx', 'gy'), may hold values from -6 to 6
- source_ids: int32 [256], P(('gx', 'gy')), may hold values from 0 to 8191, as said below
- pair_source: int32 [16384], P(('gx', 'gy')), may hold values from 0 to 255
- pair_holder: int32 [16384, 1], P(('gx', 'gy')), may hold values from 0 to 127; in each aligned block of 128 rows (0 to 127, 128 to 255, ...) at most 2 rows name the same one
- pair_receiver: int32 [16384], P(('gx', 'gy')), may hold values from 0 to 63
Outputs:
- correlations: float32 [16384, 512], P(('gx', 'gy'))
Inputs may be any that keep to these rules, and one draw needn't show every extreme that they name: The ids are distinct, and source k is a channel of the device that holds channels from (k // 2) * 64 on: source_ids[k] // 64 == k // 2. `pair_holder`: among the 128 pairs of one device, at most 2 name the same holder, a bound that some block reaches; every device is named by some pair.
All inputs are finite; a program needn't handle non-finite values.
Results may differ from a plain program's by a relative error of at most 0.0095.
Values may be sent and summed in bfloat16 or wider, within the bound.
No kernel may reach another device: no remote copies, remote signals or barrier semaphores. Data moves between devices by JAX's collectives and lax.ppermute only.
A program may use at most 128 MiB of HBM per device.

v0:
```python
import math

import jax
import jax.numpy as jnp
from jax import lax
from jax.experimental import pallas as pl
from jax.experimental.pallas import tpu as pltpu
from jax.sharding import PartitionSpec as P


NBIN = 2048
SEGLEN = 4096
NSEG = 4
BAND = 64
NLAG = 512
SIDE = 4
RADIX = 16
INNER = SEGLEN // RADIX
LANES = 128
HALF_ROWS = 2 * (RADIX // 2)


def split_table(table):
    upper = table.astype(jnp.bfloat16)
    lower = (table - upper.astype(jnp.float32)).astype(jnp.bfloat16)
    return (upper, lower)


def lane_bins():
    lane = jnp.arange(LANES, dtype=jnp.int32)
    return 4 * (lane % 32) + lane // 32


def inner_table():
    times = jnp.arange(INNER, dtype=jnp.int32)
    low = lane_bins()
    high = INNER - 1 - low
    turn = 2.0 * math.pi / INNER

    def block(bins, sign):
        angle = (times[:, None] * bins[None, :] % INNER).astype(jnp.float32) * turn
        cos, sin = jnp.cos(angle), jnp.sin(angle)
        top = jnp.concatenate([cos, -sign * sin], axis=1)
        bottom = jnp.concatenate([sin, sign * cos], axis=1)
        return jnp.concatenate([top, bottom], axis=0)

    return split_table(jnp.concatenate([block(low, 1.0), block(high, -1.0)], axis=1))


def twiddle_table():
    rows = jnp.arange(RADIX, dtype=jnp.int32)
    times = jnp.arange(INNER, dtype=jnp.int32)
    angle = (rows[:, None] * times[None, :] % SEGLEN).astype(jnp.float32) * (2.0 * math.pi / SEGLEN)
    return jnp.stack([jnp.cos(angle), -jnp.sin(angle)], axis=0)


def turns(count, lags):
    angle = (count[:, None] * lags[None, :] % SEGLEN).astype(jnp.float32) * (2.0 * math.pi / SEGLEN)
    return jnp.cos(angle), jnp.sin(angle)


def inverse_table(core, zero):
    outer = core * (RADIX // 2) + jnp.arange(RADIX // 2, dtype=jnp.int32)
    inner = RADIX * lane_bins() + zero
    lags = (jnp.arange(NLAG, dtype=jnp.int32) - NLAG // 2) % SEGLEN
    (c1, s1), (c2, s2) = lax.optimization_barrier((turns(outer, lags), turns(inner, lags)))
    c1, s1, c2, s2 = c1[:, None], s1[:, None], c2[None], s2[None]
    bins = outer[:, None, None] + inner[None, :, None]
    weight = jnp.where(bins == 0, 1.0, 2.0).astype(jnp.float32) * (0.5 / math.sqrt(NSEG * NBIN))
    table = jnp.stack([weight * (c1 * c2 - s1 * s2), -weight * (s1 * c2 + c1 * s2)], axis=0)
    return table.astype(jnp.bfloat16).reshape(NBIN, NLAG)


def real_dft(values):
    n = len(values)
    if n == 2:
        return [(values[0] + values[1], None), (values[0] - values[1], None)]
    even = real_dft(values[0::2])
    odd = real_dft(values[1::2])
    out = [None] * (n // 2 + 1)
    for k in range(n // 4 + 1):
        er, ei = even[k]
        pr, pi = odd[k]
        c, s = math.cos(2 * math.pi * k / n), math.sin(2 * math.pi * k / n)
        if k == 0:
            out[0] = (er + pr, None)
            out[n // 2] = (er - pr, None)
        elif 4 * k == n:
            out[k] = (er, -pr)
        else:
            if 8 * k == n:
                tr, ti = (pr + pi) * c, (pi - pr) * c
            else:
                tr, ti = pr * c + pi * s, pi * c - pr * s
            out[k] = (er + tr, ei + ti)
            out[n // 2 - k] = (er - tr, ti - ei)
    return out


def whiten_kernel(core_ref, x_ref, tw_ref, upper_ref, lower_ref, mine_ref, other_ref, hi_ref, lo_ref, out_ref):
    rows = x_ref.shape[1]
    slices = []
    for t in range(RADIX):
        q, u = t // SIDE, t % SIDE
        slices.append(x_ref[q, :, u * INNER:(u + 1) * INNER].astype(jnp.float32))
    outer = real_dft(slices)
    for f in range(RADIX // 2 + 1):
        re, im = outer[f]
        c, s = tw_ref[0, f:f + 1, :], tw_ref[1, f:f + 1, :]
        if f == 0:
            pair = (re, jnp.zeros_like(re))
        elif im is None:
            pair = (re * c, re * s)
        else:
            pair = (re * c - im * s, re * s + im * c)
        for k in range(2):
            hi = pair[k].astype(jnp.bfloat16)
            hi_ref[f * rows:(f + 1) * rows, k * INNER:(k + 1) * INNER] = hi
            lo_ref[f * rows:(f + 1) * rows, k * INNER:(k + 1) * INNER] = (pair[k] - hi.astype(jnp.float32)).astype(jnp.bfloat16)
    hi, lo = hi_ref[...], lo_ref[...]
    upper, lower = upper_ref[...], lower_ref[...]
    spectrum = jnp.dot(hi, upper, preferred_element_type=jnp.float32)
    spectrum += jnp.dot(hi, lower, preferred_element_type=jnp.float32)
    spectrum += jnp.dot(lo, upper, preferred_element_type=jnp.float32)

    def part(f, k):
        g, base = (f, 0) if f <= RADIX // 2 else (RADIX - f, 2)
        return spectrum[g * rows:(g + 1) * rows, (base + k) * LANES:(base + k + 1) * LANES]

    power = None
    for f in range(RADIX):
        re, im = part(f, 0), part(f, 1)
        both = re * re + im * im
        power = both if power is None else power + both
    power = power + pltpu.roll(power, 64, 1)
    power = power + pltpu.roll(power, 32, 1)
    scale = 1.0 / jnp.sqrt(power * (1.0 / BAND) + 1e-06)
    for f in range(RADIX):
        for k in range(2):
            index = (f // 8) * HALF_ROWS + k * 8 + f % 8
            out_ref[:, index, :] = part(f, k) * scale
    core = core_ref[0]
    mine_ref[...] = out_ref[:, pl.ds(pl.multiple_of(core * HALF_ROWS, HALF_ROWS), HALF_ROWS), :].astype(jnp.bfloat16)
    other_ref[...] = out_ref[:, pl.ds(pl.multiple_of((1 - core) * HALF_ROWS, HALF_ROWS), HALF_ROWS), :].astype(jnp.bfloat16)


def whiten(core, samples, twiddle, upper, lower):
    samples = pltpu.with_memory_space_constraint(samples, pltpu.MemorySpace.HBM)
    rows = samples.shape[1]
    out = jax.ShapeDtypeStruct((rows, NSEG * HALF_ROWS, LANES), jnp.bfloat16)
    spec = pl.BlockSpec((rows, HALF_ROWS, LANES), lambda s, c: (0, s, 0))
    count = RADIX // 2 + 1
    return pl.pallas_call(
        whiten_kernel,
        out_shape=(out, out),
        grid_spec=pltpu.PrefetchScalarGridSpec(
            num_scalar_prefetch=1,
            grid=(NSEG,),
            in_specs=[
                pl.BlockSpec((SIDE, rows, SEGLEN // SIDE), lambda s, c: (s, 0, 0)),
                pl.BlockSpec((2, RADIX, INNER), lambda s, c: (0, 0, 0)),
                pl.BlockSpec((2 * INNER, 4 * LANES), lambda s, c: (0, 0)),
                pl.BlockSpec((2 * INNER, 4 * LANES), lambda s, c: (0, 0)),
            ],
            out_specs=(spec, spec),
            scratch_shapes=[
                pltpu.VMEM((count * rows, 2 * INNER), jnp.bfloat16),
                pltpu.VMEM((count * rows, 2 * INNER), jnp.bfloat16),
                pltpu.VMEM((rows, 2 * HALF_ROWS, LANES), jnp.float32),
            ],
        ),
        compiler_params=pltpu.CompilerParams(vmem_limit_bytes=48 << 20),
        name="whiten",
    )(core, samples, twiddle, upper, lower)


GROUP = 8
CHUNK = 128


def load_pieces(pieces, targets, sems):
    copies = []
    n = 0
    for group, target in zip(pieces, targets):
        at = 0
        for piece in group:
            copies.append(pltpu.make_async_copy(piece, target.at[at:at + piece.shape[0]], sems.at[n]))
            at += piece.shape[0]
            n += 1
    for copy in copies:
        copy.start()
    return copies


def cross_slots(count, src_ref, rcv_ref, row_of, sources_ref, receivers_ref, cross_ref):
    def group(g, carry):
        for u in range(GROUP):
            i = g * GROUP + u
            a = sources_ref[src_ref[i]].astype(jnp.float32)
            b = receivers_ref[rcv_ref[i]].astype(jnp.float32)
            re = im = None
            for s in range(NSEG):
                ar, ai = a[s * 16:s * 16 + 8], a[s * 16 + 8:s * 16 + 16]
                br, bi = b[s * 16:s * 16 + 8], b[s * 16 + 8:s * 16 + 16]
                r = ar * br + ai * bi
                m = ai * br - ar * bi
                re = r if re is None else re + r
                im = m if im is None else im + m
            row = row_of(i)
            cross_ref[row, 0:8, :] = re
            cross_ref[row, 8:16, :] = im
        return carry

    lax.fori_loop(0, (count + GROUP - 1) // GROUP, group, 0)


def lags_of(cross_ref, first, table_ref):
    cross = jnp.concatenate(
        [cross_ref[pl.ds(first, CHUNK), g, :].astype(jnp.bfloat16) for g in range(HALF_ROWS)], axis=1
    )
    return jnp.dot(cross, table_ref[...], preferred_element_type=jnp.float32)


def near_kernel(count_ref, src_ref, rcv_ref, slot_ref, *refs):
    pieces = refs[:8]
    table_ref, out_ref, sources_ref, receivers_ref, cross_ref, sems = refs[8:]
    copies = load_pieces((pieces[:6], pieces[6:]), (sources_ref, receivers_ref), sems)
    cross_ref[...] = jnp.zeros_like(cross_ref)
    for copy in copies:
        copy.wait()
    cross_slots(count_ref[0], src_ref, rcv_ref, lambda i: slot_ref[i], sources_ref, receivers_ref, cross_ref)
    for c in range(out_ref.shape[0] // CHUNK):
        out_ref[c * CHUNK:(c + 1) * CHUNK, :] = lags_of(cross_ref, c * CHUNK, table_ref)


def far_kernel(count_ref, src_ref, rcv_ref, slot_ref, *refs):
    pieces = refs[:4]
    table_ref, near_ref, out_ref, sources_ref, receivers_ref, cross_ref, rows_ref, product_ref, sems = refs[4:]
    copies = load_pieces((pieces[:2], pieces[2:]), (sources_ref, receivers_ref), sems)
    slots = out_ref.shape[0]
    rows_ref[0:slots, :] = near_ref[...]
    for copy in copies:
        copy.wait()
    count = count_ref[0]
    cross_slots(count, src_ref, rcv_ref, lambda i: i, sources_ref, receivers_ref, cross_ref)

    def chunk(c, carry):
        first = pl.multiple_of(c * CHUNK, CHUNK)
        product_ref[...] = lags_of(cross_ref, first, table_ref)

        def place(g, inner):
            for u in range(GROUP):
                i = g * GROUP + u
                rows_ref[pl.ds(slot_ref[first + i], 1), :] = product_ref[pl.ds(i, 1), :]
            return inner

        return lax.fori_loop(0, (jnp.minimum(count - first, CHUNK) + GROUP - 1) // GROUP, place, carry)

    lax.fori_loop(0, (count + CHUNK - 1) // CHUNK, chunk, 0)
    out_ref[...] = rows_ref[0:slots, :].astype(jnp.bfloat16)


def correlate(kernel, lists, pieces, receivers, blocks, dtype, extra):
    slots = lists[1].shape[0]
    row = pieces[0].shape[1:]
    whole = lambda a: pl.BlockSpec(a.shape, lambda *_: (0,) * a.ndim)
    return pl.pallas_call(
        kernel,
        out_shape=jax.ShapeDtypeStruct((slots, NLAG), dtype),
        grid_spec=pltpu.PrefetchScalarGridSpec(
            num_scalar_prefetch=4,
            grid=(1,),
            in_specs=[pl.BlockSpec(memory_space=pl.ANY)] * (len(pieces) + len(receivers)) + [whole(b) for b in blocks],
            out_specs=pl.BlockSpec((slots, NLAG), lambda *_: (0, 0)),
            scratch_shapes=[
                pltpu.VMEM((sum(p.shape[0] for p in pieces),) + row, jnp.bfloat16),
                pltpu.VMEM((sum(p.shape[0] for p in receivers),) + row, jnp.bfloat16),
                pltpu.VMEM((slots + GROUP, HALF_ROWS, LANES), jnp.float32),
                *extra,
                pltpu.SemaphoreType.DMA((len(pieces) + len(receivers),)),
            ],
        ),
        compiler_params=pltpu.CompilerParams(vmem_limit_bytes=40 << 20),
    )(*lists, *pieces, *receivers, *blocks)


def pick_kernel(wanted_ref, raw_ref, taper_ref, out_ref, rows_ref, sems):
    rows = rows_ref.shape[0]
    copies = [
        pltpu.make_async_copy(raw_ref.at[pl.ds(wanted_ref[r], 1), :], rows_ref.at[pl.ds(r, 1), :], sems.at[r])
        for r in range(rows)
    ]
    for copy in copies:
        copy.start()
    for copy in copies:
        copy.wait()
    value = (rows_ref[...] * taper_ref[...]).astype(jnp.bfloat16)
    for g in range(out_ref.shape[0]):
        out_ref[g] = value


def pick_rows(wanted, raw_window, taper, copies):
    rows, span = wanted.shape[0], raw_window.shape[1]
    return pl.pallas_call(
        pick_kernel,
        out_shape=jax.ShapeDtypeStruct((copies, rows, span), jnp.bfloat16),
        grid_spec=pltpu.PrefetchScalarGridSpec(
            num_scalar_prefetch=1,
            grid=(1,),
            in_specs=[pl.BlockSpec(memory_space=pl.ANY), pl.BlockSpec((1, span), lambda *_: (0, 0))],
            out_specs=pl.BlockSpec((copies, rows, span), lambda *_: (0, 0, 0)),
            scratch_shapes=[pltpu.VMEM((rows, span), jnp.float32), pltpu.SemaphoreType.DMA((rows,))],
        ),
        name="pick",
    )(wanted, raw_window, taper.reshape(1, span))


def taper_kernel(raw_ref, taper_ref, out_ref):
    out_ref[...] = (raw_ref[...] * taper_ref[...]).astype(jnp.bfloat16)


def taper_rows(raw_window, taper):
    rows, span = raw_window.shape
    block = rows // 8
    return pl.pallas_call(
        taper_kernel,
        out_shape=jax.ShapeDtypeStruct((rows, span), jnp.bfloat16),
        grid=(rows // block,),
        in_specs=[pl.BlockSpec((block, span), lambda i: (i, 0)), pl.BlockSpec((1, span), lambda i: (0, 0))],
        out_specs=pl.BlockSpec((block, span), lambda i: (i, 0)),
        name="taper",
    )(raw_window, taper.reshape(1, span))


def shift(value, axis, step):
    if axis == "core":
        return lax.ppermute(value, "gx", [(g, g ^ 1) for g in range(2 * SIDE)])
    if axis == "y":
        return lax.ppermute(value, "gx", [(g, (g + 2 * step) % (2 * SIDE)) for g in range(2 * SIDE)])
    if axis == "z":
        return lax.ppermute(value, "gy", [(g, (g + SIDE * step) % (SIDE * SIDE)) for g in range(SIDE * SIDE)])
    return lax.ppermute(value, "gy", [(g, g // SIDE * SIDE + (g + step) % SIDE) for g in range(SIDE * SIDE)])


def gather_ring(value, axis):
    return jnp.stack([value] + [shift(value, axis, d) for d in (1, 2, 3)], axis=0)


def program(raw_window, source_ids, pair_source, pair_holder, pair_receiver):
    groups = lax.axis_size("gy")
    devices = lax.axis_size("gx") * groups
    gx, gy = lax.axis_index("gx"), lax.axis_index("gy")
    place = {"core": gx % 2, "y": gx // 2, "z": gy // SIDE, "x": gy % SIDE}
    core = place["core"]
    here = gx * groups + gy
    span = raw_window.shape[1]
    channels = raw_window.shape[0] // groups
    sample = (gy * span + jnp.arange(span, dtype=jnp.int32)) % SEGLEN
    taper = jnp.sin(math.pi * (sample.astype(jnp.float32) + 0.5) / SEGLEN) ** 2

    pairs = pair_source.shape[0]
    per = source_ids.shape[0]
    holder = pair_holder[:, 0]
    order = jnp.arange(pairs, dtype=jnp.int32)
    same = (holder[:, None] == holder[None, :]) & (order[None, :] < order[:, None])
    rank = jnp.sum(same.astype(jnp.int32), axis=1)
    packed = ((holder * 2 + rank) * channels + pair_receiver) * 256 + pair_source
    notes = jnp.concatenate([packed, source_ids - gx * groups * channels])
    notes = gather_ring(notes, "x")
    notes = gather_ring(notes, "z")
    ids, notes = notes[:, :, pairs:].reshape(groups, per), notes[:, :, :pairs]

    step = jnp.arange(groups, dtype=jnp.int32)
    mate = (place["z"] - step // SIDE) % SIDE * SIDE + (place["x"] - step % SIDE) % SIDE
    wanted = jnp.sum(jnp.where(mate[None, :, None] == step[:, None, None], ids[None], 0), axis=1).reshape(-1)
    first = pick_rows(wanted, raw_window, taper, groups)
    first = lax.all_to_all(first, "gy", split_axis=0, concat_axis=0, tiled=True)
    tapered = taper_rows(raw_window, taper)
    samples = lax.all_to_all(tapered.reshape(groups, channels, span), "gy", split_axis=0, concat_axis=0, tiled=True)
    notes = gather_ring(notes, "y")
    notes = jnp.stack([notes, shift(notes, "core", 1)], axis=0).reshape(devices, pairs)

    twiddle = twiddle_table()
    upper, lower = inner_table()
    near0, away = whiten(core.reshape(1), first, twiddle, upper, lower)
    near1 = shift(away, "core", 1)
    ahead0 = shift(near0, "y", 1)
    behind0 = shift(near0, "y", 3)
    ahead1 = shift(near1, "y", 1)
    behind1 = shift(near1, "y", 3)
    far0 = shift(ahead0, "y", 1)
    far1 = shift(behind1, "y", 3)

    notes, late, _ = lax.optimization_barrier((notes, core, near1))
    table = inverse_table(late, late - core)

    mine, other = whiten(core.reshape(1), samples, twiddle, upper, lower)
    sister = shift(other, "core", 1)

    dev = jnp.arange(devices, dtype=jnp.int32)
    own = (
        (((dev // 64) ^ late) + (place["y"] - dev // 16 % SIDE) % SIDE * 2) * groups
        + (place["z"] - dev // SIDE % SIDE) % SIDE * SIDE
        + (place["x"] - dev % SIDE) % SIDE
    )
    key = notes // (channels * 256)
    low = notes % (channels * 256)
    kinds = jnp.stack([here * 2, here * 2 + 1, (here ^ groups) * 2, (here ^ groups) * 2 + 1])
    found = jnp.sum(jnp.where(key[None] == kinds[:, None, None], low[None] + 1, 0), axis=2)
    asked = jnp.sum(jnp.where(own[None, None, :] == dev[None, :, None], found[:, None, :], 0), axis=2)
    valid = asked > 0
    asked = jnp.maximum(asked - 1, 0)
    slots = asked.size
    source_no = asked % 256
    source_gx = source_no // (2 * groups)
    rel_y = (place["y"] - source_gx // 2) % SIDE
    far = rel_y == 2
    piece = jnp.where(far, 0, jnp.minimum(rel_y, 2))
    source_at = (piece * 2 + (source_gx % 2 ^ core)) * (2 * groups) + source_no % (2 * groups)
    kind = jnp.arange(4, dtype=jnp.int32)[:, None]
    slot_no = dev[None, :] * 4 + kind
    receiver_at = asked // 256 + kind // 2 * channels
    entry = ((slot_no - slots) * 256 + receiver_at) * 256 + source_at
    index = jnp.arange(slots, dtype=jnp.int32)

    def compact(chosen):
        chosen = chosen.reshape(-1)
        spot = jnp.sum((chosen[None, :] & (index[None, :] < index[:, None])).astype(jnp.int32), axis=1)
        hit = chosen[None, :] & (spot[None, :] == index[:, None])
        line = jnp.sum(jnp.where(hit, entry.reshape(1, -1), 0), axis=1) + slots * 65536
        return jnp.sum(chosen.astype(jnp.int32)).reshape(1), line % 256, line // 256 % 256, line // 65536

    near_lists = compact(valid & ~far)
    far_lists = compact(valid & far)

    receivers = [mine, sister]
    near = correlate(
        near_kernel, near_lists, [near0, near1, ahead0, ahead1, behind0, behind1], receivers, [table], jnp.float32, []
    )
    extra = [pltpu.VMEM((slots + GROUP, NLAG), jnp.float32), pltpu.VMEM((CHUNK, NLAG), jnp.float32)]
    partial = correlate(far_kernel, far_lists, [far0, far1], receivers, [table, near], jnp.bfloat16, extra)
    returned = lax.all_to_all(partial.reshape(devices, 4, NLAG), ("gx", "gy"), split_axis=0, concat_axis=0, tiled=True)
    returned = returned.reshape(devices * 4, NLAG)
    row = jnp.arange(4 * devices, dtype=jnp.int32)
    row_dev, row_rel, row_rank = row // 4, row // 2 % 2, row % 2
    row_holder = jnp.where(row_rel == 0, row_dev, row_dev ^ groups)
    pick = (row_holder[None, :] == holder[:, None]) & (row_rank[None, :] == rank[:, None])
    return jnp.dot(pick.astype(jnp.bfloat16), returned, preferred_element_type=jnp.float32)


def solution(mesh):
    return jax.shard_map(
        program,
        mesh=mesh,
        in_specs=(
            P("gx", "gy"),
            P(("gx", "gy")),
            P(("gx", "gy")),
            P(("gx", "gy"), None),
            P(("gx", "gy")),
        ),
        out_specs=P(("gx", "gy"), None),
        check_vma=False,
    )
```

profile of v0, /device:TPU:1, one launch (start us, length us, event | category | flops | bytes accessed | tf_op | source)
XLA Modules:
  0.0 143.0 jit_solution(18173005244810475806)
XLA Ops:
  2.3 2.1 %collective-permute-start = (s32[130]{0:T(256)S(1)}, s32[130]{0:T(256)S(1)}, u32[]{:S(2)}, u32[]{:S(2)}) collective-permute-start(s32[130]{0:T(256)S(1)} %pad_add_fusion.4), channel_id=1, source_target_pairs={{0,1},{1,2},{2,3},{3,0},{4,5},{5,6},{6,7},{7,4},{8,9},{9,10},{10,1... | collective-permute-start | bytes 1568 | tf_op jit(solution)/shard_map/ppermute | solution.py:342
  4.4 2.5 %collective-permute-start.1 = (s32[130]{0:T(256)S(1)}, s32[130]{0:T(256)S(1)}, u32[]{:S(2)}, u32[]{:S(2)}) collective-permute-start(s32[130]{0:T(256)S(1)} %pad_add_fusion.4), channel_id=1, source_target_pairs={{0,2},{1,3},{2,0},{3,1},{4,6},{5,7},{6,4},{7,5},{8,10},{9,11},{10,... | collective-permute-start | bytes 1568 | tf_op jit(solution)/shard_map/ppermute | solution.py:342
  6.8 1.2 collective-permute-start.2
  9.6 1.7 %collective-permute-start.3 = (s32[4,130]{1,0:T(4,128)S(1)}, s32[4,130]{1,0:T(4,128)S(1)}, u32[]{:S(2)}, u32[]{:S(2)}) collective-permute-start(s32[4,130]{1,0:T(4,128)S(1)} %get-tuple-element.41), channel_id=1, source_target_pairs={{0,4},{1,5},{2,6},{3,7},{4,8},{5,9},{6,10},{7,11},{8,12},{9,13},{1... | collective-permute-start | bytes 6248 | tf_op jit(solution)/shard_map/ppermute | solution.py:341
  11.3 3.3 %collective-permute-start.4 = (s32[4,130]{1,0:T(4,128)S(1)}, s32[4,130]{1,0:T(4,128)S(1)}, u32[]{:S(2)}, u32[]{:S(2)}) collective-permute-start(s32[4,130]{1,0:T(4,128)S(1)} %get-tuple-element.41), channel_id=1, source_target_pairs={{0,8},{1,9},{2,10},{3,11},{4,12},{5,13},{6,14},{7,15},{8,0},{9,1},... | collective-permute-start | bytes 6248 | tf_op jit(solution)/shard_map/ppermute | solution.py:341
  15.6 1.4 collective-permute-done.5
  18.0 3.6 %pick.1 = bf16[16,32,1024]{2,1,0:T(8,128)(2,1)} custom-call(s32[32]{0:T(128)} %reshape.804.wanted_ref, f32[1024,1024]{1,0:T(8,128)} %raw_ref.3, f32[1,1024]{1,0:T(1,128)} %fusion.58.taper_ref), custom_call_target="tpu_custom_call" | custom-call | tf_op jit(solution)/shard_map/pick/pallas_call | solution.py:304
  21.6 5.1 %all-to-all-start = ((bf16[16,32,1024]{2,1,0:T(8,128)(2,1)}), bf16[16,32,1024]{2,1,0:T(8,128)(2,1)S(1)}, u32[]{:S(2)}, u32[]{:S(2)}) async-start(bf16[16,32,1024]{2,1,0:T(8,128)(2,1)} %pick.1), calls=%async_computation | async-start | bytes 2097152 | tf_op jit(solution)/shard_map/all_to_all | solution.py:377
  26.7 6.2 %taper.1 = bf16[1024,1024]{1,0:T(8,128)(2,1)} custom-call(f32[1024,1024]{1,0:T(8,128)} %raw_ref.3, f32[1,1024]{1,0:T(1,128)} %fusion.58.taper_ref), custom_call_target="tpu_custom_call" | custom-call | tf_op jit(solution)/shard_map/taper/pallas_call | solution.py:325
  33.0 1.0 broadcast_multiply_fusion.1
  34.2 6.1 %all-to-all-done.x_ref = bf16[16,32,1024]{2,1,0:T(8,128)(2,1)S(1)} async-done(((bf16[16,32,1024]{2,1,0:T(8,128)(2,1)}), bf16[16,32,1024]{2,1,0:T(8,128)(2,1)S(1)}, u32[]{:S(2)}, u32[]{:S(2)}) %all-to-all-start) | async-done | bytes 1048608 | tf_op jit(solution)/shard_map/all_to_all | solution.py:377
  41.3 4.4 %all-to-all-start.1 = ((bf16[16,64,1024]{2,1,0:T(8,128)(2,1)}), bf16[16,64,1024]{2,1,0:T(8,128)(2,1)}, u32[]{:S(2)}, u32[]{:S(2)}) async-start(bf16[16,64,1024]{2,1,0:T(8,128)(2,1)} %bitcast.29), calls=%async_computation.1 | async-start | bytes 4194304 | tf_op jit(solution)/shard_map/all_to_all | solution.py:379
  45.7 6.6 %whiten.2 = (bf16[32,64,128]{2,1,0:T(8,128)(2,1)}, bf16[32,64,128]{2,1,0:T(8,128)(2,1)S(1)}) custom-call(s32[1]{0:T(128)} %bitcast.16.core_ref, bf16[16,32,1024]{2,1,0:T(8,128)(2,1)} %copy-done, f32[2,16,256]{2,1,0:T(8,128)S(1)} %pad_maximum_fusion.1.tw_ref, bf16[512,512]{1,0:T(8,128)(2,1)S(1)} %fusion.11.upper_ref, ...), custom_call_target="tpu_custom_call" | custom-call | tf_op jit(solution)/shard_map/whiten/pallas_call | solution.py:153
  52.3 5.1 %collective-permute-start.10 = (bf16[32,64,128]{2,1,0:T(8,128)(2,1)S(1)}, bf16[32,64,128]{2,1,0:T(8,128)(2,1)}, u32[]{:S(2)}, u32[]{:S(2)}) collective-permute-start(bf16[32,64,128]{2,1,0:T(8,128)(2,1)S(1)} %get-tuple-element.15), channel_id=1, source_target_pairs={{0,16},{16,0},{32,48},{48,32},{64,80},{80,64},{96,112},{112,96},{1... | collective-permute-start | bytes 1572872 | tf_op jit(solution)/shard_map/ppermute | solution.py:337
  57.4 1.3 collective-permute-start.6
  58.7 2.6 %collective-permute-start.7 = (s32[4,4,128]{2,1,0:T(4,128)S(1)}, s32[4,4,128]{2,1,0:T(4,128)S(1)}, u32[]{:S(2)}, u32[]{:S(2)}) collective-permute-start(s32[4,4,128]{2,1,0:T(4,128)S(1)} %get-tuple-element.39), channel_id=1, source_target_pairs={{0,64},{16,80},{32,96},{48,112},{64,0},{80,16},{96,32},{112,48},{1... | collective-permute-start | bytes 24584 | tf_op jit(solution)/shard_map/ppermute | solution.py:339
  61.3 1.1 collective-permute-start.8
  63.1 1.1 collective-permute-done.8
  64.3 1.5 %collective-permute-start.9 = (s32[4,4,4,128]{3,2,1,0:T(4,128)S(1)}, s32[4,4,4,128]{3,2,1,0:T(4,128)S(1)}, u32[]{:S(2)}, u32[]{:S(2)}) collective-permute-start(s32[4,4,4,128]{3,2,1,0:T(4,128)S(1)} %get-tuple-element.37), channel_id=1, source_target_pairs={{0,16},{16,0},{32,48},{48,32},{64,80},{80,64},{96,112},{112,96},{1... | collective-permute-start | bytes 98312 | tf_op jit(solution)/shard_map/ppermute | solution.py:337
  66.6 2.7 %collective-permute-start.17 = (bf16[32,64,128]{2,1,0:T(8,128)(2,1)}, bf16[32,64,128]{2,1,0:T(8,128)(2,1)}, u32[]{:S(2)}, u32[]{:S(2)}) collective-permute-start(bf16[32,64,128]{2,1,0:T(8,128)(2,1)} %get-tuple-element.18.refs_0_), channel_id=1, source_target_pairs={{0,96},{16,112},{32,0},{48,16},{64,32},{80,48},{96,64},{112,80},{1... | collective-permute-start | bytes 1572872 | tf_op jit(solution)/shard_map/ppermute | solution.py:339
  69.4 1.1 fusion.18
  70.6 1.1 collective-permute-start.13
  72.1 9.1 %collective-permute-done.11.refs_2_ = bf16[32,64,128]{2,1,0:T(8,128)(2,1)} collective-permute-done((bf16[32,64,128]{2,1,0:T(8,128)(2,1)}, bf16[32,64,128]{2,1,0:T(8,128)(2,1)}, u32[]{:S(2)}, u32[]{:S(2)}) %collective-permute-start.11) | collective-permute-done | bytes 524320 | tf_op jit(solution)/shard_map/ppermute | solution.py:339
  83.0 9.9 %whiten.3 = (bf16[64,64,128]{2,1,0:T(8,128)(2,1)S(1)}, bf16[64,64,128]{2,1,0:T(8,128)(2,1)S(1)}) custom-call(s32[1]{0:T(128)} %bitcast.16.core_ref, bf16[16,64,1024]{2,1,0:T(8,128)(2,1)} %all-to-all-done.1.x_ref, f32[2,16,256]{2,1,0:T(8,128)S(1)} %pad_maximum_fusion.1.tw_ref, bf16[512,512]{1,0:T(8,128)(2,1)S(1)} %fusion.11.upper_ref, ...), custom_call_target="tpu_custom_call" | custom-call | tf_op jit(solution)/shard_map/whiten/pallas_call | solution.py:153
  92.8 2.1 %collective-permute-start.15 = (bf16[64,64,128]{2,1,0:T(8,128)(2,1)S(1)}, bf16[64,64,128]{2,1,0:T(8,128)(2,1)S(1)}, u32[]{:S(2)}, u32[]{:S(2)}) collective-permute-start(bf16[64,64,128]{2,1,0:T(8,128)(2,1)S(1)} %get-tuple-element.20), channel_id=1, source_target_pairs={{0,16},{16,0},{32,48},{48,32},{64,80},{80,64},{96,112},{112,96},{1... | collective-permute-start | bytes 3145736 | tf_op jit(solution)/shard_map/ppermute | solution.py:337
  95.7 3.0 %collective-permute-start.14 = (bf16[32,64,128]{2,1,0:T(8,128)(2,1)}, bf16[32,64,128]{2,1,0:T(8,128)(2,1)S(1)}, u32[]{:S(2)}, u32[]{:S(2)}) collective-permute-start(bf16[32,64,128]{2,1,0:T(8,128)(2,1)} %collective-permute-done.13.refs_5_), channel_id=1, source_target_pairs={{0,96},{16,112},{32,0},{48,16},{64,32},{80,48},{96,64},{112,80},{1... | collective-permute-start | bytes 1572872 | tf_op jit(solution)/shard_map/ppermute | solution.py:339
  99.5 8.7 %shard_map.55.refs_5_ = f32[512,512]{1,0:T(8,128)S(1)} custom-call(s32[1]{0:T(128)} %bitcast.31.count_ref, s32[512]{0:T(512)S(1)} %get-tuple-element.47.src_ref, s32[512]{0:T(512)S(1)} %get-tuple-element.48.rcv_ref, s32[512]{0:T(512)S(1)} %get-tuple-element.46.slot_ref, bf16[32,64,128]{2,1,0:T(8,128)(2,1)} %get-tuple-element.18.refs_0_, ...), custom_call_target="tpu_custom_call" | custom-call | tf_op jit(solution)/shard_map/pallas_call | solution.py:267
  108.2 2.1 %collective-permute-done.14.refs_1_ = bf16[32,64,128]{2,1,0:T(8,128)(2,1)S(1)} collective-permute-done((bf16[32,64,128]{2,1,0:T(8,128)(2,1)}, bf16[32,64,128]{2,1,0:T(8,128)(2,1)S(1)}, u32[]{:S(2)}, u32[]{:S(2)}) %collective-permute-start.14) | collective-permute-done | bytes 524320 | tf_op jit(solution)/shard_map/ppermute | solution.py:339
  110.3 4.1 %shard_map.56 = bf16[512,512]{1,0:T(8,128)(2,1)S(1)} custom-call(s32[1]{0:T(128)} %bitcast.22.count_ref, s32[512]{0:T(512)S(1)} %get-tuple-element.50.src_ref, s32[512]{0:T(512)S(1)} %get-tuple-element.51.rcv_ref, s32[512]{0:T(512)S(1)} %get-tuple-element.49.slot_ref, bf16[32,64,128]{2,1,0:T(8,128)(2,1)} %collective-permute-done.12.refs_0_, ...), custom_call_target="tpu_custom_call" | custom-call | tf_op jit(solution)/shard_map/pallas_call | solution.py:267
  115.4 12.4 %all-to-all-start.2 = ((bf16[128,4,512]{2,1,0:T(4,128)(2,1)}), bf16[128,4,512]{2,1,0:T(4,128)(2,1)S(1)}, u32[]{:S(2)}, u32[]{:S(2)}) async-start(bf16[128,4,512]{2,1,0:T(4,128)(2,1)} %reshape.808), calls=%async_computation.2 | async-start | bytes 1048576 | tf_op jit(solution)/shard_map/all_to_all | solution.py:442
  127.8 14.1 %all-to-all-done.2 = bf16[128,4,512]{2,1,0:T(4,128)(2,1)S(1)} async-done(((bf16[128,4,512]{2,1,0:T(4,128)(2,1)}), bf16[128,4,512]{2,1,0:T(4,128)(2,1)S(1)}, u32[]{:S(2)}, u32[]{:S(2)}) %all-to-all-start.2) | async-done | bytes 524320 | tf_op jit(solution)/shard_map/all_to_all | solution.py:442
  142.0 1.0 fusion.7
  (73 shorter events, 13.4 us)
Async XLA Ops:
  2.3 6.5 %collective-permute-start = (s32[130]{0:T(256)S(1)}, s32[130]{0:T(256)S(1)}, u32[]{:S(2)}, u32[]{:S(2)}) collective-permute-start(s32[130]{0:T(256)S(1)} %pad_add_fusion.4), channel_id=1, source_target_pairs={{0,1},{1,2},{2,3},{3,0},{4,5},{5,6},{6,7},{7,4},{8,9},{9,10},{10,1... | collective-permute-start | bytes 1568 | tf_op jit(solution)/shard_map/ppermute | solution.py:342
  4.4 4.4 %collective-permute-start.1 = (s32[130]{0:T(256)S(1)}, s32[130]{0:T(256)S(1)}, u32[]{:S(2)}, u32[]{:S(2)}) collective-permute-start(s32[130]{0:T(256)S(1)} %pad_add_fusion.4), channel_id=1, source_target_pairs={{0,2},{1,3},{2,0},{3,1},{4,6},{5,7},{6,4},{7,5},{8,10},{9,11},{10,... | collective-permute-start | bytes 1568 | tf_op jit(solution)/shard_map/ppermute | solution.py:342
  6.8 2.7 %collective-permute-start.2 = (s32[130]{0:T(256)S(1)}, s32[130]{0:T(256)S(1)}, u32[]{:S(2)}, u32[]{:S(2)}) collective-permute-start(s32[130]{0:T(256)S(1)} %pad_add_fusion.4), channel_id=1, source_target_pairs={{0,3},{1,0},{2,1},{3,2},{4,7},{5,4},{6,5},{7,6},{8,11},{9,8},{10,9... | collective-permute-start | bytes 1568 | tf_op jit(solution)/shard_map/ppermute | solution.py:342
  9.6 5.7 %collective-permute-start.3 = (s32[4,130]{1,0:T(4,128)S(1)}, s32[4,130]{1,0:T(4,128)S(1)}, u32[]{:S(2)}, u32[]{:S(2)}) collective-permute-start(s32[4,130]{1,0:T(4,128)S(1)} %get-tuple-element.41), channel_id=1, source_target_pairs={{0,4},{1,5},{2,6},{3,7},{4,8},{5,9},{6,10},{7,11},{8,12},{9,13},{1... | collective-permute-start | bytes 6248 | tf_op jit(solution)/shard_map/ppermute | solution.py:341
  11.3 4.3 %collective-permute-start.4 = (s32[4,130]{1,0:T(4,128)S(1)}, s32[4,130]{1,0:T(4,128)S(1)}, u32[]{:S(2)}, u32[]{:S(2)}) collective-permute-start(s32[4,130]{1,0:T(4,128)S(1)} %get-tuple-element.41), channel_id=1, source_target_pairs={{0,8},{1,9},{2,10},{3,11},{4,12},{5,13},{6,14},{7,15},{8,0},{9,1},... | collective-permute-start | bytes 6248 | tf_op jit(solution)/shard_map/ppermute | solution.py:341
  14.6 2.5 %collective-permute-start.5 = (s32[4,130]{1,0:T(4,128)S(1)}, s32[4,130]{1,0:T(4,128)S(1)}, u32[]{:S(2)}, u32[]{:S(2)}) collective-permute-start(s32[4,130]{1,0:T(4,128)S(1)} %get-tuple-element.41), channel_id=1, source_target_pairs={{0,12},{1,13},{2,14},{3,15},{4,0},{5,1},{6,2},{7,3},{8,4},{9,5},{1... | collective-permute-start | bytes 6248 | tf_op jit(solution)/shard_map/ppermute | solution.py:341
  21.6 18.7 %all-to-all-start = ((bf16[16,32,1024]{2,1,0:T(8,128)(2,1)}), bf16[16,32,1024]{2,1,0:T(8,128)(2,1)S(1)}, u32[]{:S(2)}, u32[]{:S(2)}) async-start(bf16[16,32,1024]{2,1,0:T(8,128)(2,1)} %pick.1), calls=%async_computation | async-start | bytes 2097152 | tf_op jit(solution)/shard_map/all_to_all | solution.py:377
  40.3 1.0 copy-start
  41.3 41.7 %all-to-all-start.1 = ((bf16[16,64,1024]{2,1,0:T(8,128)(2,1)}), bf16[16,64,1024]{2,1,0:T(8,128)(2,1)}, u32[]{:S(2)}, u32[]{:S(2)}) async-start(bf16[16,64,1024]{2,1,0:T(8,128)(2,1)} %bitcast.29), calls=%async_computation.1 | async-start | bytes 4194304 | tf_op jit(solution)/shard_map/all_to_all | solution.py:379
  52.3 17.0 %collective-permute-start.10 = (bf16[32,64,128]{2,1,0:T(8,128)(2,1)S(1)}, bf16[32,64,128]{2,1,0:T(8,128)(2,1)}, u32[]{:S(2)}, u32[]{:S(2)}) collective-permute-start(bf16[32,64,128]{2,1,0:T(8,128)(2,1)S(1)} %get-tuple-element.15), channel_id=1, source_target_pairs={{0,16},{16,0},{32,48},{48,32},{64,80},{80,64},{96,112},{112,96},{1... | collective-permute-start | bytes 1572872 | tf_op jit(solution)/shard_map/ppermute | solution.py:337
  57.4 5.0 %collective-permute-start.6 = (s32[4,4,128]{2,1,0:T(4,128)S(1)}, s32[4,4,128]{2,1,0:T(4,128)S(1)}, u32[]{:S(2)}, u32[]{:S(2)}) collective-permute-start(s32[4,4,128]{2,1,0:T(4,128)S(1)} %get-tuple-element.39), channel_id=1, source_target_pairs={{0,32},{16,48},{32,64},{48,80},{64,96},{80,112},{96,0},{112,16},{1... | collective-permute-start | bytes 24584 | tf_op jit(solution)/shard_map/ppermute | solution.py:339
  58.7 4.4 %collective-permute-start.7 = (s32[4,4,128]{2,1,0:T(4,128)S(1)}, s32[4,4,128]{2,1,0:T(4,128)S(1)}, u32[]{:S(2)}, u32[]{:S(2)}) collective-permute-start(s32[4,4,128]{2,1,0:T(4,128)S(1)} %get-tuple-element.39), channel_id=1, source_target_pairs={{0,64},{16,80},{32,96},{48,112},{64,0},{80,16},{96,32},{112,48},{1... | collective-permute-start | bytes 24584 | tf_op jit(solution)/shard_map/ppermute | solution.py:339
  61.3 2.9 %collective-permute-start.8 = (s32[4,4,128]{2,1,0:T(4,128)S(1)}, s32[4,4,128]{2,1,0:T(4,128)S(1)}, u32[]{:S(2)}, u32[]{:S(2)}) collective-permute-start(s32[4,4,128]{2,1,0:T(4,128)S(1)} %get-tuple-element.39), channel_id=1, source_target_pairs={{0,96},{16,112},{32,0},{48,16},{64,32},{80,48},{96,64},{112,80},{1... | collective-permute-start | bytes 24584 | tf_op jit(solution)/shard_map/ppermute | solution.py:339
  64.3 2.3 %collective-permute-start.9 = (s32[4,4,4,128]{3,2,1,0:T(4,128)S(1)}, s32[4,4,4,128]{3,2,1,0:T(4,128)S(1)}, u32[]{:S(2)}, u32[]{:S(2)}) collective-permute-start(s32[4,4,4,128]{3,2,1,0:T(4,128)S(1)} %get-tuple-element.37), channel_id=1, source_target_pairs={{0,16},{16,0},{32,48},{48,32},{64,80},{80,64},{96,112},{112,96},{1... | collective-permute-start | bytes 98312 | tf_op jit(solution)/shard_map/ppermute | solution.py:337
  66.6 14.7 %collective-permute-start.11 = (bf16[32,64,128]{2,1,0:T(8,128)(2,1)}, bf16[32,64,128]{2,1,0:T(8,128)(2,1)}, u32[]{:S(2)}, u32[]{:S(2)}) collective-permute-start(bf16[32,64,128]{2,1,0:T(8,128)(2,1)} %get-tuple-element.18.refs_0_), channel_id=1, source_target_pairs={{0,32},{16,48},{32,64},{48,80},{64,96},{80,112},{96,0},{112,16},{1... | collective-permute-start | bytes 1572872 | tf_op jit(solution)/shard_map/ppermute | solution.py:339
  66.6 32.8 %collective-permute-start.17 = (bf16[32,64,128]{2,1,0:T(8,128)(2,1)}, bf16[32,64,128]{2,1,0:T(8,128)(2,1)}, u32[]{:S(2)}, u32[]{:S(2)}) collective-permute-start(bf16[32,64,128]{2,1,0:T(8,128)(2,1)} %get-tuple-element.18.refs_0_), channel_id=1, source_target_pairs={{0,96},{16,112},{32,0},{48,16},{64,32},{80,48},{96,64},{112,80},{1... | collective-permute-start | bytes 1572872 | tf_op jit(solution)/shard_map/ppermute | solution.py:339
  70.6 25.1 %collective-permute-start.13 = (bf16[32,64,128]{2,1,0:T(8,128)(2,1)}, bf16[32,64,128]{2,1,0:T(8,128)(2,1)}, u32[]{:S(2)}, u32[]{:S(2)}) collective-permute-start(bf16[32,64,128]{2,1,0:T(8,128)(2,1)} %collective-permute-done.10.refs_1_), channel_id=1, source_target_pairs={{0,96},{16,112},{32,0},{48,16},{64,32},{80,48},{96,64},{112,80},{1... | collective-permute-start | bytes 1572872 | tf_op jit(solution)/shard_map/ppermute | solution.py:339
  71.7 27.7 %collective-permute-start.16 = (bf16[32,64,128]{2,1,0:T(8,128)(2,1)}, bf16[32,64,128]{2,1,0:T(8,128)(2,1)}, u32[]{:S(2)}, u32[]{:S(2)}) collective-permute-start(bf16[32,64,128]{2,1,0:T(8,128)(2,1)} %collective-permute-done.10.refs_1_), channel_id=1, source_target_pairs={{0,32},{16,48},{32,64},{48,80},{64,96},{80,112},{96,0},{112,16},{1... | collective-permute-start | bytes 1572872 | tf_op jit(solution)/shard_map/ppermute | solution.py:339
  81.3 27.0 %collective-permute-start.12 = (bf16[32,64,128]{2,1,0:T(8,128)(2,1)}, bf16[32,64,128]{2,1,0:T(8,128)(2,1)}, u32[]{:S(2)}, u32[]{:S(2)}) collective-permute-start(bf16[32,64,128]{2,1,0:T(8,128)(2,1)} %collective-permute-done.11.refs_2_), channel_id=1, source_target_pairs={{0,32},{16,48},{32,64},{48,80},{64,96},{80,112},{96,0},{112,16},{1... | collective-permute-start | bytes 1572872 | tf_op jit(solution)/shard_map/ppermute | solution.py:339
  92.8 6.6 %collective-permute-start.15 = (bf16[64,64,128]{2,1,0:T(8,128)(2,1)S(1)}, bf16[64,64,128]{2,1,0:T(8,128)(2,1)S(1)}, u32[]{:S(2)}, u32[]{:S(2)}) collective-permute-start(bf16[64,64,128]{2,1,0:T(8,128)(2,1)S(1)} %get-tuple-element.20), channel_id=1, source_target_pairs={{0,16},{16,0},{32,48},{48,32},{64,80},{80,64},{96,112},{112,96},{1... | collective-permute-start | bytes 3145736 | tf_op jit(solution)/shard_map/ppermute | solution.py:337
  95.7 14.6 %collective-permute-start.14 = (bf16[32,64,128]{2,1,0:T(8,128)(2,1)}, bf16[32,64,128]{2,1,0:T(8,128)(2,1)S(1)}, u32[]{:S(2)}, u32[]{:S(2)}) collective-permute-start(bf16[32,64,128]{2,1,0:T(8,128)(2,1)} %collective-permute-done.13.refs_5_), channel_id=1, source_target_pairs={{0,96},{16,112},{32,0},{48,16},{64,32},{80,48},{96,64},{112,80},{1... | collective-permute-start | bytes 1572872 | tf_op jit(solution)/shard_map/ppermute | solution.py:339
  114.4 27.6 %copy-start.1 = (s32[128,1]{0,1:T(1,128)S(1)}, s32[128,1]{0,1:T(1,128)}, u32[]{:S(2)}) copy-start(s32[128,1]{0,1:T(1,128)} %param.8) | copy-start | bytes 1540
  115.4 26.5 %all-to-all-start.2 = ((bf16[128,4,512]{2,1,0:T(4,128)(2,1)}), bf16[128,4,512]{2,1,0:T(4,128)(2,1)S(1)}, u32[]{:S(2)}, u32[]{:S(2)}) async-start(bf16[128,4,512]{2,1,0:T(4,128)(2,1)} %reshape.808), calls=%async_computation.2 | async-start | bytes 1048576 | tf_op jit(solution)/shard_map/all_to_all | solution.py:442
where the time goes:
time: 144 us; the launch traced here: 143 us
  starting transfers between devices  54.3 us (38%)
  Pallas kernels  39.1 us (27%)
  waiting for transfers between devices  36.5 us (25%)
  other arithmetic  8.95 us (6%)
  local copies, waits for them, and re-layouts  2.84 us (2%)
    pallas_call x2, Pallas kernels, whiten(): pl.pallas_call(whiten_kernel, out_shape=(out, out), grid_spec=pltpu.Prefe...  16.5 us
    all_to_all x1, waiting for transfers between devices, program(): lax.all_to_all(partial.reshape(devices, 4, NLAG), ('gx', 'gy'), split_axi...  14.1 us
    ppermute x9, waiting for transfers between devices, shift(): lax.ppermute(value, 'gx', [(g, (g + 2 * step) % (2 * SIDE)) for g in rang...  13.1 us
    pallas_call x2, Pallas kernels, correlate(): pl.pallas_call(kernel, out_shape=jax.ShapeDtypeStruct((slots, NLAG), dtyp...  12.9 us
    all_to_all x1, starting transfers between devices, program(): lax.all_to_all(partial.reshape(devices, 4, NLAG), ('gx', 'gy'), split_axi...  12.4 us
    ppermute x9, starting transfers between devices, shift(): lax.ppermute(value, 'gx', [(g, (g + 2 * step) % (2 * SIDE)) for g in rang...  12.2 us
    ppermute x3, starting transfers between devices, shift(): return lax.ppermute(value, 'gx', [(g, g ^ 1) for g in range(2 * SIDE)])  8.69 us
    pallas_call x1, Pallas kernels, taper_rows(): pl.pallas_call(taper_kernel, out_shape=jax.ShapeDtypeStruct((rows, span),...  6.16 us
  transfers between devices with their start and end apart: 21, of which 10 were waited for; matrix products, arithmetic and copies ran while one was open for 5% of the time, Pallas kernels for 22%

commit v1 on v0

--- a/solution.py
+++ b/solution.py
@@ -315,23 +315,6 @@
     )(wanted, raw_window, taper.reshape(1, span))
 
 
-def taper_kernel(raw_ref, taper_ref, out_ref):
-    out_ref[...] = (raw_ref[...] * taper_ref[...]).astype(jnp.bfloat16)
-
-
-def taper_rows(raw_window, taper):
-    rows, span = raw_window.shape
-    block = rows // 8
-    return pl.pallas_call(
-        taper_kernel,
-        out_shape=jax.ShapeDtypeStruct((rows, span), jnp.bfloat16),
-        grid=(rows // block,),
-        in_specs=[pl.BlockSpec((block, span), lambda i: (i, 0)), pl.BlockSpec((1, span), lambda i: (0, 0))],
-        out_specs=pl.BlockSpec((block, span), lambda i: (i, 0)),
-        name="taper",
-    )(raw_window, taper.reshape(1, span))
-
-
 def shift(value, axis, step):
     if axis == "core":
         return lax.ppermute(value, "gx", [(g, g ^ 1) for g in range(2 * SIDE)])
@@ -375,7 +358,7 @@
     wanted = jnp.sum(jnp.where(mate[None, :, None] == step[:, None, None], ids[None], 0), axis=1).reshape(-1)
     first = pick_rows(wanted, raw_window, taper, groups)
     first = lax.all_to_all(first, "gy", split_axis=0, concat_axis=0, tiled=True)
-    tapered = taper_rows(raw_window, taper)
+    tapered = (raw_window * taper[None, :]).astype(jnp.bfloat16)
     samples = lax.all_to_all(tapered.reshape(groups, channels, span), "gy", split_axis=0, concat_axis=0, tiled=True)
     notes = gather_ring(notes, "y")
     notes = jnp.stack([notes, shift(notes, "core", 1)], axis=0).reshape(devices, pairs)

time: 144 us -> 144 us (level)
  Pallas kernels: 39.1 us -> 33 us
  other arithmetic: 8.95 us -> 13.1 us
  waiting for transfers between devices: 36.5 us -> 38.5 us
    pallas_call x1 -> x0, Pallas kernels: 6.16 us -> none  [taper_rows(): pl.pallas_call(taper_kernel, out_shape=jax.ShapeDtypeStruct((rows, span),...]
    convert_element_type x0 -> x1, other arithmetic: none -> 4.12 us  [program(): tapered = (raw_window * taper[None, :]).astype(jnp.bfloat16)]
    all_to_all x1, waiting for transfers between devices: 6.1 us -> 8.27 us  [program(): first = lax.all_to_all(first, 'gy', split_axis=0, concat_axis=0, tiled=True)]
  transfers between devices with their start and end apart: 21 -> 21, of which waited for: 10 -> 10; matrix products, arithmetic and copies ran while one was open for 5% -> 8% of each run, Pallas kernels for 22% -> 18%
where the time goes in v1:
time: 144 us; the launch traced here: 143 us
  starting transfers between devices  54.3 us (38%)
  waiting for transfers between devices  38.5 us (27%)
  Pallas kernels  33 us (23%)
  other arithmetic  13.1 us (9%)
  local copies, waits for them, and re-layouts  2.84 us (2%)
    pallas_call x2, Pallas kernels, whiten(): pl.pallas_call(whiten_kernel, out_shape=(out, out), grid_spec=pltpu.Prefe...  16.5 us
    all_to_all x1, waiting for transfers between devices, program(): lax.all_to_all(partial.reshape(devices, 4, NLAG), ('gx', 'gy'), split_axi...  14.1 us
    ppermute x9, waiting for transfers between devices, shift(): lax.ppermute(value, 'gx', [(g, (g + 2 * step) % (2 * SIDE)) for g in rang...  13.1 us
    pallas_call x2, Pallas kernels, correlate(): pl.pallas_call(kernel, out_shape=jax.ShapeDtypeStruct((slots, NLAG), dtyp...  12.9 us
    all_to_all x1, starting transfers between devices, program(): lax.all_to_all(partial.reshape(devices, 4, NLAG), ('gx', 'gy'), split_axi...  12.4 us
    ppermute x9, starting transfers between devices, shift(): lax.ppermute(value, 'gx', [(g, (g + 2 * step) % (2 * SIDE)) for g in rang...  12.2 us
    ppermute x3, starting transfers between devices, shift(): return lax.ppermute(value, 'gx', [(g, g ^ 1) for g in range(2 * SIDE)])  8.69 us
    all_to_all x1, waiting for transfers between devices, program(): first = lax.all_to_all(first, 'gy', split_axis=0, concat_axis=0, tiled=True)  8.27 us
  transfers between devices with their start and end apart: 21, of which 10 were waited for; matrix products, arithmetic and copies ran while one was open for 8% of the time, Pallas kernels for 18%

profile of v1, /device:TPU:1, one launch (start us, length us, event | category | flops | bytes accessed | tf_op | source)
XLA Modules:
  0.0 143.0 jit_solution(6182720696854705314)
XLA Ops:
  2.3 2.1 %collective-permute-start = (s32[130]{0:T(256)S(1)}, s32[130]{0:T(256)S(1)}, u32[]{:S(2)}, u32[]{:S(2)}) collective-permute-start(s32[130]{0:T(256)S(1)} %pad_add_fusion.4), channel_id=1, source_target_pairs={{0,1},{1,2},{2,3},{3,0},{4,5},{5,6},{6,7},{7,4},{8,9},{9,10},{10,1... | collective-permute-start | bytes 1568 | tf_op jit(solution)/shard_map/ppermute | solution.py:325
  4.4 2.5 %collective-permute-start.1 = (s32[130]{0:T(256)S(1)}, s32[130]{0:T(256)S(1)}, u32[]{:S(2)}, u32[]{:S(2)}) collective-permute-start(s32[130]{0:T(256)S(1)} %pad_add_fusion.4), channel_id=1, source_target_pairs={{0,2},{1,3},{2,0},{3,1},{4,6},{5,7},{6,4},{7,5},{8,10},{9,11},{10,... | collective-permute-start | bytes 1568 | tf_op jit(solution)/shard_map/ppermute | solution.py:325
  6.8 1.2 collective-permute-start.2
  9.6 1.7 %collective-permute-start.3 = (s32[4,130]{1,0:T(4,128)S(1)}, s32[4,130]{1,0:T(4,128)S(1)}, u32[]{:S(2)}, u32[]{:S(2)}) collective-permute-start(s32[4,130]{1,0:T(4,128)S(1)} %get-tuple-element.41), channel_id=1, source_target_pairs={{0,4},{1,5},{2,6},{3,7},{4,8},{5,9},{6,10},{7,11},{8,12},{9,13},{1... | collective-permute-start | bytes 6248 | tf_op jit(solution)/shard_map/ppermute | solution.py:324
  11.3 3.3 %collective-permute-start.4 = (s32[4,130]{1,0:T(4,128)S(1)}, s32[4,130]{1,0:T(4,128)S(1)}, u32[]{:S(2)}, u32[]{:S(2)}) collective-permute-start(s32[4,130]{1,0:T(4,128)S(1)} %get-tuple-element.41), channel_id=1, source_target_pairs={{0,8},{1,9},{2,10},{3,11},{4,12},{5,13},{6,14},{7,15},{8,0},{9,1},... | collective-permute-start | bytes 6248 | tf_op jit(solution)/shard_map/ppermute | solution.py:324
  15.6 1.4 collective-permute-done.5
  18.0 3.6 %pick.1 = bf16[16,32,1024]{2,1,0:T(8,128)(2,1)} custom-call(s32[32]{0:T(128)} %reshape.804.wanted_ref, f32[1024,1024]{1,0:T(8,128)} %raw_ref.1, f32[1,1024]{1,0:T(1,128)} %fusion.64.taper_ref), custom_call_target="tpu_custom_call" | custom-call | tf_op jit(solution)/shard_map/pick/pallas_call | solution.py:304
  21.6 5.1 %all-to-all-start = ((bf16[16,32,1024]{2,1,0:T(8,128)(2,1)}), bf16[16,32,1024]{2,1,0:T(8,128)(2,1)S(1)}, u32[]{:S(2)}, u32[]{:S(2)}) async-start(bf16[16,32,1024]{2,1,0:T(8,128)(2,1)} %pick.1), calls=%async_computation | async-start | bytes 2097152 | tf_op jit(solution)/shard_map/all_to_all | solution.py:360
  26.7 1.0 broadcast_multiply_fusion.1
  27.9 4.1 %multiply_convert_fusion = bf16[1024,1024]{1,0:T(8,128)(2,1)} fusion(f32[1024,1024]{1,0:T(8,128)} %raw_ref.1, f32[1024]{0:T(1024)S(1)} %fusion.59), kind=kLoop, calls=%fused_computation | loop fusion | flops 2097152 | bytes 6295552 | tf_op jit(solution)/shard_map/convert_element_type | solution.py:361
  32.0 8.3 %all-to-all-done.x_ref = bf16[16,32,1024]{2,1,0:T(8,128)(2,1)S(1)} async-done(((bf16[16,32,1024]{2,1,0:T(8,128)(2,1)}), bf16[16,32,1024]{2,1,0:T(8,128)(2,1)S(1)}, u32[]{:S(2)}, u32[]{:S(2)}) %all-to-all-start) | async-done | bytes 1048608 | tf_op jit(solution)/shard_map/all_to_all | solution.py:360
  41.3 4.4 %all-to-all-start.1 = ((bf16[16,64,1024]{2,1,0:T(8,128)(2,1)}), bf16[16,64,1024]{2,1,0:T(8,128)(2,1)}, u32[]{:S(2)}, u32[]{:S(2)}) async-start(bf16[16,64,1024]{2,1,0:T(8,128)(2,1)} %bitcast.29), calls=%async_computation.1 | async-start | bytes 4194304 | tf_op jit(solution)/shard_map/all_to_all | solution.py:362
  45.7 6.6 %whiten.2 = (bf16[32,64,128]{2,1,0:T(8,128)(2,1)}, bf16[32,64,128]{2,1,0:T(8,128)(2,1)S(1)}) custom-call(s32[1]{0:T(128)} %bitcast.16.core_ref, bf16[16,32,1024]{2,1,0:T(8,128)(2,1)} %copy-done, f32[2,16,256]{2,1,0:T(8,128)S(1)} %pad_maximum_fusion.1.tw_ref, bf16[512,512]{1,0:T(8,128)(2,1)S(1)} %fusion.11.upper_ref, ...), custom_call_target="tpu_custom_call" | custom-call | tf_op jit(solution)/shard_map/whiten/pallas_call | solution.py:153
  52.3 5.1 %collective-permute-start.10 = (bf16[32,64,128]{2,1,0:T(8,128)(2,1)S(1)}, bf16[32,64,128]{2,1,0:T(8,128)(2,1)}, u32[]{:S(2)}, u32[]{:S(2)}) collective-permute-start(bf16[32,64,128]{2,1,0:T(8,128)(2,1)S(1)} %get-tuple-element.15), channel_id=1, source_target_pairs={{0,16},{16,0},{32,48},{48,32},{64,80},{80,64},{96,112},{112,96},{1... | collective-permute-start | bytes 1572872 | tf_op jit(solution)/shard_map/ppermute | solution.py:320
  57.4 1.3 collective-permute-start.6
  58.7 2.6 %collective-permute-start.7 = (s32[4,4,128]{2,1,0:T(4,128)S(1)}, s32[4,4,128]{2,1,0:T(4,128)S(1)}, u32[]{:S(2)}, u32[]{:S(2)}) collective-permute-start(s32[4,4,128]{2,1,0:T(4,128)S(1)} %get-tuple-element.39), channel_id=1, source_target_pairs={{0,64},{16,80},{32,96},{48,112},{64,0},{80,16},{96,32},{112,48},{1... | collective-permute-start | bytes 24584 | tf_op jit(solution)/shard_map/ppermute | solution.py:322
  61.3 1.1 collective-permute-start.8
  63.1 1.1 collective-permute-done.8
  64.3 1.5 %collective-permute-start.9 = (s32[4,4,4,128]{3,2,1,0:T(4,128)S(1)}, s32[4,4,4,128]{3,2,1,0:T(4,128)S(1)}, u32[]{:S(2)}, u32[]{:S(2)}) collective-permute-start(s32[4,4,4,128]{3,2,1,0:T(4,128)S(1)} %get-tuple-element.37), channel_id=1, source_target_pairs={{0,16},{16,0},{32,48},{48,32},{64,80},{80,64},{96,112},{112,96},{1... | collective-permute-start | bytes 98312 | tf_op jit(solution)/shard_map/ppermute | solution.py:320
  66.6 2.7 %collective-permute-start.17 = (bf16[32,64,128]{2,1,0:T(8,128)(2,1)}, bf16[32,64,128]{2,1,0:T(8,128)(2,1)}, u32[]{:S(2)}, u32[]{:S(2)}) collective-permute-start(bf16[32,64,128]{2,1,0:T(8,128)(2,1)} %get-tuple-element.18.refs_0_), channel_id=1, source_target_pairs={{0,96},{16,112},{32,0},{48,16},{64,32},{80,48},{96,64},{112,80},{1... | collective-permute-start | bytes 1572872 | tf_op jit(solution)/shard_map/ppermute | solution.py:322
  69.4 1.1 fusion.18
  70.6 1.1 collective-permute-start.13
  72.1 9.1 %collective-permute-done.11.refs_2_ = bf16[32,64,128]{2,1,0:T(8,128)(2,1)} collective-permute-done((bf16[32,64,128]{2,1,0:T(8,128)(2,1)}, bf16[32,64,128]{2,1,0:T(8,128)(2,1)}, u32[]{:S(2)}, u32[]{:S(2)}) %collective-permute-start.11) | collective-permute-done | bytes 524320 | tf_op jit(solution)/shard_map/ppermute | solution.py:322
  83.0 9.9 %whiten.3 = (bf16[64,64,128]{2,1,0:T(8,128)(2,1)S(1)}, bf16[64,64,128]{2,1,0:T(8,128)(2,1)S(1)}) custom-call(s32[1]{0:T(128)} %bitcast.16.core_ref, bf16[16,64,1024]{2,1,0:T(8,128)(2,1)} %all-to-all-done.1.x_ref, f32[2,16,256]{2,1,0:T(8,128)S(1)} %pad_maximum_fusion.1.tw_ref, bf16[512,512]{1,0:T(8,128)(2,1)S(1)} %fusion.11.upper_ref, ...), custom_call_target="tpu_custom_call" | custom-call | tf_op jit(solution)/shard_map/whiten/pallas_call | solution.py:153
  92.8 2.1 %collective-permute-start.15 = (bf16[64,64,128]{2,1,0:T(8,128)(2,1)S(1)}, bf16[64,64,128]{2,1,0:T(8,128)(2,1)S(1)}, u32[]{:S(2)}, u32[]{:S(2)}) collective-permute-start(bf16[64,64,128]{2,1,0:T(8,128)(2,1)S(1)} %get-tuple-element.20), channel_id=1, source_target_pairs={{0,16},{16,0},{32,48},{48,32},{64,80},{80,64},{96,112},{112,96},{1... | collective-permute-start | bytes 3145736 | tf_op jit(solution)/shard_map/ppermute | solution.py:320
  95.7 3.0 %collective-permute-start.14 = (bf16[32,64,128]{2,1,0:T(8,128)(2,1)}, bf16[32,64,128]{2,1,0:T(8,128)(2,1)S(1)}, u32[]{:S(2)}, u32[]{:S(2)}) collective-permute-start(bf16[32,64,128]{2,1,0:T(8,128)(2,1)} %collective-permute-done.13.refs_5_), channel_id=1, source_target_pairs={{0,96},{16,112},{32,0},{48,16},{64,32},{80,48},{96,64},{112,80},{1... | collective-permute-start | bytes 1572872 | tf_op jit(solution)/shard_map/ppermute | solution.py:322
  99.5 8.7 %shard_map.55.refs_5_ = f32[512,512]{1,0:T(8,128)S(1)} custom-call(s32[1]{0:T(128)} %bitcast.31.count_ref, s32[512]{0:T(512)S(1)} %get-tuple-element.47.src_ref, s32[512]{0:T(512)S(1)} %get-tuple-element.48.rcv_ref, s32[512]{0:T(512)S(1)} %get-tuple-element.46.slot_ref, bf16[32,64,128]{2,1,0:T(8,128)(2,1)} %get-tuple-element.18.refs_0_, ...), custom_call_target="tpu_custom_call" | custom-call | tf_op jit(solution)/shard_map/pallas_call | solution.py:267
  108.2 2.1 %collective-permute-done.14.refs_1_ = bf16[32,64,128]{2,1,0:T(8,128)(2,1)S(1)} collective-permute-done((bf16[32,64,128]{2,1,0:T(8,128)(2,1)}, bf16[32,64,128]{2,1,0:T(8,128)(2,1)S(1)}, u32[]{:S(2)}, u32[]{:S(2)}) %collective-permute-start.14) | collective-permute-done | bytes 524320 | tf_op jit(solution)/shard_map/ppermute | solution.py:322
  110.3 4.1 %shard_map.56 = bf16[512,512]{1,0:T(8,128)(2,1)S(1)} custom-call(s32[1]{0:T(128)} %bitcast.22.count_ref, s32[512]{0:T(512)S(1)} %get-tuple-element.50.src_ref, s32[512]{0:T(512)S(1)} %get-tuple-element.51.rcv_ref, s32[512]{0:T(512)S(1)} %get-tuple-element.49.slot_ref, bf16[32,64,128]{2,1,0:T(8,128)(2,1)} %collective-permute-done.12.refs_0_, ...), custom_call_target="tpu_custom_call" | custom-call | tf_op jit(solution)/shard_map/pallas_call | solution.py:267
  115.4 12.4 %all-to-all-start.2 = ((bf16[128,4,512]{2,1,0:T(4,128)(2,1)}), bf16[128,4,512]{2,1,0:T(4,128)(2,1)S(1)}, u32[]{:S(2)}, u32[]{:S(2)}) async-start(bf16[128,4,512]{2,1,0:T(4,128)(2,1)} %reshape.808), calls=%async_computation.2 | async-start | bytes 1048576 | tf_op jit(solution)/shard_map/all_to_all | solution.py:425
  127.8 14.1 %all-to-all-done.2 = bf16[128,4,512]{2,1,0:T(4,128)(2,1)S(1)} async-done(((bf16[128,4,512]{2,1,0:T(4,128)(2,1)}), bf16[128,4,512]{2,1,0:T(4,128)(2,1)S(1)}, u32[]{:S(2)}, u32[]{:S(2)}) %all-to-all-start.2) | async-done | bytes 524320 | tf_op jit(solution)/shard_map/all_to_all | solution.py:425
  142.0 1.0 fusion.7
  (74 shorter events, 13.2 us)
Async XLA Ops:
  2.3 6.7 %collective-permute-start = (s32[130]{0:T(256)S(1)}, s32[130]{0:T(256)S(1)}, u32[]{:S(2)}, u32[]{:S(2)}) collective-permute-start(s32[130]{0:T(256)S(1)} %pad_add_fusion.4), channel_id=1, source_target_pairs={{0,1},{1,2},{2,3},{3,0},{4,5},{5,6},{6,7},{7,4},{8,9},{9,10},{10,1... | collective-permute-start | bytes 1568 | tf_op jit(solution)/shard_map/ppermute | solution.py:325
  4.4 4.6 %collective-permute-start.1 = (s32[130]{0:T(256)S(1)}, s32[130]{0:T(256)S(1)}, u32[]{:S(2)}, u32[]{:S(2)}) collective-permute-start(s32[130]{0:T(256)S(1)} %pad_add_fusion.4), channel_id=1, source_target_pairs={{0,2},{1,3},{2,0},{3,1},{4,6},{5,7},{6,4},{7,5},{8,10},{9,11},{10,... | collective-permute-start | bytes 1568 | tf_op jit(solution)/shard_map/ppermute | solution.py:325
  6.8 2.7 %collective-permute-start.2 = (s32[130]{0:T(256)S(1)}, s32[130]{0:T(256)S(1)}, u32[]{:S(2)}, u32[]{:S(2)}) collective-permute-start(s32[130]{0:T(256)S(1)} %pad_add_fusion.4), channel_id=1, source_target_pairs={{0,3},{1,0},{2,1},{3,2},{4,7},{5,4},{6,5},{7,6},{8,11},{9,8},{10,9... | collective-permute-start | bytes 1568 | tf_op jit(solution)/shard_map/ppermute | solution.py:325
  9.6 5.7 %collective-permute-start.3 = (s32[4,130]{1,0:T(4,128)S(1)}, s32[4,130]{1,0:T(4,128)S(1)}, u32[]{:S(2)}, u32[]{:S(2)}) collective-permute-start(s32[4,130]{1,0:T(4,128)S(1)} %get-tuple-element.41), channel_id=1, source_target_pairs={{0,4},{1,5},{2,6},{3,7},{4,8},{5,9},{6,10},{7,11},{8,12},{9,13},{1... | collective-permute-start | bytes 6248 | tf_op jit(solution)/shard_map/ppermute | solution.py:324
  11.3 4.3 %collective-permute-start.4 = (s32[4,130]{1,0:T(4,128)S(1)}, s32[4,130]{1,0:T(4,128)S(1)}, u32[]{:S(2)}, u32[]{:S(2)}) collective-permute-start(s32[4,130]{1,0:T(4,128)S(1)} %get-tuple-element.41), channel_id=1, source_target_pairs={{0,8},{1,9},{2,10},{3,11},{4,12},{5,13},{6,14},{7,15},{8,0},{9,1},... | collective-permute-start | bytes 6248 | tf_op jit(solution)/shard_map/ppermute | solution.py:324
  14.6 2.5 %collective-permute-start.5 = (s32[4,130]{1,0:T(4,128)S(1)}, s32[4,130]{1,0:T(4,128)S(1)}, u32[]{:S(2)}, u32[]{:S(2)}) collective-permute-start(s32[4,130]{1,0:T(4,128)S(1)} %get-tuple-element.41), channel_id=1, source_target_pairs={{0,12},{1,13},{2,14},{3,15},{4,0},{5,1},{6,2},{7,3},{8,4},{9,5},{1... | collective-permute-start | bytes 6248 | tf_op jit(solution)/shard_map/ppermute | solution.py:324
  21.6 18.7 %all-to-all-start = ((bf16[16,32,1024]{2,1,0:T(8,128)(2,1)}), bf16[16,32,1024]{2,1,0:T(8,128)(2,1)S(1)}, u32[]{:S(2)}, u32[]{:S(2)}) async-start(bf16[16,32,1024]{2,1,0:T(8,128)(2,1)} %pick.1), calls=%async_computation | async-start | bytes 2097152 | tf_op jit(solution)/shard_map/all_to_all | solution.py:360
  40.3 1.0 copy-start
  41.3 41.7 %all-to-all-start.1 = ((bf16[16,64,1024]{2,1,0:T(8,128)(2,1)}), bf16[16,64,1024]{2,1,0:T(8,128)(2,1)}, u32[]{:S(2)}, u32[]{:S(2)}) async-start(bf16[16,64,1024]{2,1,0:T(8,128)(2,1)} %bitcast.29), calls=%async_computation.1 | async-start | bytes 4194304 | tf_op jit(solution)/shard_map/all_to_all | solution.py:362
  52.3 17.0 %collective-permute-start.10 = (bf16[32,64,128]{2,1,0:T(8,128)(2,1)S(1)}, bf16[32,64,128]{2,1,0:T(8,128)(2,1)}, u32[]{:S(2)}, u32[]{:S(2)}) collective-permute-start(bf16[32,64,128]{2,1,0:T(8,128)(2,1)S(1)} %get-tuple-element.15), channel_id=1, source_target_pairs={{0,16},{16,0},{32,48},{48,32},{64,80},{80,64},{96,112},{112,96},{1... | collective-permute-start | bytes 1572872 | tf_op jit(solution)/shard_map/ppermute | solution.py:320
  57.4 5.0 %collective-permute-start.6 = (s32[4,4,128]{2,1,0:T(4,128)S(1)}, s32[4,4,128]{2,1,0:T(4,128)S(1)}, u32[]{:S(2)}, u32[]{:S(2)}) collective-permute-start(s32[4,4,128]{2,1,0:T(4,128)S(1)} %get-tuple-element.39), channel_id=1, source_target_pairs={{0,32},{16,48},{32,64},{48,80},{64,96},{80,112},{96,0},{112,16},{1... | collective-permute-start | bytes 24584 | tf_op jit(solution)/shard_map/ppermute | solution.py:322
  58.7 4.4 %collective-permute-start.7 = (s32[4,4,128]{2,1,0:T(4,128)S(1)}, s32[4,4,128]{2,1,0:T(4,128)S(1)}, u32[]{:S(2)}, u32[]{:S(2)}) collective-permute-start(s32[4,4,128]{2,1,0:T(4,128)S(1)} %get-tuple-element.39), channel_id=1, source_target_pairs={{0,64},{16,80},{32,96},{48,112},{64,0},{80,16},{96,32},{112,48},{1... | collective-permute-start | bytes 24584 | tf_op jit(solution)/shard_map/ppermute | solution.py:322
  61.3 2.9 %collective-permute-start.8 = (s32[4,4,128]{2,1,0:T(4,128)S(1)}, s32[4,4,128]{2,1,0:T(4,128)S(1)}, u32[]{:S(2)}, u32[]{:S(2)}) collective-permute-start(s32[4,4,128]{2,1,0:T(4,128)S(1)} %get-tuple-element.39), channel_id=1, source_target_pairs={{0,96},{16,112},{32,0},{48,16},{64,32},{80,48},{96,64},{112,80},{1... | collective-permute-start | bytes 24584 | tf_op jit(solution)/shard_map/ppermute | solution.py:322
  64.3 2.3 %collective-permute-start.9 = (s32[4,4,4,128]{3,2,1,0:T(4,128)S(1)}, s32[4,4,4,128]{3,2,1,0:T(4,128)S(1)}, u32[]{:S(2)}, u32[]{:S(2)}) collective-permute-start(s32[4,4,4,128]{3,2,1,0:T(4,128)S(1)} %get-tuple-element.37), channel_id=1, source_target_pairs={{0,16},{16,0},{32,48},{48,32},{64,80},{80,64},{96,112},{112,96},{1... | collective-permute-start | bytes 98312 | tf_op jit(solution)/shard_map/ppermute | solution.py:320
  66.6 14.7 %collective-permute-start.11 = (bf16[32,64,128]{2,1,0:T(8,128)(2,1)}, bf16[32,64,128]{2,1,0:T(8,128)(2,1)}, u32[]{:S(2)}, u32[]{:S(2)}) collective-permute-start(bf16[32,64,128]{2,1,0:T(8,128)(2,1)} %get-tuple-element.18.refs_0_), channel_id=1, source_target_pairs={{0,32},{16,48},{32,64},{48,80},{64,96},{80,112},{96,0},{112,16},{1... | collective-permute-start | bytes 1572872 | tf_op jit(solution)/shard_map/ppermute | solution.py:322
  66.6 32.8 %collective-permute-start.17 = (bf16[32,64,128]{2,1,0:T(8,128)(2,1)}, bf16[32,64,128]{2,1,0:T(8,128)(2,1)}, u32[]{:S(2)}, u32[]{:S(2)}) collective-permute-start(bf16[32,64,128]{2,1,0:T(8,128)(2,1)} %get-tuple-element.18.refs_0_), channel_id=1, source_target_pairs={{0,96},{16,112},{32,0},{48,16},{64,32},{80,48},{96,64},{112,80},{1... | collective-permute-start | bytes 1572872 | tf_op jit(solution)/shard_map/ppermute | solution.py:322
  70.6 25.1 %collective-permute-start.13 = (bf16[32,64,128]{2,1,0:T(8,128)(2,1)}, bf16[32,64,128]{2,1,0:T(8,128)(2,1)}, u32[]{:S(2)}, u32[]{:S(2)}) collective-permute-start(bf16[32,64,128]{2,1,0:T(8,128)(2,1)} %collective-permute-done.10.refs_1_), channel_id=1, source_target_pairs={{0,96},{16,112},{32,0},{48,16},{64,32},{80,48},{96,64},{112,80},{1... | collective-permute-start | bytes 1572872 | tf_op jit(solution)/shard_map/ppermute | solution.py:322
  71.7 27.7 %collective-permute-start.16 = (bf16[32,64,128]{2,1,0:T(8,128)(2,1)}, bf16[32,64,128]{2,1,0:T(8,128)(2,1)}, u32[]{:S(2)}, u32[]{:S(2)}) collective-permute-start(bf16[32,64,128]{2,1,0:T(8,128)(2,1)} %collective-permute-done.10.refs_1_), channel_id=1, source_target_pairs={{0,32},{16,48},{32,64},{48,80},{64,96},{80,112},{96,0},{112,16},{1... | collective-permute-start | bytes 1572872 | tf_op jit(solution)/shard_map/ppermute | solution.py:322
  81.3 27.0 %collective-permute-start.12 = (bf16[32,64,128]{2,1,0:T(8,128)(2,1)}, bf16[32,64,128]{2,1,0:T(8,128)(2,1)}, u32[]{:S(2)}, u32[]{:S(2)}) collective-permute-start(bf16[32,64,128]{2,1,0:T(8,128)(2,1)} %collective-permute-done.11.refs_2_), channel_id=1, source_target_pairs={{0,32},{16,48},{32,64},{48,80},{64,96},{80,112},{96,0},{112,16},{1... | collective-permute-start | bytes 1572872 | tf_op jit(solution)/shard_map/ppermute | solution.py:322
  92.8 6.6 %collective-permute-start.15 = (bf16[64,64,128]{2,1,0:T(8,128)(2,1)S(1)}, bf16[64,64,128]{2,1,0:T(8,128)(2,1)S(1)}, u32[]{:S(2)}, u32[]{:S(2)}) collective-permute-start(bf16[64,64,128]{2,1,0:T(8,128)(2,1)S(1)} %get-tuple-element.20), channel_id=1, source_target_pairs={{0,16},{16,0},{32,48},{48,32},{64,80},{80,64},{96,112},{112,96},{1... | collective-permute-start | bytes 3145736 | tf_op jit(solution)/shard_map/ppermute | solution.py:320
  95.7 14.6 %collective-permute-start.14 = (bf16[32,64,128]{2,1,0:T(8,128)(2,1)}, bf16[32,64,128]{2,1,0:T(8,128)(2,1)S(1)}, u32[]{:S(2)}, u32[]{:S(2)}) collective-permute-start(bf16[32,64,128]{2,1,0:T(8,128)(2,1)} %collective-permute-done.13.refs_5_), channel_id=1, source_target_pairs={{0,96},{16,112},{32,0},{48,16},{64,32},{80,48},{96,64},{112,80},{1... | collective-permute-start | bytes 1572872 | tf_op jit(solution)/shard_map/ppermute | solution.py:322
  114.4 27.6 %copy-start.1 = (s32[128,1]{0,1:T(1,128)S(1)}, s32[128,1]{0,1:T(1,128)}, u32[]{:S(2)}) copy-start(s32[128,1]{0,1:T(1,128)} %param.8) | copy-start | bytes 1540
  115.4 26.5 %all-to-all-start.2 = ((bf16[128,4,512]{2,1,0:T(4,128)(2,1)}), bf16[128,4,512]{2,1,0:T(4,128)(2,1)S(1)}, u32[]{:S(2)}, u32[]{:S(2)}) async-start(bf16[128,4,512]{2,1,0:T(4,128)(2,1)} %reshape.808), calls=%async_computation.2 | async-start | bytes 1048576 | tf_op jit(solution)/shard_map/all_to_all | solution.py:425

commit v2 on v1

--- a/solution.py
+++ b/solution.py
@@ -97,35 +97,53 @@
     return out
 
 
-def whiten_kernel(core_ref, x_ref, tw_ref, upper_ref, lower_ref, mine_ref, other_ref, hi_ref, lo_ref, out_ref):
+def whiten_kernel(core_ref, x_ref, tw_ref, upper_ref, lower_ref, mine_ref, other_ref, hi_ref, lo_ref):
     rows = x_ref.shape[1]
-    slices = []
-    for t in range(RADIX):
-        q, u = t // SIDE, t % SIDE
-        slices.append(x_ref[q, :, u * INNER:(u + 1) * INNER].astype(jnp.float32))
-    outer = real_dft(slices)
-    for f in range(RADIX // 2 + 1):
-        re, im = outer[f]
-        c, s = tw_ref[0, f:f + 1, :], tw_ref[1, f:f + 1, :]
+    half = RADIX // 2
+    where = lambda f: (f - 1) % (half + 1)
+    for block in range(rows // 16):
+        r = slice(block * 16, block * 16 + 16)
+        for k in range(INNER // LANES):
+            slices = []
+            for t in range(RADIX):
+                at = (t % SIDE) * INNER + k * LANES
+                slices.append(x_ref[t // SIDE, r, at:at + LANES].astype(jnp.float32))
+            outer = real_dft(slices)
+            for f in range(half + 1):
+                re, im = outer[f]
+                lanes = slice(k * LANES, (k + 1) * LANES)
+                c, s = tw_ref[0, f:f + 1, lanes], tw_ref[1, f:f + 1, lanes]
+                if f == 0:
+                    parts = (re,)
+                elif im is None:
+                    parts = (re * c, re * s)
+                else:
+                    parts = (re * c - im * s, re * s + im * c)
+                row = slice(where(f) * rows + block * 16, where(f) * rows + block * 16 + 16)
+                for n, part in enumerate(parts):
+                    hi = part.astype(jnp.bfloat16)
+                    at = slice(n * INNER + k * LANES, n * INNER + (k + 1) * LANES)
+                    hi_ref[row, at] = hi
+                    lo_ref[row, at] = (part - hi.astype(jnp.float32)).astype(jnp.bfloat16)
+
+    def spectrum(row, depth, width):
+        hi, lo = hi_ref[row, :depth], lo_ref[row, :depth]
+        upper, lower = upper_ref[:depth, :width], lower_ref[:depth, :width]
+        out = jnp.dot(hi, upper, preferred_element_type=jnp.float32)
+        out += jnp.dot(hi, lower, preferred_element_type=jnp.float32)
+        return out + jnp.dot(lo, upper, preferred_element_type=jnp.float32)
+
+    most = spectrum(slice(0, (half - 1) * rows), 2 * INNER, 4 * LANES)
+    middle = spectrum(slice((half - 1) * rows, half * rows), 2 * INNER, 2 * LANES)
+    first = spectrum(slice(half * rows, (half + 1) * rows), INNER, 2 * LANES)
+
+    def part(f, k):
         if f == 0:
-            pair = (re, jnp.zeros_like(re))
-        elif im is None:
-            pair = (re * c, re * s)
-        else:
-            pair = (re * c - im * s, re * s + im * c)
-        for k in range(2):
-            hi = pair[k].astype(jnp.bfloat16)
-            hi_ref[f * rows:(f + 1) * rows, k * INNER:(k + 1) * INNER] = hi
-            lo_ref[f * rows:(f + 1) * rows, k * INNER:(k + 1) * INNER] = (pair[k] - hi.astype(jnp.float32)).astype(jnp.bfloat16)
-    hi, lo = hi_ref[...], lo_ref[...]
-    upper, lower = upper_ref[...], lower_ref[...]
-    spectrum = jnp.dot(hi, upper, preferred_element_type=jnp.float32)
-    spectrum += jnp.dot(hi, lower, preferred_element_type=jnp.float32)
-    spectrum += jnp.dot(lo, upper, preferred_element_type=jnp.float32)
-
-    def part(f, k):
-        g, base = (f, 0) if f <= RADIX // 2 else (RADIX - f, 2)
-        return spectrum[g * rows:(g + 1) * rows, (base + k) * LANES:(base + k + 1) * LANES]
+            return first[:, k * LANES:(k + 1) * LANES]
+        if f == half:
+            return middle[:, k * LANES:(k + 1) * LANES]
+        g, base = (f, 0) if f < half else (RADIX - f, 2)
+        return most[(g - 1) * rows:g * rows, (base + k) * LANES:(base + k + 1) * LANES]
 
     power = None
     for f in range(RADIX):
@@ -135,13 +153,15 @@
     power = power + pltpu.roll(power, 64, 1)
     power = power + pltpu.roll(power, 32, 1)
     scale = 1.0 / jnp.sqrt(power * (1.0 / BAND) + 1e-06)
-    for f in range(RADIX):
-        for k in range(2):
-            index = (f // 8) * HALF_ROWS + k * 8 + f % 8
-            out_ref[:, index, :] = part(f, k) * scale
-    core = core_ref[0]
-    mine_ref[...] = out_ref[:, pl.ds(pl.multiple_of(core * HALF_ROWS, HALF_ROWS), HALF_ROWS), :].astype(jnp.bfloat16)
-    other_ref[...] = out_ref[:, pl.ds(pl.multiple_of((1 - core) * HALF_ROWS, HALF_ROWS), HALF_ROWS), :].astype(jnp.bfloat16)
+    low = core_ref[0] == 0
+    for block in range(rows // 8):
+        r = slice(block * 8, block * 8 + 8)
+        halves = []
+        for h in range(2):
+            tiles = [part(h * 8 + f, k)[r] * scale[r] for k in range(2) for f in range(8)]
+            halves.append(jnp.transpose(jnp.stack(tiles, axis=0), (1, 0, 2)))
+        mine_ref[r] = jnp.where(low, halves[0], halves[1]).astype(jnp.bfloat16)
+        other_ref[r] = jnp.where(low, halves[1], halves[0]).astype(jnp.bfloat16)
 
 
 def whiten(core, samples, twiddle, upper, lower):
@@ -166,7 +186,6 @@
             scratch_shapes=[
                 pltpu.VMEM((count * rows, 2 * INNER), jnp.bfloat16),
                 pltpu.VMEM((count * rows, 2 * INNER), jnp.bfloat16),
-                pltpu.VMEM((rows, 2 * HALF_ROWS, LANES), jnp.float32),
             ],
         ),
         compiler_params=pltpu.CompilerParams(vmem_limit_bytes=48 << 20),
@@ -207,16 +226,18 @@
                 re = r if re is None else re + r
                 im = m if im is None else im + m
             row = row_of(i)
-            cross_ref[row, 0:8, :] = re
-            cross_ref[row, 8:16, :] = im
+            at = pl.multiple_of(row * HALF_ROWS, HALF_ROWS)
+            cross_ref[pl.ds(at, 8), :] = re
+            cross_ref[pl.ds(at + 8, 8), :] = im
         return carry
 
     lax.fori_loop(0, (count + GROUP - 1) // GROUP, group, 0)
 
 
-def lags_of(cross_ref, first, table_ref):
+def lags_of(cross_ref, first, count, table_ref):
     cross = jnp.concatenate(
-        [cross_ref[pl.ds(first, CHUNK), g, :].astype(jnp.bfloat16) for g in range(HALF_ROWS)], axis=1
+        [cross_ref[pl.ds(first * HALF_ROWS + g, count, stride=HALF_ROWS), :].astype(jnp.bfloat16) for g in range(HALF_ROWS)],
+        axis=1,
     )
     return jnp.dot(cross, table_ref[...], preferred_element_type=jnp.float32)
 
@@ -229,8 +250,7 @@
     for copy in copies:
         copy.wait()
     cross_slots(count_ref[0], src_ref, rcv_ref, lambda i: slot_ref[i], sources_ref, receivers_ref, cross_ref)
-    for c in range(out_ref.shape[0] // CHUNK):
-        out_ref[c * CHUNK:(c + 1) * CHUNK, :] = lags_of(cross_ref, c * CHUNK, table_ref)
+    out_ref[...] = lags_of(cross_ref, 0, out_ref.shape[0], table_ref)
 
 
 def far_kernel(count_ref, src_ref, rcv_ref, slot_ref, *refs):
@@ -246,7 +266,7 @@
 
     def chunk(c, carry):
         first = pl.multiple_of(c * CHUNK, CHUNK)
-        product_ref[...] = lags_of(cross_ref, first, table_ref)
+        product_ref[...] = lags_of(cross_ref, first, CHUNK, table_ref)
 
         def place(g, inner):
             for u in range(GROUP):
@@ -275,7 +295,7 @@
             scratch_shapes=[
                 pltpu.VMEM((sum(p.shape[0] for p in pieces),) + row, jnp.bfloat16),
                 pltpu.VMEM((sum(p.shape[0] for p in receivers),) + row, jnp.bfloat16),
-                pltpu.VMEM((slots + GROUP, HALF_ROWS, LANES), jnp.float32),
+                pltpu.VMEM(((slots + GROUP) * HALF_ROWS, LANES), jnp.float32),
                 *extra,
                 pltpu.SemaphoreType.DMA((len(pieces) + len(receivers),)),
             ],

time: 144 us -> 141 us (0.979)
  Pallas kernels: 33 us -> 27.7 us
  waiting for transfers between devices: 38.5 us -> 41.4 us
    pallas_call x2, Pallas kernels: 12.9 us -> 9.32 us  [correlate(): pl.pallas_call(kernel, out_shape=jax.ShapeDtypeStruct((slots, NLAG), dtyp...]
    ppermute x9, waiting for transfers between devices: 13.1 us -> 16 us  [shift(): lax.ppermute(value, 'gx', [(g, (g + 2 * step) % (2 * SIDE)) for g in rang...]
    pallas_call x2, Pallas kernels: 16.5 us -> 14.7 us  [whiten(): pl.pallas_call(whiten_kernel, out_shape=(out, out), grid_spec=pltpu.Prefe...]
  transfers between devices with their start and end apart: 21 -> 21, of which waited for: 10 -> 10; matrix products, arithmetic and copies ran while one was open for 8% -> 8% of each run, Pallas kernels for 18% -> 15%
where the time goes in v2:
time: 141 us; the launch traced here: 140 us
  starting transfers between devices  53.6 us (38%)
  waiting for transfers between devices  41.4 us (29%)
  Pallas kernels  27.7 us (20%)
  other arithmetic  13.1 us (9%)
  local copies, waits for them, and re-layouts  2.84 us (2%)
    ppermute x9, waiting for transfers between devices, shift(): lax.ppermute(value, 'gx', [(g, (g + 2 * step) % (2 * SIDE)) for g in rang...  16 us
    pallas_call x2, Pallas kernels, whiten(): pl.pallas_call(whiten_kernel, out_shape=(out, out), grid_spec=pltpu.Prefe...  14.7 us
    all_to_all x1, waiting for transfers between devices, program(): lax.all_to_all(partial.reshape(devices, 4, NLAG), ('gx', 'gy'), split_axi...  14.1 us
    ppermute x9, starting transfers between devices, shift(): lax.ppermute(value, 'gx', [(g, (g + 2 * step) % (2 * SIDE)) for g in rang...  12.2 us
    all_to_all x1, starting transfers between devices, program(): lax.all_to_all(partial.reshape(devices, 4, NLAG), ('gx', 'gy'), split_axi...  11.7 us
    pallas_call x2, Pallas kernels, correlate(): pl.pallas_call(kernel, out_shape=jax.ShapeDtypeStruct((slots, NLAG), dtyp...  9.32 us
    ppermute x3, starting transfers between devices, shift(): return lax.ppermute(value, 'gx', [(g, g ^ 1) for g in range(2 * SIDE)])  8.66 us
    all_to_all x1, waiting for transfers between devices, program(): first = lax.all_to_all(first, 'gy', split_axis=0, concat_axis=0, tiled=True)  8.27 us
  transfers between devices with their start and end apart: 21, of which 10 were waited for; matrix products, arithmetic and copies ran while one was open for 8% of the time, Pallas kernels for 15%

profile of v2, /device:TPU:1, one launch (start us, length us, event | category | flops | bytes accessed | tf_op | source)
XLA Modules:
  0.0 139.9 jit_solution(2217675569739974252)
XLA Ops:
  2.3 2.1 %collective-permute-start = (s32[130]{0:T(256)S(1)}, s32[130]{0:T(256)S(1)}, u32[]{:S(2)}, u32[]{:S(2)}) collective-permute-start(s32[130]{0:T(256)S(1)} %pad_add_fusion.4), channel_id=1, source_target_pairs={{0,1},{1,2},{2,3},{3,0},{4,5},{5,6},{6,7},{7,4},{8,9},{9,10},{10,1... | collective-permute-start | bytes 1568 | tf_op jit(solution)/shard_map/ppermute | solution.py:345
  4.4 2.5 %collective-permute-start.1 = (s32[130]{0:T(256)S(1)}, s32[130]{0:T(256)S(1)}, u32[]{:S(2)}, u32[]{:S(2)}) collective-permute-start(s32[130]{0:T(256)S(1)} %pad_add_fusion.4), channel_id=1, source_target_pairs={{0,2},{1,3},{2,0},{3,1},{4,6},{5,7},{6,4},{7,5},{8,10},{9,11},{10,... | collective-permute-start | bytes 1568 | tf_op jit(solution)/shard_map/ppermute | solution.py:345
  6.8 1.2 collective-permute-start.2
  9.6 1.7 %collective-permute-start.3 = (s32[4,130]{1,0:T(4,128)S(1)}, s32[4,130]{1,0:T(4,128)S(1)}, u32[]{:S(2)}, u32[]{:S(2)}) collective-permute-start(s32[4,130]{1,0:T(4,128)S(1)} %get-tuple-element.41), channel_id=1, source_target_pairs={{0,4},{1,5},{2,6},{3,7},{4,8},{5,9},{6,10},{7,11},{8,12},{9,13},{1... | collective-permute-start | bytes 6248 | tf_op jit(solution)/shard_map/ppermute | solution.py:344
  11.3 3.3 %collective-permute-start.4 = (s32[4,130]{1,0:T(4,128)S(1)}, s32[4,130]{1,0:T(4,128)S(1)}, u32[]{:S(2)}, u32[]{:S(2)}) collective-permute-start(s32[4,130]{1,0:T(4,128)S(1)} %get-tuple-element.41), channel_id=1, source_target_pairs={{0,8},{1,9},{2,10},{3,11},{4,12},{5,13},{6,14},{7,15},{8,0},{9,1},... | collective-permute-start | bytes 6248 | tf_op jit(solution)/shard_map/ppermute | solution.py:344
  15.6 1.4 %collective-permute-done.5 = s32[4,130]{1,0:T(4,128)S(1)} collective-permute-done((s32[4,130]{1,0:T(4,128)S(1)}, s32[4,130]{1,0:T(4,128)S(1)}, u32[]{:S(2)}, u32[]{:S(2)}) %collective-permute-start.5) | collective-permute-done | bytes 2112 | tf_op jit(solution)/shard_map/ppermute | solution.py:344
  18.0 3.6 %pick.1 = bf16[16,32,1024]{2,1,0:T(8,128)(2,1)} custom-call(s32[32]{0:T(128)} %reshape.804.wanted_ref, f32[1024,1024]{1,0:T(8,128)} %raw_ref.1, f32[1,1024]{1,0:T(1,128)} %fusion.64.taper_ref), custom_call_target="tpu_custom_call" | custom-call | tf_op jit(solution)/shard_map/pick/pallas_call | solution.py:324
  21.6 5.1 %all-to-all-start = ((bf16[16,32,1024]{2,1,0:T(8,128)(2,1)}), bf16[16,32,1024]{2,1,0:T(8,128)(2,1)S(1)}, u32[]{:S(2)}, u32[]{:S(2)}) async-start(bf16[16,32,1024]{2,1,0:T(8,128)(2,1)} %pick.1), calls=%async_computation | async-start | bytes 2097152 | tf_op jit(solution)/shard_map/all_to_all | solution.py:380
  26.7 1.0 broadcast_multiply_fusion.1
  27.9 4.1 %multiply_convert_fusion = bf16[1024,1024]{1,0:T(8,128)(2,1)} fusion(f32[1024,1024]{1,0:T(8,128)} %raw_ref.1, f32[1024]{0:T(1024)S(1)} %fusion.59), kind=kLoop, calls=%fused_computation | loop fusion | flops 2097152 | bytes 6295552 | tf_op jit(solution)/shard_map/convert_element_type | solution.py:381
  32.0 8.3 %all-to-all-done.x_ref = bf16[16,32,1024]{2,1,0:T(8,128)(2,1)S(1)} async-done(((bf16[16,32,1024]{2,1,0:T(8,128)(2,1)}), bf16[16,32,1024]{2,1,0:T(8,128)(2,1)S(1)}, u32[]{:S(2)}, u32[]{:S(2)}) %all-to-all-start) | async-done | bytes 1048608 | tf_op jit(solution)/shard_map/all_to_all | solution.py:380
  41.3 4.4 %all-to-all-start.1 = ((bf16[16,64,1024]{2,1,0:T(8,128)(2,1)}), bf16[16,64,1024]{2,1,0:T(8,128)(2,1)}, u32[]{:S(2)}, u32[]{:S(2)}) async-start(bf16[16,64,1024]{2,1,0:T(8,128)(2,1)} %bitcast.29), calls=%async_computation.1 | async-start | bytes 4194304 | tf_op jit(solution)/shard_map/all_to_all | solution.py:382
  45.7 6.2 %whiten.2 = (bf16[32,64,128]{2,1,0:T(8,128)(2,1)}, bf16[32,64,128]{2,1,0:T(8,128)(2,1)S(1)}) custom-call(s32[1]{0:T(128)} %bitcast.16.core_ref, bf16[16,32,1024]{2,1,0:T(8,128)(2,1)} %copy-done, f32[2,16,256]{2,1,0:T(8,128)S(1)} %pad_maximum_fusion.1.tw_ref, bf16[512,512]{1,0:T(8,128)(2,1)S(1)} %fusion.11.upper_ref, ...), custom_call_target="tpu_custom_call" | custom-call | tf_op jit(solution)/shard_map/whiten/pallas_call | solution.py:173
  51.9 5.1 %collective-permute-start.10 = (bf16[32,64,128]{2,1,0:T(8,128)(2,1)S(1)}, bf16[32,64,128]{2,1,0:T(8,128)(2,1)}, u32[]{:S(2)}, u32[]{:S(2)}) collective-permute-start(bf16[32,64,128]{2,1,0:T(8,128)(2,1)S(1)} %get-tuple-element.15), channel_id=1, source_target_pairs={{0,16},{16,0},{32,48},{48,32},{64,80},{80,64},{96,112},{112,96},{1... | collective-permute-start | bytes 1572872 | tf_op jit(solution)/shard_map/ppermute | solution.py:340
  57.0 1.3 collective-permute-start.6
  58.3 2.6 %collective-permute-start.7 = (s32[4,4,128]{2,1,0:T(4,128)S(1)}, s32[4,4,128]{2,1,0:T(4,128)S(1)}, u32[]{:S(2)}, u32[]{:S(2)}) collective-permute-start(s32[4,4,128]{2,1,0:T(4,128)S(1)} %get-tuple-element.39), channel_id=1, source_target_pairs={{0,64},{16,80},{32,96},{48,112},{64,0},{80,16},{96,32},{112,48},{1... | collective-permute-start | bytes 24584 | tf_op jit(solution)/shard_map/ppermute | solution.py:342
  60.9 1.1 collective-permute-start.8
  62.7 1.1 collective-permute-done.8
  63.9 1.5 %collective-permute-start.9 = (s32[4,4,4,128]{3,2,1,0:T(4,128)S(1)}, s32[4,4,4,128]{3,2,1,0:T(4,128)S(1)}, u32[]{:S(2)}, u32[]{:S(2)}) collective-permute-start(s32[4,4,4,128]{3,2,1,0:T(4,128)S(1)} %get-tuple-element.37), channel_id=1, source_target_pairs={{0,16},{16,0},{32,48},{48,32},{64,80},{80,64},{96,112},{112,96},{1... | collective-permute-start | bytes 98312 | tf_op jit(solution)/shard_map/ppermute | solution.py:340
  66.2 2.7 %collective-permute-start.17 = (bf16[32,64,128]{2,1,0:T(8,128)(2,1)}, bf16[32,64,128]{2,1,0:T(8,128)(2,1)}, u32[]{:S(2)}, u32[]{:S(2)}) collective-permute-start(bf16[32,64,128]{2,1,0:T(8,128)(2,1)} %get-tuple-element.18.refs_0_), channel_id=1, source_target_pairs={{0,96},{16,112},{32,0},{48,16},{64,32},{80,48},{96,64},{112,80},{1... | collective-permute-start | bytes 1572872 | tf_op jit(solution)/shard_map/ppermute | solution.py:342
  69.0 1.1 fusion.18
  70.2 1.1 collective-permute-start.13
  71.7 9.1 %collective-permute-done.11.refs_2_ = bf16[32,64,128]{2,1,0:T(8,128)(2,1)} collective-permute-done((bf16[32,64,128]{2,1,0:T(8,128)(2,1)}, bf16[32,64,128]{2,1,0:T(8,128)(2,1)}, u32[]{:S(2)}, u32[]{:S(2)}) %collective-permute-start.11) | collective-permute-done | bytes 524320 | tf_op jit(solution)/shard_map/ppermute | solution.py:342
  82.6 8.5 %whiten.3 = (bf16[64,64,128]{2,1,0:T(8,128)(2,1)S(1)}, bf16[64,64,128]{2,1,0:T(8,128)(2,1)S(1)}) custom-call(s32[1]{0:T(128)} %bitcast.16.core_ref, bf16[16,64,1024]{2,1,0:T(8,128)(2,1)} %all-to-all-done.1.x_ref, f32[2,16,256]{2,1,0:T(8,128)S(1)} %pad_maximum_fusion.1.tw_ref, bf16[512,512]{1,0:T(8,128)(2,1)S(1)} %fusion.11.upper_ref, ...), custom_call_target="tpu_custom_call" | custom-call | tf_op jit(solution)/shard_map/whiten/pallas_call | solution.py:173
  91.1 2.1 %collective-permute-start.15 = (bf16[64,64,128]{2,1,0:T(8,128)(2,1)S(1)}, bf16[64,64,128]{2,1,0:T(8,128)(2,1)S(1)}, u32[]{:S(2)}, u32[]{:S(2)}) collective-permute-start(bf16[64,64,128]{2,1,0:T(8,128)(2,1)S(1)} %get-tuple-element.20), channel_id=1, source_target_pairs={{0,16},{16,0},{32,48},{48,32},{64,80},{80,64},{96,112},{112,96},{1... | collective-permute-start | bytes 3145736 | tf_op jit(solution)/shard_map/ppermute | solution.py:340
  93.9 3.0 %collective-permute-start.14 = (bf16[32,64,128]{2,1,0:T(8,128)(2,1)}, bf16[32,64,128]{2,1,0:T(8,128)(2,1)S(1)}, u32[]{:S(2)}, u32[]{:S(2)}) collective-permute-start(bf16[32,64,128]{2,1,0:T(8,128)(2,1)} %collective-permute-done.13.refs_5_), channel_id=1, source_target_pairs={{0,96},{16,112},{32,0},{48,16},{64,32},{80,48},{96,64},{112,80},{1... | collective-permute-start | bytes 1572872 | tf_op jit(solution)/shard_map/ppermute | solution.py:342
  97.7 5.8 %shard_map.55.refs_5_ = f32[512,512]{1,0:T(8,128)S(1)} custom-call(s32[1]{0:T(128)} %bitcast.31.count_ref, s32[512]{0:T(512)S(1)} %get-tuple-element.47.src_ref, s32[512]{0:T(512)S(1)} %get-tuple-element.48.rcv_ref, s32[512]{0:T(512)S(1)} %get-tuple-element.46.slot_ref, bf16[32,64,128]{2,1,0:T(8,128)(2,1)} %get-tuple-element.18.refs_0_, ...), custom_call_target="tpu_custom_call" | custom-call | tf_op jit(solution)/shard_map/pallas_call | solution.py:287
  103.6 5.0 %collective-permute-done.14.refs_1_ = bf16[32,64,128]{2,1,0:T(8,128)(2,1)S(1)} collective-permute-done((bf16[32,64,128]{2,1,0:T(8,128)(2,1)}, bf16[32,64,128]{2,1,0:T(8,128)(2,1)S(1)}, u32[]{:S(2)}, u32[]{:S(2)}) %collective-permute-start.14) | collective-permute-done | bytes 524320 | tf_op jit(solution)/shard_map/ppermute | solution.py:342
  108.5 3.5 %shard_map.56 = bf16[512,512]{1,0:T(8,128)(2,1)S(1)} custom-call(s32[1]{0:T(128)} %bitcast.22.count_ref, s32[512]{0:T(512)S(1)} %get-tuple-element.50.src_ref, s32[512]{0:T(512)S(1)} %get-tuple-element.51.rcv_ref, s32[512]{0:T(512)S(1)} %get-tuple-element.49.slot_ref, bf16[32,64,128]{2,1,0:T(8,128)(2,1)} %collective-permute-done.12.refs_0_, ...), custom_call_target="tpu_custom_call" | custom-call | tf_op jit(solution)/shard_map/pallas_call | solution.py:287
  113.0 11.7 %all-to-all-start.2 = ((bf16[128,4,512]{2,1,0:T(4,128)(2,1)}), bf16[128,4,512]{2,1,0:T(4,128)(2,1)S(1)}, u32[]{:S(2)}, u32[]{:S(2)}) async-start(bf16[128,4,512]{2,1,0:T(4,128)(2,1)} %reshape.808), calls=%async_computation.2 | async-start | bytes 1048576 | tf_op jit(solution)/shard_map/all_to_all | solution.py:445
  124.7 14.1 %all-to-all-done.2 = bf16[128,4,512]{2,1,0:T(4,128)(2,1)S(1)} async-done(((bf16[128,4,512]{2,1,0:T(4,128)(2,1)}), bf16[128,4,512]{2,1,0:T(4,128)(2,1)S(1)}, u32[]{:S(2)}, u32[]{:S(2)}) %all-to-all-start.2) | async-done | bytes 524320 | tf_op jit(solution)/shard_map/all_to_all | solution.py:445
  139.0 1.0 fusion.7
  (74 shorter events, 13.2 us)
Async XLA Ops:
  2.3 6.7 %collective-permute-start = (s32[130]{0:T(256)S(1)}, s32[130]{0:T(256)S(1)}, u32[]{:S(2)}, u32[]{:S(2)}) collective-permute-start(s32[130]{0:T(256)S(1)} %pad_add_fusion.4), channel_id=1, source_target_pairs={{0,1},{1,2},{2,3},{3,0},{4,5},{5,6},{6,7},{7,4},{8,9},{9,10},{10,1... | collective-permute-start | bytes 1568 | tf_op jit(solution)/shard_map/ppermute | solution.py:345
  4.4 4.6 %collective-permute-start.1 = (s32[130]{0:T(256)S(1)}, s32[130]{0:T(256)S(1)}, u32[]{:S(2)}, u32[]{:S(2)}) collective-permute-start(s32[130]{0:T(256)S(1)} %pad_add_fusion.4), channel_id=1, source_target_pairs={{0,2},{1,3},{2,0},{3,1},{4,6},{5,7},{6,4},{7,5},{8,10},{9,11},{10,... | collective-permute-start | bytes 1568 | tf_op jit(solution)/shard_map/ppermute | solution.py:345
  6.8 2.7 %collective-permute-start.2 = (s32[130]{0:T(256)S(1)}, s32[130]{0:T(256)S(1)}, u32[]{:S(2)}, u32[]{:S(2)}) collective-permute-start(s32[130]{0:T(256)S(1)} %pad_add_fusion.4), channel_id=1, source_target_pairs={{0,3},{1,0},{2,1},{3,2},{4,7},{5,4},{6,5},{7,6},{8,11},{9,8},{10,9... | collective-permute-start | bytes 1568 | tf_op jit(solution)/shard_map/ppermute | solution.py:345
  9.6 5.7 %collective-permute-start.3 = (s32[4,130]{1,0:T(4,128)S(1)}, s32[4,130]{1,0:T(4,128)S(1)}, u32[]{:S(2)}, u32[]{:S(2)}) collective-permute-start(s32[4,130]{1,0:T(4,128)S(1)} %get-tuple-element.41), channel_id=1, source_target_pairs={{0,4},{1,5},{2,6},{3,7},{4,8},{5,9},{6,10},{7,11},{8,12},{9,13},{1... | collective-permute-start | bytes 6248 | tf_op jit(solution)/shard_map/ppermute | solution.py:344
  11.3 4.3 %collective-permute-start.4 = (s32[4,130]{1,0:T(4,128)S(1)}, s32[4,130]{1,0:T(4,128)S(1)}, u32[]{:S(2)}, u32[]{:S(2)}) collective-permute-start(s32[4,130]{1,0:T(4,128)S(1)} %get-tuple-element.41), channel_id=1, source_target_pairs={{0,8},{1,9},{2,10},{3,11},{4,12},{5,13},{6,14},{7,15},{8,0},{9,1},... | collective-permute-start | bytes 6248 | tf_op jit(solution)/shard_map/ppermute | solution.py:344
  14.6 2.5 %collective-permute-start.5 = (s32[4,130]{1,0:T(4,128)S(1)}, s32[4,130]{1,0:T(4,128)S(1)}, u32[]{:S(2)}, u32[]{:S(2)}) collective-permute-start(s32[4,130]{1,0:T(4,128)S(1)} %get-tuple-element.41), channel_id=1, source_target_pairs={{0,12},{1,13},{2,14},{3,15},{4,0},{5,1},{6,2},{7,3},{8,4},{9,5},{1... | collective-permute-start | bytes 6248 | tf_op jit(solution)/shard_map/ppermute | solution.py:344
  21.6 18.7 %all-to-all-start = ((bf16[16,32,1024]{2,1,0:T(8,128)(2,1)}), bf16[16,32,1024]{2,1,0:T(8,128)(2,1)S(1)}, u32[]{:S(2)}, u32[]{:S(2)}) async-start(bf16[16,32,1024]{2,1,0:T(8,128)(2,1)} %pick.1), calls=%async_computation | async-start | bytes 2097152 | tf_op jit(solution)/shard_map/all_to_all | solution.py:380
  40.3 1.0 copy-start
  41.3 41.3 %all-to-all-start.1 = ((bf16[16,64,1024]{2,1,0:T(8,128)(2,1)}), bf16[16,64,1024]{2,1,0:T(8,128)(2,1)}, u32[]{:S(2)}, u32[]{:S(2)}) async-start(bf16[16,64,1024]{2,1,0:T(8,128)(2,1)} %bitcast.29), calls=%async_computation.1 | async-start | bytes 4194304 | tf_op jit(solution)/shard_map/all_to_all | solution.py:382
  51.9 17.0 %collective-permute-start.10 = (bf16[32,64,128]{2,1,0:T(8,128)(2,1)S(1)}, bf16[32,64,128]{2,1,0:T(8,128)(2,1)}, u32[]{:S(2)}, u32[]{:S(2)}) collective-permute-start(bf16[32,64,128]{2,1,0:T(8,128)(2,1)S(1)} %get-tuple-element.15), channel_id=1, source_target_pairs={{0,16},{16,0},{32,48},{48,32},{64,80},{80,64},{96,112},{112,96},{1... | collective-permute-start | bytes 1572872 | tf_op jit(solution)/shard_map/ppermute | solution.py:340
  57.0 5.0 %collective-permute-start.6 = (s32[4,4,128]{2,1,0:T(4,128)S(1)}, s32[4,4,128]{2,1,0:T(4,128)S(1)}, u32[]{:S(2)}, u32[]{:S(2)}) collective-permute-start(s32[4,4,128]{2,1,0:T(4,128)S(1)} %get-tuple-element.39), channel_id=1, source_target_pairs={{0,32},{16,48},{32,64},{48,80},{64,96},{80,112},{96,0},{112,16},{1... | collective-permute-start | bytes 24584 | tf_op jit(solution)/shard_map/ppermute | solution.py:342
  58.3 4.4 %collective-permute-start.7 = (s32[4,4,128]{2,1,0:T(4,128)S(1)}, s32[4,4,128]{2,1,0:T(4,128)S(1)}, u32[]{:S(2)}, u32[]{:S(2)}) collective-permute-start(s32[4,4,128]{2,1,0:T(4,128)S(1)} %get-tuple-element.39), channel_id=1, source_target_pairs={{0,64},{16,80},{32,96},{48,112},{64,0},{80,16},{96,32},{112,48},{1... | collective-permute-start | bytes 24584 | tf_op jit(solution)/shard_map/ppermute | solution.py:342
  60.9 2.9 %collective-permute-start.8 = (s32[4,4,128]{2,1,0:T(4,128)S(1)}, s32[4,4,128]{2,1,0:T(4,128)S(1)}, u32[]{:S(2)}, u32[]{:S(2)}) collective-permute-start(s32[4,4,128]{2,1,0:T(4,128)S(1)} %get-tuple-element.39), channel_id=1, source_target_pairs={{0,96},{16,112},{32,0},{48,16},{64,32},{80,48},{96,64},{112,80},{1... | collective-permute-start | bytes 24584 | tf_op jit(solution)/shard_map/ppermute | solution.py:342
  63.9 2.3 %collective-permute-start.9 = (s32[4,4,4,128]{3,2,1,0:T(4,128)S(1)}, s32[4,4,4,128]{3,2,1,0:T(4,128)S(1)}, u32[]{:S(2)}, u32[]{:S(2)}) collective-permute-start(s32[4,4,4,128]{3,2,1,0:T(4,128)S(1)} %get-tuple-element.37), channel_id=1, source_target_pairs={{0,16},{16,0},{32,48},{48,32},{64,80},{80,64},{96,112},{112,96},{1... | collective-permute-start | bytes 98312 | tf_op jit(solution)/shard_map/ppermute | solution.py:340
  66.2 14.7 %collective-permute-start.11 = (bf16[32,64,128]{2,1,0:T(8,128)(2,1)}, bf16[32,64,128]{2,1,0:T(8,128)(2,1)}, u32[]{:S(2)}, u32[]{:S(2)}) collective-permute-start(bf16[32,64,128]{2,1,0:T(8,128)(2,1)} %get-tuple-element.18.refs_0_), channel_id=1, source_target_pairs={{0,32},{16,48},{32,64},{48,80},{64,96},{80,112},{96,0},{112,16},{1... | collective-permute-start | bytes 1572872 | tf_op jit(solution)/shard_map/ppermute | solution.py:342
  66.2 31.5 %collective-permute-start.17 = (bf16[32,64,128]{2,1,0:T(8,128)(2,1)}, bf16[32,64,128]{2,1,0:T(8,128)(2,1)}, u32[]{:S(2)}, u32[]{:S(2)}) collective-permute-start(bf16[32,64,128]{2,1,0:T(8,128)(2,1)} %get-tuple-element.18.refs_0_), channel_id=1, source_target_pairs={{0,96},{16,112},{32,0},{48,16},{64,32},{80,48},{96,64},{112,80},{1... | collective-permute-start | bytes 1572872 | tf_op jit(solution)/shard_map/ppermute | solution.py:342
  70.2 23.8 %collective-permute-start.13 = (bf16[32,64,128]{2,1,0:T(8,128)(2,1)}, bf16[32,64,128]{2,1,0:T(8,128)(2,1)}, u32[]{:S(2)}, u32[]{:S(2)}) collective-permute-start(bf16[32,64,128]{2,1,0:T(8,128)(2,1)} %collective-permute-done.10.refs_1_), channel_id=1, source_target_pairs={{0,96},{16,112},{32,0},{48,16},{64,32},{80,48},{96,64},{112,80},{1... | collective-permute-start | bytes 1572872 | tf_op jit(solution)/shard_map/ppermute | solution.py:342
  71.3 26.4 %collective-permute-start.16 = (bf16[32,64,128]{2,1,0:T(8,128)(2,1)}, bf16[32,64,128]{2,1,0:T(8,128)(2,1)}, u32[]{:S(2)}, u32[]{:S(2)}) collective-permute-start(bf16[32,64,128]{2,1,0:T(8,128)(2,1)} %collective-permute-done.10.refs_1_), channel_id=1, source_target_pairs={{0,32},{16,48},{32,64},{48,80},{64,96},{80,112},{96,0},{112,16},{1... | collective-permute-start | bytes 1572872 | tf_op jit(solution)/shard_map/ppermute | solution.py:342
  80.8 22.7 %collective-permute-start.12 = (bf16[32,64,128]{2,1,0:T(8,128)(2,1)}, bf16[32,64,128]{2,1,0:T(8,128)(2,1)}, u32[]{:S(2)}, u32[]{:S(2)}) collective-permute-start(bf16[32,64,128]{2,1,0:T(8,128)(2,1)} %collective-permute-done.11.refs_2_), channel_id=1, source_target_pairs={{0,32},{16,48},{32,64},{48,80},{64,96},{80,112},{96,0},{112,16},{1... | collective-permute-start | bytes 1572872 | tf_op jit(solution)/shard_map/ppermute | solution.py:342
  91.1 6.6 %collective-permute-start.15 = (bf16[64,64,128]{2,1,0:T(8,128)(2,1)S(1)}, bf16[64,64,128]{2,1,0:T(8,128)(2,1)S(1)}, u32[]{:S(2)}, u32[]{:S(2)}) collective-permute-start(bf16[64,64,128]{2,1,0:T(8,128)(2,1)S(1)} %get-tuple-element.20), channel_id=1, source_target_pairs={{0,16},{16,0},{32,48},{48,32},{64,80},{80,64},{96,112},{112,96},{1... | collective-permute-start | bytes 3145736 | tf_op jit(solution)/shard_map/ppermute | solution.py:340
  93.9 14.6 %collective-permute-start.14 = (bf16[32,64,128]{2,1,0:T(8,128)(2,1)}, bf16[32,64,128]{2,1,0:T(8,128)(2,1)S(1)}, u32[]{:S(2)}, u32[]{:S(2)}) collective-permute-start(bf16[32,64,128]{2,1,0:T(8,128)(2,1)} %collective-permute-done.13.refs_5_), channel_id=1, source_target_pairs={{0,96},{16,112},{32,0},{48,16},{64,32},{80,48},{96,64},{112,80},{1... | collective-permute-start | bytes 1572872 | tf_op jit(solution)/shard_map/ppermute | solution.py:342
  112.0 26.9 %copy-start.1 = (s32[128,1]{0,1:T(1,128)S(1)}, s32[128,1]{0,1:T(1,128)}, u32[]{:S(2)}) copy-start(s32[128,1]{0,1:T(1,128)} %param.8) | copy-start | bytes 1540
  113.0 25.9 %all-to-all-start.2 = ((bf16[128,4,512]{2,1,0:T(4,128)(2,1)}), bf16[128,4,512]{2,1,0:T(4,128)(2,1)S(1)}, u32[]{:S(2)}, u32[]{:S(2)}) async-start(bf16[128,4,512]{2,1,0:T(4,128)(2,1)} %reshape.808), calls=%async_computation.2 | async-start | bytes 1048576 | tf_op jit(solution)/shard_map/all_to_all | solution.py:445

commit v3 on v2

--- a/solution.py
+++ b/solution.py
@@ -97,7 +97,19 @@
     return out
 
 
-def whiten_kernel(core_ref, x_ref, tw_ref, upper_ref, lower_ref, mine_ref, other_ref, hi_ref, lo_ref):
+def whiten_kernel(core_ref, x_ref, tw_ref, upper_ref, lower_ref, mine_ref, other_ref, *scratch):
+    count = x_ref.shape[0] // SIDE
+    parts = [(x_ref.at[n * SIDE:(n + 1) * SIDE], scratch[2 * n], scratch[2 * n + 1]) for n in range(count)]
+    butterflies(tw_ref, *parts[0])
+    for n in range(count):
+        spectra = products(x_ref.shape[1], upper_ref, lower_ref, *parts[n][1:])
+        if n + 1 < count:
+            butterflies(tw_ref, *parts[n + 1])
+        at = slice(n * HALF_ROWS, (n + 1) * HALF_ROWS)
+        finish(core_ref, x_ref.shape[1], spectra, mine_ref.at[:, at], other_ref.at[:, at])
+
+
+def butterflies(tw_ref, x_ref, hi_ref, lo_ref):
     rows = x_ref.shape[1]
     half = RADIX // 2
     where = lambda f: (f - 1) % (half + 1)
@@ -126,6 +138,10 @@
                     hi_ref[row, at] = hi
                     lo_ref[row, at] = (part - hi.astype(jnp.float32)).astype(jnp.bfloat16)
 
+
+def products(rows, upper_ref, lower_ref, hi_ref, lo_ref):
+    half = RADIX // 2
+
     def spectrum(row, depth, width):
         hi, lo = hi_ref[row, :depth], lo_ref[row, :depth]
         upper, lower = upper_ref[:depth, :width], lower_ref[:depth, :width]
@@ -136,6 +152,12 @@
     most = spectrum(slice(0, (half - 1) * rows), 2 * INNER, 4 * LANES)
     middle = spectrum(slice((half - 1) * rows, half * rows), 2 * INNER, 2 * LANES)
     first = spectrum(slice(half * rows, (half + 1) * rows), INNER, 2 * LANES)
+    return first, middle, most
+
+
+def finish(core_ref, rows, spectra, mine_ref, other_ref):
+    half = RADIX // 2
+    first, middle, most = spectra
 
     def part(f, k):
         if f == 0:
@@ -164,29 +186,25 @@
         other_ref[r] = jnp.where(low, halves[1], halves[0]).astype(jnp.bfloat16)
 
 
-def whiten(core, samples, twiddle, upper, lower):
-    samples = pltpu.with_memory_space_constraint(samples, pltpu.MemorySpace.HBM)
+def whiten(core, samples, twiddle, upper, lower, per):
     rows = samples.shape[1]
     out = jax.ShapeDtypeStruct((rows, NSEG * HALF_ROWS, LANES), jnp.bfloat16)
-    spec = pl.BlockSpec((rows, HALF_ROWS, LANES), lambda s, c: (0, s, 0))
+    spec = pl.BlockSpec((rows, per * HALF_ROWS, LANES), lambda s, c: (0, s, 0))
     count = RADIX // 2 + 1
     return pl.pallas_call(
         whiten_kernel,
         out_shape=(out, out),
         grid_spec=pltpu.PrefetchScalarGridSpec(
             num_scalar_prefetch=1,
-            grid=(NSEG,),
+            grid=(NSEG // per,),
             in_specs=[
-                pl.BlockSpec((SIDE, rows, SEGLEN // SIDE), lambda s, c: (s, 0, 0)),
+                pl.BlockSpec((per * SIDE, rows, SEGLEN // SIDE), lambda s, c: (s, 0, 0)),
                 pl.BlockSpec((2, RADIX, INNER), lambda s, c: (0, 0, 0)),
                 pl.BlockSpec((2 * INNER, 4 * LANES), lambda s, c: (0, 0)),
                 pl.BlockSpec((2 * INNER, 4 * LANES), lambda s, c: (0, 0)),
             ],
             out_specs=(spec, spec),
-            scratch_shapes=[
-                pltpu.VMEM((count * rows, 2 * INNER), jnp.bfloat16),
-                pltpu.VMEM((count * rows, 2 * INNER), jnp.bfloat16),
-            ],
+            scratch_shapes=[pltpu.VMEM((count * rows, 2 * INNER), jnp.bfloat16)] * (2 * per),
         ),
         compiler_params=pltpu.CompilerParams(vmem_limit_bytes=48 << 20),
         name="whiten",
@@ -365,10 +383,8 @@
     per = source_ids.shape[0]
     holder = pair_holder[:, 0]
     order = jnp.arange(pairs, dtype=jnp.int32)
-    same = (holder[:, None] == holder[None, :]) & (order[None, :] < order[:, None])
-    rank = jnp.sum(same.astype(jnp.int32), axis=1)
-    packed = ((holder * 2 + rank) * channels + pair_receiver) * 256 + pair_source
-    notes = jnp.concatenate([packed, source_ids - gx * groups * channels])
+    packed = (holder * channels + pair_receiver) * 256 + pair_source
+    notes = jnp.concatenate([packed, source_ids])
     notes = gather_ring(notes, "x")
     notes = gather_ring(notes, "z")
     ids, notes = notes[:, :, pairs:].reshape(groups, per), notes[:, :, :pairs]
@@ -376,6 +392,7 @@
     step = jnp.arange(groups, dtype=jnp.int32)
     mate = (place["z"] - step // SIDE) % SIDE * SIDE + (place["x"] - step % SIDE) % SIDE
     wanted = jnp.sum(jnp.where(mate[None, :, None] == step[:, None, None], ids[None], 0), axis=1).reshape(-1)
+    wanted = wanted - gx * groups * channels
     first = pick_rows(wanted, raw_window, taper, groups)
     first = lax.all_to_all(first, "gy", split_axis=0, concat_axis=0, tiled=True)
     tapered = (raw_window * taper[None, :]).astype(jnp.bfloat16)
@@ -385,7 +402,7 @@
 
     twiddle = twiddle_table()
     upper, lower = inner_table()
-    near0, away = whiten(core.reshape(1), first, twiddle, upper, lower)
+    near0, away = whiten(core.reshape(1), first, twiddle, upper, lower, NSEG)
     near1 = shift(away, "core", 1)
     ahead0 = shift(near0, "y", 1)
     behind0 = shift(near0, "y", 3)
@@ -397,7 +414,8 @@
     notes, late, _ = lax.optimization_barrier((notes, core, near1))
     table = inverse_table(late, late - core)
 
-    mine, other = whiten(core.reshape(1), samples, twiddle, upper, lower)
+    samples = pltpu.with_memory_space_constraint(samples, pltpu.MemorySpace.HBM)
+    mine, other = whiten(core.reshape(1), samples, twiddle, upper, lower, 2)
     sister = shift(other, "core", 1)
 
     dev = jnp.arange(devices, dtype=jnp.int32)
@@ -406,13 +424,20 @@
         + (place["z"] - dev // SIDE % SIDE) % SIDE * SIDE
         + (place["x"] - dev % SIDE) % SIDE
     )
-    key = notes // (channels * 256)
-    low = notes % (channels * 256)
-    kinds = jnp.stack([here * 2, here * 2 + 1, (here ^ groups) * 2, (here ^ groups) * 2 + 1])
-    found = jnp.sum(jnp.where(key[None] == kinds[:, None, None], low[None] + 1, 0), axis=2)
+    each = channels * 256
+    key = notes // each
+    entry = order[None, :] * each + notes % each + 1
+    first_last = []
+    for name in (here, here ^ groups):
+        match = key == name
+        high = jnp.max(jnp.where(match, entry, 0), axis=1)
+        low = jnp.max(jnp.where(match, pairs * each + 1 - entry, 0), axis=1)
+        low = jnp.where(low > 0, pairs * each + 1 - low, 0)
+        first_last += [low, jnp.where(high > low, high, 0)]
+    found = jnp.stack(first_last)
     asked = jnp.sum(jnp.where(own[None, None, :] == dev[None, :, None], found[:, None, :], 0), axis=2)
     valid = asked > 0
-    asked = jnp.maximum(asked - 1, 0)
+    asked = jnp.maximum(asked - 1, 0) % each
     slots = asked.size
     source_no = asked % 256
     source_gx = source_no // (2 * groups)
@@ -444,6 +469,8 @@
     partial = correlate(far_kernel, far_lists, [far0, far1], receivers, [table, near], jnp.bfloat16, extra)
     returned = lax.all_to_all(partial.reshape(devices, 4, NLAG), ("gx", "gy"), split_axis=0, concat_axis=0, tiled=True)
     returned = returned.reshape(devices * 4, NLAG)
+    same = (holder[:, None] == holder[None, :]) & (order[None, :] < order[:, None])
+    rank = jnp.sum(same.astype(jnp.int32), axis=1)
     row = jnp.arange(4 * devices, dtype=jnp.int32)
     row_dev, row_rel, row_rank = row // 4, row // 2 % 2, row % 2
     row_holder = jnp.where(row_rel == 0, row_dev, row_dev ^ groups)

time: 141 us -> 136 us (0.965)
  Pallas kernels: 27.7 us -> 25.3 us
    pallas_call x2, Pallas kernels: 14.7 us -> 12.4 us  [whiten(): pl.pallas_call(whiten_kernel, out_shape=(out, out), grid_spec=pltpu.Prefe...]
  transfers between devices with their start and end apart: 21 -> 21, of which waited for: 10 -> 11; matrix products, arithmetic and copies ran while one was open for 8% -> 8% of each run, Pallas kernels for 15% -> 13%
where the time goes in v3:
time: 136 us; the launch traced here: 135 us
  starting transfers between devices  53.5 us (39%)
  waiting for transfers between devices  41 us (30%)
  Pallas kernels  25.3 us (19%)
  other arithmetic  12.3 us (9%)
  local copies, waits for them, and re-layouts  1.82 us (1%)
    ppermute x9, waiting for transfers between devices, shift(): lax.ppermute(value, 'gx', [(g, (g + 2 * step) % (2 * SIDE)) for g in rang...  15.7 us
    all_to_all x1, waiting for transfers between devices, program(): lax.all_to_all(partial.reshape(devices, 4, NLAG), ('gx', 'gy'), split_axi...  13.9 us
    pallas_call x2, Pallas kernels, whiten(): pl.pallas_call(whiten_kernel, out_shape=(out, out), grid_spec=pltpu.Prefe...  12.4 us
    ppermute x9, starting transfers between devices, shift(): lax.ppermute(value, 'gx', [(g, (g + 2 * step) % (2 * SIDE)) for g in rang...  12.2 us
    all_to_all x1, starting transfers between devices, program(): lax.all_to_all(partial.reshape(devices, 4, NLAG), ('gx', 'gy'), split_axi...  11.8 us
    pallas_call x2, Pallas kernels, correlate(): pl.pallas_call(kernel, out_shape=jax.ShapeDtypeStruct((slots, NLAG), dtyp...  9.25 us
    ppermute x3, starting transfers between devices, shift(): return lax.ppermute(value, 'gx', [(g, g ^ 1) for g in range(2 * SIDE)])  8.58 us
    all_to_all x1, waiting for transfers between devices, program(): first = lax.all_to_all(first, 'gy', split_axis=0, concat_axis=0, tiled=True)  8.26 us
  transfers between devices with their start and end apart: 21, of which 11 were waited for; matrix products, arithmetic and copies ran while one was open for 8% of the time, Pallas kernels for 13%

profile of v3, /device:TPU:1, one launch (start us, length us, event | category | flops | bytes accessed | tf_op | source)
XLA Modules:
  0.0 135.2 jit_solution(15193869252626601428)
XLA Ops:
  1.4 2.0 %collective-permute-start = (s32[130]{0:T(256)S(1)}, s32[130]{0:T(256)S(1)}, u32[]{:S(2)}, u32[]{:S(2)}) collective-permute-start(s32[130]{0:T(256)S(1)} %pad_add_fusion.5), channel_id=1, source_target_pairs={{0,1},{1,2},{2,3},{3,0},{4,5},{5,6},{6,7},{7,4},{8,9},{9,10},{10,1... | collective-permute-start | bytes 1568 | tf_op jit(solution)/shard_map/ppermute | solution.py:363
  3.4 2.5 %collective-permute-start.1 = (s32[130]{0:T(256)S(1)}, s32[130]{0:T(256)S(1)}, u32[]{:S(2)}, u32[]{:S(2)}) collective-permute-start(s32[130]{0:T(256)S(1)} %pad_add_fusion.5), channel_id=1, source_target_pairs={{0,2},{1,3},{2,0},{3,1},{4,6},{5,7},{6,4},{7,5},{8,10},{9,11},{10,... | collective-permute-start | bytes 1568 | tf_op jit(solution)/shard_map/ppermute | solution.py:363
  5.8 1.2 collective-permute-start.2
  8.6 1.7 %collective-permute-start.3 = (s32[4,130]{1,0:T(4,128)S(1)}, s32[4,130]{1,0:T(4,128)S(1)}, u32[]{:S(2)}, u32[]{:S(2)}) collective-permute-start(s32[4,130]{1,0:T(4,128)S(1)} %get-tuple-element.48), channel_id=1, source_target_pairs={{0,4},{1,5},{2,6},{3,7},{4,8},{5,9},{6,10},{7,11},{8,12},{9,13},{1... | collective-permute-start | bytes 6248 | tf_op jit(solution)/shard_map/ppermute | solution.py:362
  10.3 3.3 %collective-permute-start.4 = (s32[4,130]{1,0:T(4,128)S(1)}, s32[4,130]{1,0:T(4,128)S(1)}, u32[]{:S(2)}, u32[]{:S(2)}) collective-permute-start(s32[4,130]{1,0:T(4,128)S(1)} %get-tuple-element.48), channel_id=1, source_target_pairs={{0,8},{1,9},{2,10},{3,11},{4,12},{5,13},{6,14},{7,15},{8,0},{9,1},... | collective-permute-start | bytes 6248 | tf_op jit(solution)/shard_map/ppermute | solution.py:362
  14.6 1.4 %collective-permute-done.5 = s32[4,130]{1,0:T(4,128)S(1)} collective-permute-done((s32[4,130]{1,0:T(4,128)S(1)}, s32[4,130]{1,0:T(4,128)S(1)}, u32[]{:S(2)}, u32[]{:S(2)}) %collective-permute-start.5) | collective-permute-done | bytes 2112 | tf_op jit(solution)/shard_map/ppermute | solution.py:362
  16.9 3.6 %pick.1 = bf16[16,32,1024]{2,1,0:T(8,128)(2,1)} custom-call(s32[32]{0:T(128)} %sub.274.wanted_ref, f32[1024,1024]{1,0:T(8,128)} %raw_ref.1, f32[1,1024]{1,0:T(1,128)} %fusion.65.taper_ref), custom_call_target="tpu_custom_call" | custom-call | tf_op jit(solution)/shard_map/pick/pallas_call | solution.py:342
  20.6 5.1 %all-to-all-start = ((bf16[16,32,1024]{2,1,0:T(8,128)(2,1)}), bf16[16,32,1024]{2,1,0:T(8,128)(2,1)S(1)}, u32[]{:S(2)}, u32[]{:S(2)}) async-start(bf16[16,32,1024]{2,1,0:T(8,128)(2,1)} %pick.1), calls=%async_computation | async-start | bytes 2097152 | tf_op jit(solution)/shard_map/all_to_all | solution.py:397
  25.7 1.0 broadcast_multiply_fusion.1
  26.9 4.1 %multiply_convert_fusion = bf16[1024,1024]{1,0:T(8,128)(2,1)} fusion(f32[1024,1024]{1,0:T(8,128)} %raw_ref.1, f32[1024]{0:T(1024)S(1)} %fusion.60), kind=kLoop, calls=%fused_computation | loop fusion | flops 2097152 | bytes 6295552 | tf_op jit(solution)/shard_map/convert_element_type | solution.py:398
  31.0 8.3 %all-to-all-done.x_ref = bf16[16,32,1024]{2,1,0:T(8,128)(2,1)S(1)} async-done(((bf16[16,32,1024]{2,1,0:T(8,128)(2,1)}), bf16[16,32,1024]{2,1,0:T(8,128)(2,1)S(1)}, u32[]{:S(2)}, u32[]{:S(2)}) %all-to-all-start) | async-done | bytes 1048608 | tf_op jit(solution)/shard_map/all_to_all | solution.py:397
  39.3 4.4 %all-to-all-start.1 = ((bf16[16,64,1024]{2,1,0:T(8,128)(2,1)}), bf16[16,64,1024]{2,1,0:T(8,128)(2,1)}, u32[]{:S(2)}, u32[]{:S(2)}) async-start(bf16[16,64,1024]{2,1,0:T(8,128)(2,1)} %bitcast.63), calls=%async_computation.1 | async-start | bytes 4194304 | tf_op jit(solution)/shard_map/all_to_all | solution.py:399
  43.7 4.5 %whiten.2 = (bf16[32,64,128]{2,1,0:T(8,128)(2,1)}, bf16[32,64,128]{2,1,0:T(8,128)(2,1)S(1)}) custom-call(s32[1]{0:T(128)} %bitcast.16.core_ref, bf16[16,32,1024]{2,1,0:T(8,128)(2,1)S(1)} %all-to-all-done.x_ref, f32[2,16,256]{2,1,0:T(8,128)S(1)} %pad_maximum_fusion.1.tw_ref, bf16[512,512]{1,0:T(8,128)(2,1)S(1)} %fusion.11.upper_ref, ...), custom_call_target="tpu_custom_call" | custom-call | tf_op jit(solution)/shard_map/whiten/pallas_call | solution.py:194
  48.3 5.1 %collective-permute-start.10 = (bf16[32,64,128]{2,1,0:T(8,128)(2,1)S(1)}, bf16[32,64,128]{2,1,0:T(8,128)(2,1)}, u32[]{:S(2)}, u32[]{:S(2)}) collective-permute-start(bf16[32,64,128]{2,1,0:T(8,128)(2,1)S(1)} %get-tuple-element.15), channel_id=1, source_target_pairs={{0,16},{16,0},{32,48},{48,32},{64,80},{80,64},{96,112},{112,96},{1... | collective-permute-start | bytes 1572872 | tf_op jit(solution)/shard_map/ppermute | solution.py:358
  53.4 1.3 collective-permute-start.6
  54.7 2.6 %collective-permute-start.7 = (s32[4,4,128]{2,1,0:T(4,128)S(1)}, s32[4,4,128]{2,1,0:T(4,128)S(1)}, u32[]{:S(2)}, u32[]{:S(2)}) collective-permute-start(s32[4,4,128]{2,1,0:T(4,128)S(1)} %get-tuple-element.46), channel_id=1, source_target_pairs={{0,64},{16,80},{32,96},{48,112},{64,0},{80,16},{96,32},{112,48},{1... | collective-permute-start | bytes 24584 | tf_op jit(solution)/shard_map/ppermute | solution.py:360
  57.3 1.1 collective-permute-start.8
  59.1 1.1 collective-permute-done.8
  60.2 1.4 %collective-permute-start.9 = (s32[4,4,4,128]{3,2,1,0:T(4,128)S(1)}, s32[4,4,4,128]{3,2,1,0:T(4,128)S(1)}, u32[]{:S(2)}, u32[]{:S(2)}) collective-permute-start(s32[4,4,4,128]{3,2,1,0:T(4,128)S(1)} %get-tuple-element.44), channel_id=1, source_target_pairs={{0,16},{16,0},{32,48},{48,32},{64,80},{80,64},{96,112},{112,96},{1... | collective-permute-start | bytes 98312 | tf_op jit(solution)/shard_map/ppermute | solution.py:358
  62.5 2.7 %collective-permute-start.17 = (bf16[32,64,128]{2,1,0:T(8,128)(2,1)}, bf16[32,64,128]{2,1,0:T(8,128)(2,1)}, u32[]{:S(2)}, u32[]{:S(2)}) collective-permute-start(bf16[32,64,128]{2,1,0:T(8,128)(2,1)} %get-tuple-element.18.refs_0_), channel_id=1, source_target_pairs={{0,96},{16,112},{32,0},{48,16},{64,32},{80,48},{96,64},{112,80},{1... | collective-permute-start | bytes 1572872 | tf_op jit(solution)/shard_map/ppermute | solution.py:360
  65.6 1.1 fusion.18
  66.7 1.1 collective-permute-start.13
  68.2 8.9 %collective-permute-done.11.refs_2_ = bf16[32,64,128]{2,1,0:T(8,128)(2,1)} collective-permute-done((bf16[32,64,128]{2,1,0:T(8,128)(2,1)}, bf16[32,64,128]{2,1,0:T(8,128)(2,1)}, u32[]{:S(2)}, u32[]{:S(2)}) %collective-permute-start.11) | collective-permute-done | bytes 524320 | tf_op jit(solution)/shard_map/ppermute | solution.py:360
  78.6 7.8 %whiten.3 = (bf16[64,64,128]{2,1,0:T(8,128)(2,1)S(1)}, bf16[64,64,128]{2,1,0:T(8,128)(2,1)S(1)}) custom-call(s32[1]{0:T(128)} %bitcast.16.core_ref, bf16[16,64,1024]{2,1,0:T(8,128)(2,1)} %all-to-all-done.1.x_ref, f32[2,16,256]{2,1,0:T(8,128)S(1)} %pad_maximum_fusion.1.tw_ref, bf16[512,512]{1,0:T(8,128)(2,1)S(1)} %fusion.11.upper_ref, ...), custom_call_target="tpu_custom_call" | custom-call | tf_op jit(solution)/shard_map/whiten/pallas_call | solution.py:194
  86.4 2.1 %collective-permute-start.15 = (bf16[64,64,128]{2,1,0:T(8,128)(2,1)S(1)}, bf16[64,64,128]{2,1,0:T(8,128)(2,1)S(1)}, u32[]{:S(2)}, u32[]{:S(2)}) collective-permute-start(bf16[64,64,128]{2,1,0:T(8,128)(2,1)S(1)} %get-tuple-element.20), channel_id=1, source_target_pairs={{0,16},{16,0},{32,48},{48,32},{64,80},{80,64},{96,112},{112,96},{1... | collective-permute-start | bytes 3145736 | tf_op jit(solution)/shard_map/ppermute | solution.py:358
  89.3 3.0 %collective-permute-start.14 = (bf16[32,64,128]{2,1,0:T(8,128)(2,1)}, bf16[32,64,128]{2,1,0:T(8,128)(2,1)S(1)}, u32[]{:S(2)}, u32[]{:S(2)}) collective-permute-start(bf16[32,64,128]{2,1,0:T(8,128)(2,1)} %collective-permute-done.13.refs_5_), channel_id=1, source_target_pairs={{0,96},{16,112},{32,0},{48,16},{64,32},{80,48},{96,64},{112,80},{1... | collective-permute-start | bytes 1572872 | tf_op jit(solution)/shard_map/ppermute | solution.py:360
  93.0 5.8 %shard_map.55.refs_5_ = f32[512,512]{1,0:T(8,128)S(1)} custom-call(s32[1]{0:T(128)} %bitcast.29.count_ref, s32[512]{0:T(512)S(1)} %get-tuple-element.54.src_ref, s32[512]{0:T(512)S(1)} %get-tuple-element.55.rcv_ref, s32[512]{0:T(512)S(1)} %get-tuple-element.53.slot_ref, bf16[32,64,128]{2,1,0:T(8,128)(2,1)} %get-tuple-element.18.refs_0_, ...), custom_call_target="tpu_custom_call" | custom-call | tf_op jit(solution)/shard_map/pallas_call | solution.py:305
  99.6 4.3 %collective-permute-done.14.refs_1_ = bf16[32,64,128]{2,1,0:T(8,128)(2,1)S(1)} collective-permute-done((bf16[32,64,128]{2,1,0:T(8,128)(2,1)}, bf16[32,64,128]{2,1,0:T(8,128)(2,1)S(1)}, u32[]{:S(2)}, u32[]{:S(2)}) %collective-permute-start.14) | collective-permute-done | bytes 524320 | tf_op jit(solution)/shard_map/ppermute | solution.py:360
  103.9 3.4 %shard_map.56 = bf16[512,512]{1,0:T(8,128)(2,1)S(1)} custom-call(s32[1]{0:T(128)} %bitcast.22.count_ref, s32[512]{0:T(512)S(1)} %get-tuple-element.57.src_ref, s32[512]{0:T(512)S(1)} %get-tuple-element.58.rcv_ref, s32[512]{0:T(512)S(1)} %get-tuple-element.56.slot_ref, bf16[32,64,128]{2,1,0:T(8,128)(2,1)} %collective-permute-done.12.refs_0_, ...), custom_call_target="tpu_custom_call" | custom-call | tf_op jit(solution)/shard_map/pallas_call | solution.py:305
  108.2 11.8 %all-to-all-start.2 = ((bf16[128,4,512]{2,1,0:T(4,128)(2,1)}), bf16[128,4,512]{2,1,0:T(4,128)(2,1)S(1)}, u32[]{:S(2)}, u32[]{:S(2)}) async-start(bf16[128,4,512]{2,1,0:T(4,128)(2,1)} %reshape.887), calls=%async_computation.2 | async-start | bytes 1048576 | tf_op jit(solution)/shard_map/all_to_all | solution.py:470
  120.2 13.9 %all-to-all-done.2 = bf16[128,4,512]{2,1,0:T(4,128)(2,1)S(1)} async-done(((bf16[128,4,512]{2,1,0:T(4,128)(2,1)}), bf16[128,4,512]{2,1,0:T(4,128)(2,1)S(1)}, u32[]{:S(2)}, u32[]{:S(2)}) %all-to-all-start.2) | async-done | bytes 524320 | tf_op jit(solution)/shard_map/all_to_all | solution.py:470
  134.2 1.0 fusion.7
  (77 shorter events, 12.1 us)
Async XLA Ops:
  1.4 6.6 %collective-permute-start = (s32[130]{0:T(256)S(1)}, s32[130]{0:T(256)S(1)}, u32[]{:S(2)}, u32[]{:S(2)}) collective-permute-start(s32[130]{0:T(256)S(1)} %pad_add_fusion.5), channel_id=1, source_target_pairs={{0,1},{1,2},{2,3},{3,0},{4,5},{5,6},{6,7},{7,4},{8,9},{9,10},{10,1... | collective-permute-start | bytes 1568 | tf_op jit(solution)/shard_map/ppermute | solution.py:363
  3.4 4.6 %collective-permute-start.1 = (s32[130]{0:T(256)S(1)}, s32[130]{0:T(256)S(1)}, u32[]{:S(2)}, u32[]{:S(2)}) collective-permute-start(s32[130]{0:T(256)S(1)} %pad_add_fusion.5), channel_id=1, source_target_pairs={{0,2},{1,3},{2,0},{3,1},{4,6},{5,7},{6,4},{7,5},{8,10},{9,11},{10,... | collective-permute-start | bytes 1568 | tf_op jit(solution)/shard_map/ppermute | solution.py:363
  5.8 2.7 %collective-permute-start.2 = (s32[130]{0:T(256)S(1)}, s32[130]{0:T(256)S(1)}, u32[]{:S(2)}, u32[]{:S(2)}) collective-permute-start(s32[130]{0:T(256)S(1)} %pad_add_fusion.5), channel_id=1, source_target_pairs={{0,3},{1,0},{2,1},{3,2},{4,7},{5,4},{6,5},{7,6},{8,11},{9,8},{10,9... | collective-permute-start | bytes 1568 | tf_op jit(solution)/shard_map/ppermute | solution.py:363
  8.6 5.7 %collective-permute-start.3 = (s32[4,130]{1,0:T(4,128)S(1)}, s32[4,130]{1,0:T(4,128)S(1)}, u32[]{:S(2)}, u32[]{:S(2)}) collective-permute-start(s32[4,130]{1,0:T(4,128)S(1)} %get-tuple-element.48), channel_id=1, source_target_pairs={{0,4},{1,5},{2,6},{3,7},{4,8},{5,9},{6,10},{7,11},{8,12},{9,13},{1... | collective-permute-start | bytes 6248 | tf_op jit(solution)/shard_map/ppermute | solution.py:362
  10.3 4.3 %collective-permute-start.4 = (s32[4,130]{1,0:T(4,128)S(1)}, s32[4,130]{1,0:T(4,128)S(1)}, u32[]{:S(2)}, u32[]{:S(2)}) collective-permute-start(s32[4,130]{1,0:T(4,128)S(1)} %get-tuple-element.48), channel_id=1, source_target_pairs={{0,8},{1,9},{2,10},{3,11},{4,12},{5,13},{6,14},{7,15},{8,0},{9,1},... | collective-permute-start | bytes 6248 | tf_op jit(solution)/shard_map/ppermute | solution.py:362
  13.6 2.5 %collective-permute-start.5 = (s32[4,130]{1,0:T(4,128)S(1)}, s32[4,130]{1,0:T(4,128)S(1)}, u32[]{:S(2)}, u32[]{:S(2)}) collective-permute-start(s32[4,130]{1,0:T(4,128)S(1)} %get-tuple-element.48), channel_id=1, source_target_pairs={{0,12},{1,13},{2,14},{3,15},{4,0},{5,1},{6,2},{7,3},{8,4},{9,5},{1... | collective-permute-start | bytes 6248 | tf_op jit(solution)/shard_map/ppermute | solution.py:362
  20.6 18.7 %all-to-all-start = ((bf16[16,32,1024]{2,1,0:T(8,128)(2,1)}), bf16[16,32,1024]{2,1,0:T(8,128)(2,1)S(1)}, u32[]{:S(2)}, u32[]{:S(2)}) async-start(bf16[16,32,1024]{2,1,0:T(8,128)(2,1)} %pick.1), calls=%async_computation | async-start | bytes 2097152 | tf_op jit(solution)/shard_map/all_to_all | solution.py:397
  39.3 39.3 %all-to-all-start.1 = ((bf16[16,64,1024]{2,1,0:T(8,128)(2,1)}), bf16[16,64,1024]{2,1,0:T(8,128)(2,1)}, u32[]{:S(2)}, u32[]{:S(2)}) async-start(bf16[16,64,1024]{2,1,0:T(8,128)(2,1)} %bitcast.63), calls=%async_computation.1 | async-start | bytes 4194304 | tf_op jit(solution)/shard_map/all_to_all | solution.py:399
  48.3 16.9 %collective-permute-start.10 = (bf16[32,64,128]{2,1,0:T(8,128)(2,1)S(1)}, bf16[32,64,128]{2,1,0:T(8,128)(2,1)}, u32[]{:S(2)}, u32[]{:S(2)}) collective-permute-start(bf16[32,64,128]{2,1,0:T(8,128)(2,1)S(1)} %get-tuple-element.15), channel_id=1, source_target_pairs={{0,16},{16,0},{32,48},{48,32},{64,80},{80,64},{96,112},{112,96},{1... | collective-permute-start | bytes 1572872 | tf_op jit(solution)/shard_map/ppermute | solution.py:358
  53.4 5.0 %collective-permute-start.6 = (s32[4,4,128]{2,1,0:T(4,128)S(1)}, s32[4,4,128]{2,1,0:T(4,128)S(1)}, u32[]{:S(2)}, u32[]{:S(2)}) collective-permute-start(s32[4,4,128]{2,1,0:T(4,128)S(1)} %get-tuple-element.46), channel_id=1, source_target_pairs={{0,32},{16,48},{32,64},{48,80},{64,96},{80,112},{96,0},{112,16},{1... | collective-permute-start | bytes 24584 | tf_op jit(solution)/shard_map/ppermute | solution.py:360
  54.7 4.4 %collective-permute-start.7 = (s32[4,4,128]{2,1,0:T(4,128)S(1)}, s32[4,4,128]{2,1,0:T(4,128)S(1)}, u32[]{:S(2)}, u32[]{:S(2)}) collective-permute-start(s32[4,4,128]{2,1,0:T(4,128)S(1)} %get-tuple-element.46), channel_id=1, source_target_pairs={{0,64},{16,80},{32,96},{48,112},{64,0},{80,16},{96,32},{112,48},{1... | collective-permute-start | bytes 24584 | tf_op jit(solution)/shard_map/ppermute | solution.py:360
  57.3 2.9 %collective-permute-start.8 = (s32[4,4,128]{2,1,0:T(4,128)S(1)}, s32[4,4,128]{2,1,0:T(4,128)S(1)}, u32[]{:S(2)}, u32[]{:S(2)}) collective-permute-start(s32[4,4,128]{2,1,0:T(4,128)S(1)} %get-tuple-element.46), channel_id=1, source_target_pairs={{0,96},{16,112},{32,0},{48,16},{64,32},{80,48},{96,64},{112,80},{1... | collective-permute-start | bytes 24584 | tf_op jit(solution)/shard_map/ppermute | solution.py:360
  60.2 2.3 %collective-permute-start.9 = (s32[4,4,4,128]{3,2,1,0:T(4,128)S(1)}, s32[4,4,4,128]{3,2,1,0:T(4,128)S(1)}, u32[]{:S(2)}, u32[]{:S(2)}) collective-permute-start(s32[4,4,4,128]{3,2,1,0:T(4,128)S(1)} %get-tuple-element.44), channel_id=1, source_target_pairs={{0,16},{16,0},{32,48},{48,32},{64,80},{80,64},{96,112},{112,96},{1... | collective-permute-start | bytes 98312 | tf_op jit(solution)/shard_map/ppermute | solution.py:358
  62.5 14.7 %collective-permute-start.11 = (bf16[32,64,128]{2,1,0:T(8,128)(2,1)}, bf16[32,64,128]{2,1,0:T(8,128)(2,1)}, u32[]{:S(2)}, u32[]{:S(2)}) collective-permute-start(bf16[32,64,128]{2,1,0:T(8,128)(2,1)} %get-tuple-element.18.refs_0_), channel_id=1, source_target_pairs={{0,32},{16,48},{32,64},{48,80},{64,96},{80,112},{96,0},{112,16},{1... | collective-permute-start | bytes 1572872 | tf_op jit(solution)/shard_map/ppermute | solution.py:360
  62.5 30.5 %collective-permute-start.17 = (bf16[32,64,128]{2,1,0:T(8,128)(2,1)}, bf16[32,64,128]{2,1,0:T(8,128)(2,1)}, u32[]{:S(2)}, u32[]{:S(2)}) collective-permute-start(bf16[32,64,128]{2,1,0:T(8,128)(2,1)} %get-tuple-element.18.refs_0_), channel_id=1, source_target_pairs={{0,96},{16,112},{32,0},{48,16},{64,32},{80,48},{96,64},{112,80},{1... | collective-permute-start | bytes 1572872 | tf_op jit(solution)/shard_map/ppermute | solution.py:360
  66.7 22.5 %collective-permute-start.13 = (bf16[32,64,128]{2,1,0:T(8,128)(2,1)}, bf16[32,64,128]{2,1,0:T(8,128)(2,1)}, u32[]{:S(2)}, u32[]{:S(2)}) collective-permute-start(bf16[32,64,128]{2,1,0:T(8,128)(2,1)} %collective-permute-done.10.refs_1_), channel_id=1, source_target_pairs={{0,96},{16,112},{32,0},{48,16},{64,32},{80,48},{96,64},{112,80},{1... | collective-permute-start | bytes 1572872 | tf_op jit(solution)/shard_map/ppermute | solution.py:360
  67.8 25.2 %collective-permute-start.16 = (bf16[32,64,128]{2,1,0:T(8,128)(2,1)}, bf16[32,64,128]{2,1,0:T(8,128)(2,1)}, u32[]{:S(2)}, u32[]{:S(2)}) collective-permute-start(bf16[32,64,128]{2,1,0:T(8,128)(2,1)} %collective-permute-done.10.refs_1_), channel_id=1, source_target_pairs={{0,32},{16,48},{32,64},{48,80},{64,96},{80,112},{96,0},{112,16},{1... | collective-permute-start | bytes 1572872 | tf_op jit(solution)/shard_map/ppermute | solution.py:360
  77.1 22.5 %collective-permute-start.12 = (bf16[32,64,128]{2,1,0:T(8,128)(2,1)}, bf16[32,64,128]{2,1,0:T(8,128)(2,1)}, u32[]{:S(2)}, u32[]{:S(2)}) collective-permute-start(bf16[32,64,128]{2,1,0:T(8,128)(2,1)} %collective-permute-done.11.refs_2_), channel_id=1, source_target_pairs={{0,32},{16,48},{32,64},{48,80},{64,96},{80,112},{96,0},{112,16},{1... | collective-permute-start | bytes 1572872 | tf_op jit(solution)/shard_map/ppermute | solution.py:360
  86.4 6.6 %collective-permute-start.15 = (bf16[64,64,128]{2,1,0:T(8,128)(2,1)S(1)}, bf16[64,64,128]{2,1,0:T(8,128)(2,1)S(1)}, u32[]{:S(2)}, u32[]{:S(2)}) collective-permute-start(bf16[64,64,128]{2,1,0:T(8,128)(2,1)S(1)} %get-tuple-element.20), channel_id=1, source_target_pairs={{0,16},{16,0},{32,48},{48,32},{64,80},{80,64},{96,112},{112,96},{1... | collective-permute-start | bytes 3145736 | tf_op jit(solution)/shard_map/ppermute | solution.py:358
  89.3 14.6 %collective-permute-start.14 = (bf16[32,64,128]{2,1,0:T(8,128)(2,1)}, bf16[32,64,128]{2,1,0:T(8,128)(2,1)S(1)}, u32[]{:S(2)}, u32[]{:S(2)}) collective-permute-start(bf16[32,64,128]{2,1,0:T(8,128)(2,1)} %collective-permute-done.13.refs_5_), channel_id=1, source_target_pairs={{0,96},{16,112},{32,0},{48,16},{64,32},{80,48},{96,64},{112,80},{1... | collective-permute-start | bytes 1572872 | tf_op jit(solution)/shard_map/ppermute | solution.py:360
  107.3 12.7 %copy-start = (s32[128,1]{0,1:T(1,128)S(1)}, s32[128,1]{0,1:T(1,128)}, u32[]{:S(2)}) copy-start(s32[128,1]{0,1:T(1,128)} %param.8) | copy-start | bytes 1540
  108.2 25.9 %all-to-all-start.2 = ((bf16[128,4,512]{2,1,0:T(4,128)(2,1)}), bf16[128,4,512]{2,1,0:T(4,128)(2,1)S(1)}, u32[]{:S(2)}, u32[]{:S(2)}) async-start(bf16[128,4,512]{2,1,0:T(4,128)(2,1)} %reshape.887), calls=%async_computation.2 | async-start | bytes 1048576 | tf_op jit(solution)/shard_map/all_to_all | solution.py:470

commit v4 on v3

--- a/solution.py
+++ b/solution.py
@@ -275,7 +275,7 @@
     pieces = refs[:4]
     table_ref, near_ref, out_ref, sources_ref, receivers_ref, cross_ref, rows_ref, product_ref, sems = refs[4:]
     copies = load_pieces((pieces[:2], pieces[2:]), (sources_ref, receivers_ref), sems)
-    slots = out_ref.shape[0]
+    slots = near_ref.shape[0]
     rows_ref[0:slots, :] = near_ref[...]
     for copy in copies:
         copy.wait()
@@ -295,21 +295,21 @@
         return lax.fori_loop(0, (jnp.minimum(count - first, CHUNK) + GROUP - 1) // GROUP, place, carry)
 
     lax.fori_loop(0, (count + CHUNK - 1) // CHUNK, chunk, 0)
-    out_ref[...] = rows_ref[0:slots, :].astype(jnp.bfloat16)
-
-
-def correlate(kernel, lists, pieces, receivers, blocks, dtype, extra):
+    out_ref[...] = rows_ref[0:slots, :].reshape(out_ref.shape).astype(jnp.bfloat16)
+
+
+def correlate(kernel, lists, pieces, receivers, blocks, shape, dtype, extra):
     slots = lists[1].shape[0]
     row = pieces[0].shape[1:]
     whole = lambda a: pl.BlockSpec(a.shape, lambda *_: (0,) * a.ndim)
     return pl.pallas_call(
         kernel,
-        out_shape=jax.ShapeDtypeStruct((slots, NLAG), dtype),
+        out_shape=jax.ShapeDtypeStruct(shape, dtype),
         grid_spec=pltpu.PrefetchScalarGridSpec(
             num_scalar_prefetch=4,
             grid=(1,),
             in_specs=[pl.BlockSpec(memory_space=pl.ANY)] * (len(pieces) + len(receivers)) + [whole(b) for b in blocks],
-            out_specs=pl.BlockSpec((slots, NLAG), lambda *_: (0, 0)),
+            out_specs=pl.BlockSpec(shape, lambda *_: (0,) * len(shape)),
             scratch_shapes=[
                 pltpu.VMEM((sum(p.shape[0] for p in pieces),) + row, jnp.bfloat16),
                 pltpu.VMEM((sum(p.shape[0] for p in receivers),) + row, jnp.bfloat16),
@@ -356,11 +356,7 @@
 def shift(value, axis, step):
     if axis == "core":
         return lax.ppermute(value, "gx", [(g, g ^ 1) for g in range(2 * SIDE)])
-    if axis == "y":
-        return lax.ppermute(value, "gx", [(g, (g + 2 * step) % (2 * SIDE)) for g in range(2 * SIDE)])
-    if axis == "z":
-        return lax.ppermute(value, "gy", [(g, (g + SIDE * step) % (SIDE * SIDE)) for g in range(SIDE * SIDE)])
-    return lax.ppermute(value, "gy", [(g, g // SIDE * SIDE + (g + step) % SIDE) for g in range(SIDE * SIDE)])
+    return lax.ppermute(value, "gx", [(g, (g + 2 * step) % (2 * SIDE)) for g in range(2 * SIDE)])
 
 
 def gather_ring(value, axis):
@@ -371,7 +367,7 @@
     groups = lax.axis_size("gy")
     devices = lax.axis_size("gx") * groups
     gx, gy = lax.axis_index("gx"), lax.axis_index("gy")
-    place = {"core": gx % 2, "y": gx // 2, "z": gy // SIDE, "x": gy % SIDE}
+    place = {"core": gx % 2, "y": gx // 2}
     core = place["core"]
     here = gx * groups + gy
     span = raw_window.shape[1]
@@ -380,19 +376,14 @@
     taper = jnp.sin(math.pi * (sample.astype(jnp.float32) + 0.5) / SEGLEN) ** 2
 
     pairs = pair_source.shape[0]
-    per = source_ids.shape[0]
     holder = pair_holder[:, 0]
     order = jnp.arange(pairs, dtype=jnp.int32)
     packed = (holder * channels + pair_receiver) * 256 + pair_source
     notes = jnp.concatenate([packed, source_ids])
-    notes = gather_ring(notes, "x")
-    notes = gather_ring(notes, "z")
-    ids, notes = notes[:, :, pairs:].reshape(groups, per), notes[:, :, :pairs]
-
-    step = jnp.arange(groups, dtype=jnp.int32)
-    mate = (place["z"] - step // SIDE) % SIDE * SIDE + (place["x"] - step % SIDE) % SIDE
-    wanted = jnp.sum(jnp.where(mate[None, :, None] == step[:, None, None], ids[None], 0), axis=1).reshape(-1)
-    wanted = wanted - gx * groups * channels
+    notes = jnp.broadcast_to(notes[None], (groups,) + notes.shape)
+    notes = lax.all_to_all(notes, "gy", split_axis=0, concat_axis=0, tiled=True)
+    wanted = (notes[:, pairs:] - gx * groups * channels).reshape(-1)
+    notes = notes[:, :pairs]
     first = pick_rows(wanted, raw_window, taper, groups)
     first = lax.all_to_all(first, "gy", split_axis=0, concat_axis=0, tiled=True)
     tapered = (raw_window * taper[None, :]).astype(jnp.bfloat16)
@@ -420,10 +411,8 @@
 
     dev = jnp.arange(devices, dtype=jnp.int32)
     own = (
-        (((dev // 64) ^ late) + (place["y"] - dev // 16 % SIDE) % SIDE * 2) * groups
-        + (place["z"] - dev // SIDE % SIDE) % SIDE * SIDE
-        + (place["x"] - dev % SIDE) % SIDE
-    )
+        (dev // (SIDE * groups) ^ late) + (place["y"] - dev // groups % SIDE) % SIDE * 2
+    ) * groups + dev % groups
     each = channels * 256
     key = notes // each
     entry = order[None, :] * each + notes % each + 1
@@ -463,11 +452,11 @@
 
     receivers = [mine, sister]
     near = correlate(
-        near_kernel, near_lists, [near0, near1, ahead0, ahead1, behind0, behind1], receivers, [table], jnp.float32, []
+        near_kernel, near_lists, [near0, near1, ahead0, ahead1, behind0, behind1], receivers, [table], (slots, NLAG), jnp.float32, []
     )
     extra = [pltpu.VMEM((slots + GROUP, NLAG), jnp.float32), pltpu.VMEM((CHUNK, NLAG), jnp.float32)]
-    partial = correlate(far_kernel, far_lists, [far0, far1], receivers, [table, near], jnp.bfloat16, extra)
-    returned = lax.all_to_all(partial.reshape(devices, 4, NLAG), ("gx", "gy"), split_axis=0, concat_axis=0, tiled=True)
+    partial = correlate(far_kernel, far_lists, [far0, far1], receivers, [table, near], (devices, 4, NLAG), jnp.bfloat16, extra)
+    returned = lax.all_to_all(partial, ("gx", "gy"), split_axis=0, concat_axis=0, tiled=True)
     returned = returned.reshape(devices * 4, NLAG)
     same = (holder[:, None] == holder[None, :]) & (order[None, :] < order[:, None])
     rank = jnp.sum(same.astype(jnp.int32), axis=1)

time: 136 us -> 137 us (level)
  waiting for transfers between devices: 41 us -> 46.8 us
  starting transfers between devices: 53.5 us -> 48.7 us
    ppermute x6 -> x0, starting transfers between devices: 11.4 us -> none  [the longest x3 5.74 us: shift(): lax.ppermute(value, 'gy', [(g, (g + SIDE * step) % (SIDE * SIDE)) for g i...]
    all_to_all x1 -> x2, starting transfers between devices: 11.8 us -> 20.2 us  [the longest x1 11.8 us: program(): lax.all_to_all(partial, ('gx', 'gy'), split_axis=0, concat_axis=0, tiled=...]
    all_to_all x1 -> x2, waiting for transfers between devices: 13.9 us -> 19.4 us  [the longest x1 13.9 us: program(): lax.all_to_all(partial, ('gx', 'gy'), split_axis=0, concat_axis=0, tiled=...]
    ppermute x6 -> x0, waiting for transfers between devices: 2.29 us -> none  [the longest x3 1.72 us: shift(): lax.ppermute(value, 'gy', [(g, (g + SIDE * step) % (SIDE * SIDE)) for g i...]
    ppermute x3, starting transfers between devices: 8.58 us -> 6.94 us  [shift(): return lax.ppermute(value, 'gx', [(g, g ^ 1) for g in range(2 * SIDE)])]
    all_to_all x1, starting transfers between devices: 5.12 us -> 3.66 us  [program(): first = lax.all_to_all(first, 'gy', split_axis=0, concat_axis=0, tiled=True)]
    all_to_all x1, waiting for transfers between devices: 8.26 us -> 9.69 us  [program(): first = lax.all_to_all(first, 'gy', split_axis=0, concat_axis=0, tiled=True)]
  transfers between devices with their start and end apart: 21 -> 16, of which waited for: 11 -> 9; matrix products, arithmetic and copies ran while one was open for 8% -> 8% of each run, Pallas kernels for 13% -> 13%
where the time goes in v4:
time: 137 us; the launch traced here: 136 us
  starting transfers between devices  48.7 us (36%)
  waiting for transfers between devices  46.8 us (34%)
  Pallas kernels  26.2 us (19%)
  other arithmetic  12.1 us (9%)
    ppermute x9, waiting for transfers between devices, shift(): lax.ppermute(value, 'gx', [(g, (g + 2 * step) % (2 * SIDE)) for g in rang...  16.8 us
    all_to_all x1, waiting for transfers between devices, program(): lax.all_to_all(partial, ('gx', 'gy'), split_axis=0, concat_axis=0, tiled=...  13.9 us
    ppermute x9, starting transfers between devices, shift(): lax.ppermute(value, 'gx', [(g, (g + 2 * step) % (2 * SIDE)) for g in rang...  13.1 us
    pallas_call x2, Pallas kernels, whiten(): pl.pallas_call(whiten_kernel, out_shape=(out, out), grid_spec=pltpu.Prefe...  12.4 us
    all_to_all x1, starting transfers between devices, program(): lax.all_to_all(partial, ('gx', 'gy'), split_axis=0, concat_axis=0, tiled=...  11.8 us
    pallas_call x2, Pallas kernels, correlate(): pl.pallas_call(kernel, out_shape=jax.ShapeDtypeStruct(shape, dtype), grid...  10.2 us
    all_to_all x1, waiting for transfers between devices, program(): first = lax.all_to_all(first, 'gy', split_axis=0, concat_axis=0, tiled=True)  9.69 us
    all_to_all x1, starting transfers between devices, program(): notes = lax.all_to_all(notes, 'gy', split_axis=0, concat_axis=0, tiled=True)  8.42 us
  transfers between devices with their start and end apart: 16, of which 9 were waited for; matrix products, arithmetic and copies ran while one was open for 8% of the time, Pallas kernels for 13%

profile of v4, /device:TPU:1, one launch (start us, length us, event | category | flops | bytes accessed | tf_op | source)
XLA Modules:
  0.0 136.4 jit_solution(361525836289720098)
XLA Ops:
  2.0 8.4 %all-to-all-start = ((s32[16,1,130]{2,1,0:T(1,128)}), s32[16,1,130]{2,1,0:T(1,128)S(1)}, u32[]{:S(2)}, u32[]{:S(2)}) async-start(s32[16,1,130]{2,1,0:T(1,128)} %broadcast_in_dim.54), calls=%async_computation | async-start | bytes 32768 | tf_op jit(solution)/shard_map/all_to_all | solution.py:384
  10.5 0.7 fusion.65.taper_ref
  11.4 5.5 %all-to-all-done = s32[16,1,130]{2,1,0:T(1,128)S(1)} async-done(((s32[16,1,130]{2,1,0:T(1,128)}), s32[16,1,130]{2,1,0:T(1,128)S(1)}, u32[]{:S(2)}, u32[]{:S(2)}) %all-to-all-start) | async-done | bytes 8352 | tf_op jit(solution)/shard_map/all_to_all | solution.py:384
  17.4 3.6 %pick.1 = bf16[16,32,1024]{2,1,0:T(8,128)(2,1)} custom-call(s32[32]{0:T(128)} %reshape.772.wanted_ref, f32[1024,1024]{1,0:T(8,128)} %raw_ref.1, f32[1,1024]{1,0:T(1,128)} %fusion.65.taper_ref), custom_call_target="tpu_custom_call" | custom-call | tf_op jit(solution)/shard_map/pick/pallas_call | solution.py:342
  21.1 3.7 %all-to-all-start.1 = ((bf16[16,32,1024]{2,1,0:T(8,128)(2,1)}), bf16[16,32,1024]{2,1,0:T(8,128)(2,1)S(1)}, u32[]{:S(2)}, u32[]{:S(2)}) async-start(bf16[16,32,1024]{2,1,0:T(8,128)(2,1)} %pick.1), calls=%async_computation.1 | async-start | bytes 2097152 | tf_op jit(solution)/shard_map/all_to_all | solution.py:388
  24.8 1.0 broadcast_multiply_fusion.1
  25.9 4.1 %multiply_convert_fusion = bf16[1024,1024]{1,0:T(8,128)(2,1)} fusion(f32[1024,1024]{1,0:T(8,128)} %raw_ref.1, f32[1024]{0:T(1024)S(1)} %fusion.60), kind=kLoop, calls=%fused_computation | loop fusion | flops 2097152 | bytes 6295552 | tf_op jit(solution)/shard_map/convert_element_type | solution.py:389
  30.1 9.7 %all-to-all-done.1.x_ref = bf16[16,32,1024]{2,1,0:T(8,128)(2,1)S(1)} async-done(((bf16[16,32,1024]{2,1,0:T(8,128)(2,1)}), bf16[16,32,1024]{2,1,0:T(8,128)(2,1)S(1)}, u32[]{:S(2)}, u32[]{:S(2)}) %all-to-all-start.1) | async-done | bytes 1048608 | tf_op jit(solution)/shard_map/all_to_all | solution.py:388
  39.8 4.8 %all-to-all-start.2 = ((bf16[16,64,1024]{2,1,0:T(8,128)(2,1)}), bf16[16,64,1024]{2,1,0:T(8,128)(2,1)}, u32[]{:S(2)}, u32[]{:S(2)}) async-start(bf16[16,64,1024]{2,1,0:T(8,128)(2,1)} %bitcast.56), calls=%async_computation.2 | async-start | bytes 4194304 | tf_op jit(solution)/shard_map/all_to_all | solution.py:390
  44.6 4.5 %whiten.2 = (bf16[32,64,128]{2,1,0:T(8,128)(2,1)}, bf16[32,64,128]{2,1,0:T(8,128)(2,1)S(1)}) custom-call(s32[1]{0:T(128)} %bitcast.8.core_ref, bf16[16,32,1024]{2,1,0:T(8,128)(2,1)S(1)} %all-to-all-done.1.x_ref, f32[2,16,256]{2,1,0:T(8,128)S(1)} %pad_maximum_fusion.1.tw_ref, bf16[512,512]{1,0:T(8,128)(2,1)S(1)} %fusion.11.upper_ref, ...), custom_call_target="tpu_custom_call" | custom-call | tf_op jit(solution)/shard_map/whiten/pallas_call | solution.py:194
  49.1 3.0 %collective-permute-start.4 = (bf16[32,64,128]{2,1,0:T(8,128)(2,1)S(1)}, bf16[32,64,128]{2,1,0:T(8,128)(2,1)}, u32[]{:S(2)}, u32[]{:S(2)}) collective-permute-start(bf16[32,64,128]{2,1,0:T(8,128)(2,1)S(1)} %get-tuple-element.15), channel_id=1, source_target_pairs={{0,16},{16,0},{32,48},{48,32},{64,80},{80,64},{96,112},{112,96},{1... | collective-permute-start | bytes 1572872 | tf_op jit(solution)/shard_map/ppermute | solution.py:358
  52.1 1.3 collective-permute-start
  53.4 2.6 %collective-permute-start.1 = (s32[16,128]{1,0:T(8,128)S(1)}, s32[16,128]{1,0:T(8,128)S(1)}, u32[]{:S(2)}, u32[]{:S(2)}) collective-permute-start(s32[16,128]{1,0:T(8,128)S(1)} %get-tuple-element.46), channel_id=1, source_target_pairs={{0,64},{16,80},{32,96},{48,112},{64,0},{80,16},{96,32},{112,48},{1... | collective-permute-start | bytes 24584 | tf_op jit(solution)/shard_map/ppermute | solution.py:359
  56.0 1.1 collective-permute-start.2
  57.1 0.7 collective-permute-done.1
  57.8 1.1 collective-permute-done.2
  58.9 1.3 collective-permute-start.3
  60.3 0.9 collective-permute-done.3
  61.1 2.3 %collective-permute-start.11 = (bf16[32,64,128]{2,1,0:T(8,128)(2,1)}, bf16[32,64,128]{2,1,0:T(8,128)(2,1)}, u32[]{:S(2)}, u32[]{:S(2)}) collective-permute-start(bf16[32,64,128]{2,1,0:T(8,128)(2,1)} %get-tuple-element.18.refs_0_), channel_id=1, source_target_pairs={{0,96},{16,112},{32,0},{48,16},{64,32},{80,48},{96,64},{112,80},{1... | collective-permute-start | bytes 1572872 | tf_op jit(solution)/shard_map/ppermute | solution.py:359
  63.8 1.1 fusion.18
  65.0 2.7 %collective-permute-start.7 = (bf16[32,64,128]{2,1,0:T(8,128)(2,1)}, bf16[32,64,128]{2,1,0:T(8,128)(2,1)}, u32[]{:S(2)}, u32[]{:S(2)}) collective-permute-start(bf16[32,64,128]{2,1,0:T(8,128)(2,1)} %collective-permute-done.4.refs_1_), channel_id=1, source_target_pairs={{0,96},{16,112},{32,0},{48,16},{64,32},{80,48},{96,64},{112,80},{1... | collective-permute-start | bytes 1572872 | tf_op jit(solution)/shard_map/ppermute | solution.py:359
  67.8 10.0 %collective-permute-done.5.refs_2_ = bf16[32,64,128]{2,1,0:T(8,128)(2,1)} collective-permute-done((bf16[32,64,128]{2,1,0:T(8,128)(2,1)}, bf16[32,64,128]{2,1,0:T(8,128)(2,1)}, u32[]{:S(2)}, u32[]{:S(2)}) %collective-permute-start.5) | collective-permute-done | bytes 524320 | tf_op jit(solution)/shard_map/ppermute | solution.py:359
  78.3 0.8 multiply_convert_fusion.2
  79.2 7.8 %whiten.3 = (bf16[64,64,128]{2,1,0:T(8,128)(2,1)S(1)}, bf16[64,64,128]{2,1,0:T(8,128)(2,1)S(1)}) custom-call(s32[1]{0:T(128)} %bitcast.8.core_ref, bf16[16,64,1024]{2,1,0:T(8,128)(2,1)} %all-to-all-done.2.x_ref, f32[2,16,256]{2,1,0:T(8,128)S(1)} %pad_maximum_fusion.1.tw_ref, bf16[512,512]{1,0:T(8,128)(2,1)S(1)} %fusion.11.upper_ref, ...), custom_call_target="tpu_custom_call" | custom-call | tf_op jit(solution)/shard_map/whiten/pallas_call | solution.py:194
  87.1 2.7 %collective-permute-start.9 = (bf16[64,64,128]{2,1,0:T(8,128)(2,1)S(1)}, bf16[64,64,128]{2,1,0:T(8,128)(2,1)S(1)}, u32[]{:S(2)}, u32[]{:S(2)}) collective-permute-start(bf16[64,64,128]{2,1,0:T(8,128)(2,1)S(1)} %get-tuple-element.20), channel_id=1, source_target_pairs={{0,16},{16,0},{32,48},{48,32},{64,80},{80,64},{96,112},{112,96},{1... | collective-permute-start | bytes 3145736 | tf_op jit(solution)/shard_map/ppermute | solution.py:358
  90.5 3.0 %collective-permute-start.8 = (bf16[32,64,128]{2,1,0:T(8,128)(2,1)}, bf16[32,64,128]{2,1,0:T(8,128)(2,1)S(1)}, u32[]{:S(2)}, u32[]{:S(2)}) collective-permute-start(bf16[32,64,128]{2,1,0:T(8,128)(2,1)} %collective-permute-done.7.refs_5_), channel_id=1, source_target_pairs={{0,96},{16,112},{32,0},{48,16},{64,32},{80,48},{96,64},{112,80},{1... | collective-permute-start | bytes 1572872 | tf_op jit(solution)/shard_map/ppermute | solution.py:359
  94.2 5.8 %shard_map.55.refs_5_ = f32[512,512]{1,0:T(8,128)S(1)} custom-call(s32[1]{0:T(128)} %bitcast.20.count_ref, s32[512]{0:T(512)S(1)} %get-tuple-element.52.src_ref, s32[512]{0:T(512)S(1)} %get-tuple-element.53.rcv_ref, s32[512]{0:T(512)S(1)} %get-tuple-element.51.slot_ref, bf16[32,64,128]{2,1,0:T(8,128)(2,1)} %get-tuple-element.18.refs_0_, ...), custom_call_target="tpu_custom_call" | custom-call | tf_op jit(solution)/shard_map/pallas_call | solution.py:305
  100.2 4.8 %collective-permute-done.8.refs_1_ = bf16[32,64,128]{2,1,0:T(8,128)(2,1)S(1)} collective-permute-done((bf16[32,64,128]{2,1,0:T(8,128)(2,1)}, bf16[32,64,128]{2,1,0:T(8,128)(2,1)S(1)}, u32[]{:S(2)}, u32[]{:S(2)}) %collective-permute-start.8) | collective-permute-done | bytes 524320 | tf_op jit(solution)/shard_map/ppermute | solution.py:359
  105.1 4.3 %shard_map.56 = bf16[128,4,512]{2,1,0:T(4,128)(2,1)} custom-call(s32[1]{0:T(128)} %bitcast.13.count_ref, s32[512]{0:T(512)S(1)} %get-tuple-element.55.src_ref, s32[512]{0:T(512)S(1)} %get-tuple-element.56.rcv_ref, s32[512]{0:T(512)S(1)} %get-tuple-element.54.slot_ref, bf16[32,64,128]{2,1,0:T(8,128)(2,1)} %collective-permute-done.6.refs_0_, ...), custom_call_target="tpu_custom_call" | custom-call | tf_op jit(solution)/shard_map/pallas_call | solution.py:305
  109.4 11.8 %all-to-all-start.3 = ((bf16[128,4,512]{2,1,0:T(4,128)(2,1)}), bf16[128,4,512]{2,1,0:T(4,128)(2,1)S(1)}, u32[]{:S(2)}, u32[]{:S(2)}) async-start(bf16[128,4,512]{2,1,0:T(4,128)(2,1)} %shard_map.56), calls=%async_computation.3 | async-start | bytes 1048576 | tf_op jit(solution)/shard_map/all_to_all | solution.py:459
  121.4 13.9 %all-to-all-done.3 = bf16[128,4,512]{2,1,0:T(4,128)(2,1)S(1)} async-done(((bf16[128,4,512]{2,1,0:T(4,128)(2,1)}), bf16[128,4,512]{2,1,0:T(4,128)(2,1)S(1)}, u32[]{:S(2)}, u32[]{:S(2)}) %all-to-all-start.3) | async-done | bytes 524320 | tf_op jit(solution)/shard_map/all_to_all | solution.py:459
  135.4 1.0 fusion.7
  (60 shorter events, 6.0 us)
Async XLA Ops:
  2.0 14.9 %all-to-all-start = ((s32[16,1,130]{2,1,0:T(1,128)}), s32[16,1,130]{2,1,0:T(1,128)S(1)}, u32[]{:S(2)}, u32[]{:S(2)}) async-start(s32[16,1,130]{2,1,0:T(1,128)} %broadcast_in_dim.54), calls=%async_computation | async-start | bytes 32768 | tf_op jit(solution)/shard_map/all_to_all | solution.py:384
  21.1 18.7 %all-to-all-start.1 = ((bf16[16,32,1024]{2,1,0:T(8,128)(2,1)}), bf16[16,32,1024]{2,1,0:T(8,128)(2,1)S(1)}, u32[]{:S(2)}, u32[]{:S(2)}) async-start(bf16[16,32,1024]{2,1,0:T(8,128)(2,1)} %pick.1), calls=%async_computation.1 | async-start | bytes 2097152 | tf_op jit(solution)/shard_map/all_to_all | solution.py:388
  39.8 39.5 %all-to-all-start.2 = ((bf16[16,64,1024]{2,1,0:T(8,128)(2,1)}), bf16[16,64,1024]{2,1,0:T(8,128)(2,1)}, u32[]{:S(2)}, u32[]{:S(2)}) async-start(bf16[16,64,1024]{2,1,0:T(8,128)(2,1)} %bitcast.56), calls=%async_computation.2 | async-start | bytes 4194304 | tf_op jit(solution)/shard_map/all_to_all | solution.py:390
  49.1 14.3 %collective-permute-start.4 = (bf16[32,64,128]{2,1,0:T(8,128)(2,1)S(1)}, bf16[32,64,128]{2,1,0:T(8,128)(2,1)}, u32[]{:S(2)}, u32[]{:S(2)}) collective-permute-start(bf16[32,64,128]{2,1,0:T(8,128)(2,1)S(1)} %get-tuple-element.15), channel_id=1, source_target_pairs={{0,16},{16,0},{32,48},{48,32},{64,80},{80,64},{96,112},{112,96},{1... | collective-permute-start | bytes 1572872 | tf_op jit(solution)/shard_map/ppermute | solution.py:358
  52.1 5.0 %collective-permute-start = (s32[16,128]{1,0:T(8,128)S(1)}, s32[16,128]{1,0:T(8,128)S(1)}, u32[]{:S(2)}, u32[]{:S(2)}) collective-permute-start(s32[16,128]{1,0:T(8,128)S(1)} %get-tuple-element.46), channel_id=1, source_target_pairs={{0,32},{16,48},{32,64},{48,80},{64,96},{80,112},{96,0},{112,16},{1... | collective-permute-start | bytes 24584 | tf_op jit(solution)/shard_map/ppermute | solution.py:359
  53.4 4.4 %collective-permute-start.1 = (s32[16,128]{1,0:T(8,128)S(1)}, s32[16,128]{1,0:T(8,128)S(1)}, u32[]{:S(2)}, u32[]{:S(2)}) collective-permute-start(s32[16,128]{1,0:T(8,128)S(1)} %get-tuple-element.46), channel_id=1, source_target_pairs={{0,64},{16,80},{32,96},{48,112},{64,0},{80,16},{96,32},{112,48},{1... | collective-permute-start | bytes 24584 | tf_op jit(solution)/shard_map/ppermute | solution.py:359
  56.0 2.9 %collective-permute-start.2 = (s32[16,128]{1,0:T(8,128)S(1)}, s32[16,128]{1,0:T(8,128)S(1)}, u32[]{:S(2)}, u32[]{:S(2)}) collective-permute-start(s32[16,128]{1,0:T(8,128)S(1)} %get-tuple-element.46), channel_id=1, source_target_pairs={{0,96},{16,112},{32,0},{48,16},{64,32},{80,48},{96,64},{112,80},{1... | collective-permute-start | bytes 24584 | tf_op jit(solution)/shard_map/ppermute | solution.py:359
  58.9 2.2 %collective-permute-start.3 = (s32[4,16,128]{2,1,0:T(8,128)S(1)}, s32[4,16,128]{2,1,0:T(8,128)S(1)}, u32[]{:S(2)}, u32[]{:S(2)}) collective-permute-start(s32[4,16,128]{2,1,0:T(8,128)S(1)} %get-tuple-element.44), channel_id=1, source_target_pairs={{0,16},{16,0},{32,48},{48,32},{64,80},{80,64},{96,112},{112,96},{1... | collective-permute-start | bytes 98312 | tf_op jit(solution)/shard_map/ppermute | solution.py:358
  61.1 33.1 %collective-permute-start.11 = (bf16[32,64,128]{2,1,0:T(8,128)(2,1)}, bf16[32,64,128]{2,1,0:T(8,128)(2,1)}, u32[]{:S(2)}, u32[]{:S(2)}) collective-permute-start(bf16[32,64,128]{2,1,0:T(8,128)(2,1)} %get-tuple-element.18.refs_0_), channel_id=1, source_target_pairs={{0,96},{16,112},{32,0},{48,16},{64,32},{80,48},{96,64},{112,80},{1... | collective-permute-start | bytes 1572872 | tf_op jit(solution)/shard_map/ppermute | solution.py:359
  63.4 14.4 %collective-permute-start.5 = (bf16[32,64,128]{2,1,0:T(8,128)(2,1)}, bf16[32,64,128]{2,1,0:T(8,128)(2,1)}, u32[]{:S(2)}, u32[]{:S(2)}) collective-permute-start(bf16[32,64,128]{2,1,0:T(8,128)(2,1)} %get-tuple-element.18.refs_0_), channel_id=1, source_target_pairs={{0,32},{16,48},{32,64},{48,80},{64,96},{80,112},{96,0},{112,16},{1... | collective-permute-start | bytes 1572872 | tf_op jit(solution)/shard_map/ppermute | solution.py:359
  65.0 29.3 %collective-permute-start.10 = (bf16[32,64,128]{2,1,0:T(8,128)(2,1)}, bf16[32,64,128]{2,1,0:T(8,128)(2,1)}, u32[]{:S(2)}, u32[]{:S(2)}) collective-permute-start(bf16[32,64,128]{2,1,0:T(8,128)(2,1)} %collective-permute-done.4.refs_1_), channel_id=1, source_target_pairs={{0,32},{16,48},{32,64},{48,80},{64,96},{80,112},{96,0},{112,16},{1... | collective-permute-start | bytes 1572872 | tf_op jit(solution)/shard_map/ppermute | solution.py:359
  65.0 25.4 %collective-permute-start.7 = (bf16[32,64,128]{2,1,0:T(8,128)(2,1)}, bf16[32,64,128]{2,1,0:T(8,128)(2,1)}, u32[]{:S(2)}, u32[]{:S(2)}) collective-permute-start(bf16[32,64,128]{2,1,0:T(8,128)(2,1)} %collective-permute-done.4.refs_1_), channel_id=1, source_target_pairs={{0,96},{16,112},{32,0},{48,16},{64,32},{80,48},{96,64},{112,80},{1... | collective-permute-start | bytes 1572872 | tf_op jit(solution)/shard_map/ppermute | solution.py:359
  77.8 22.5 %collective-permute-start.6 = (bf16[32,64,128]{2,1,0:T(8,128)(2,1)}, bf16[32,64,128]{2,1,0:T(8,128)(2,1)}, u32[]{:S(2)}, u32[]{:S(2)}) collective-permute-start(bf16[32,64,128]{2,1,0:T(8,128)(2,1)} %collective-permute-done.5.refs_2_), channel_id=1, source_target_pairs={{0,32},{16,48},{32,64},{48,80},{64,96},{80,112},{96,0},{112,16},{1... | collective-permute-start | bytes 1572872 | tf_op jit(solution)/shard_map/ppermute | solution.py:359
  87.1 7.2 %collective-permute-start.9 = (bf16[64,64,128]{2,1,0:T(8,128)(2,1)S(1)}, bf16[64,64,128]{2,1,0:T(8,128)(2,1)S(1)}, u32[]{:S(2)}, u32[]{:S(2)}) collective-permute-start(bf16[64,64,128]{2,1,0:T(8,128)(2,1)S(1)} %get-tuple-element.20), channel_id=1, source_target_pairs={{0,16},{16,0},{32,48},{48,32},{64,80},{80,64},{96,112},{112,96},{1... | collective-permute-start | bytes 3145736 | tf_op jit(solution)/shard_map/ppermute | solution.py:358
  90.5 14.6 %collective-permute-start.8 = (bf16[32,64,128]{2,1,0:T(8,128)(2,1)}, bf16[32,64,128]{2,1,0:T(8,128)(2,1)S(1)}, u32[]{:S(2)}, u32[]{:S(2)}) collective-permute-start(bf16[32,64,128]{2,1,0:T(8,128)(2,1)} %collective-permute-done.7.refs_5_), channel_id=1, source_target_pairs={{0,96},{16,112},{32,0},{48,16},{64,32},{80,48},{96,64},{112,80},{1... | collective-permute-start | bytes 1572872 | tf_op jit(solution)/shard_map/ppermute | solution.py:359
  105.1 16.1 %copy-start = (s32[128,1]{0,1:T(1,128)S(1)}, s32[128,1]{0,1:T(1,128)}, u32[]{:S(2)}) copy-start(s32[128,1]{0,1:T(1,128)} %param.8) | copy-start | bytes 1540
  109.4 25.9 %all-to-all-start.3 = ((bf16[128,4,512]{2,1,0:T(4,128)(2,1)}), bf16[128,4,512]{2,1,0:T(4,128)(2,1)S(1)}, u32[]{:S(2)}, u32[]{:S(2)}) async-start(bf16[128,4,512]{2,1,0:T(4,128)(2,1)} %shard_map.56), calls=%async_computation.3 | async-start | bytes 1048576 | tf_op jit(solution)/shard_map/all_to_all | solution.py:459

commit v5 on v4

--- a/solution.py
+++ b/solution.py
@@ -14,6 +14,8 @@
 BAND = 64
 NLAG = 512
 SIDE = 4
+SOURCES = 256
+PER_DEVICE = 64
 RADIX = 16
 INNER = SEGLEN // RADIX
 LANES = 128
@@ -262,25 +264,32 @@
 
 def near_kernel(count_ref, src_ref, rcv_ref, slot_ref, *refs):
     pieces = refs[:8]
-    table_ref, out_ref, sources_ref, receivers_ref, cross_ref, sems = refs[8:]
-    copies = load_pieces((pieces[:6], pieces[6:]), (sources_ref, receivers_ref), sems)
+    table_hbm, out_ref, sources_ref, receivers_ref, cross_ref, table_ref, sems = refs[8:]
+    *copies, table_copy = load_pieces(
+        (pieces[:6], pieces[6:], (table_hbm,)), (sources_ref, receivers_ref, table_ref), sems
+    )
     cross_ref[...] = jnp.zeros_like(cross_ref)
     for copy in copies:
         copy.wait()
     cross_slots(count_ref[0], src_ref, rcv_ref, lambda i: slot_ref[i], sources_ref, receivers_ref, cross_ref)
+    table_copy.wait()
     out_ref[...] = lags_of(cross_ref, 0, out_ref.shape[0], table_ref)
 
 
 def far_kernel(count_ref, src_ref, rcv_ref, slot_ref, *refs):
     pieces = refs[:4]
-    table_ref, near_ref, out_ref, sources_ref, receivers_ref, cross_ref, rows_ref, product_ref, sems = refs[4:]
-    copies = load_pieces((pieces[:2], pieces[2:]), (sources_ref, receivers_ref), sems)
-    slots = near_ref.shape[0]
-    rows_ref[0:slots, :] = near_ref[...]
+    table_hbm, near_hbm, out_ref, sources_ref, receivers_ref, cross_ref, table_ref, rows_ref, product_ref, sems = refs[4:]
+    slots = near_hbm.shape[0]
+    *copies, table_copy, near_copy = load_pieces(
+        (pieces[:2], pieces[2:], (table_hbm,), (near_hbm,)), (sources_ref, receivers_ref, table_ref, rows_ref), sems
+    )
     for copy in copies:
         copy.wait()
     count = count_ref[0]
     cross_slots(count, src_ref, rcv_ref, lambda i: i, sources_ref, receivers_ref, cross_ref)
+
+    table_copy.wait()
+    near_copy.wait()
 
     def chunk(c, carry):
         first = pl.multiple_of(c * CHUNK, CHUNK)
@@ -301,25 +310,56 @@
 def correlate(kernel, lists, pieces, receivers, blocks, shape, dtype, extra):
     slots = lists[1].shape[0]
     row = pieces[0].shape[1:]
-    whole = lambda a: pl.BlockSpec(a.shape, lambda *_: (0,) * a.ndim)
+    inputs = len(pieces) + len(receivers) + len(blocks)
     return pl.pallas_call(
         kernel,
         out_shape=jax.ShapeDtypeStruct(shape, dtype),
         grid_spec=pltpu.PrefetchScalarGridSpec(
             num_scalar_prefetch=4,
             grid=(1,),
-            in_specs=[pl.BlockSpec(memory_space=pl.ANY)] * (len(pieces) + len(receivers)) + [whole(b) for b in blocks],
+            in_specs=[pl.BlockSpec(memory_space=pl.ANY)] * inputs,
             out_specs=pl.BlockSpec(shape, lambda *_: (0,) * len(shape)),
             scratch_shapes=[
                 pltpu.VMEM((sum(p.shape[0] for p in pieces),) + row, jnp.bfloat16),
                 pltpu.VMEM((sum(p.shape[0] for p in receivers),) + row, jnp.bfloat16),
                 pltpu.VMEM(((slots + GROUP) * HALF_ROWS, LANES), jnp.float32),
+                pltpu.VMEM(blocks[0].shape, blocks[0].dtype),
                 *extra,
-                pltpu.SemaphoreType.DMA((len(pieces) + len(receivers),)),
+                pltpu.SemaphoreType.DMA((inputs,)),
             ],
         ),
         compiler_params=pltpu.CompilerParams(vmem_limit_bytes=40 << 20),
     )(*lists, *pieces, *receivers, *blocks)
+
+
+def pack_kernel(ids_ref, holder_ref, receiver_ref, source_ref, out_ref):
+    pairs = holder_ref.shape[1]
+    per = ids_ref.shape[0]
+    packed = (holder_ref[...] * PER_DEVICE + receiver_ref[...]) * SOURCES + source_ref[...]
+    lane = lax.broadcasted_iota(jnp.int32, (1, pairs), 1)
+    ids = jnp.zeros((1, pairs), jnp.int32)
+    for n in range(per):
+        ids = jnp.where(lane == n, ids_ref[n], ids)
+    row = jnp.concatenate([packed, ids], axis=1)
+    for g in range(out_ref.shape[0]):
+        out_ref[g] = row
+
+
+def pack_notes(source_ids, holder, receiver, source, copies):
+    pairs = holder.shape[0]
+    line = lambda a: a.reshape(1, pairs)
+    spec = pl.BlockSpec((1, pairs), lambda *_: (0, 0))
+    return pl.pallas_call(
+        pack_kernel,
+        out_shape=jax.ShapeDtypeStruct((copies, 1, 2 * pairs), jnp.int32),
+        grid_spec=pltpu.PrefetchScalarGridSpec(
+            num_scalar_prefetch=1,
+            grid=(1,),
+            in_specs=[spec, spec, spec],
+            out_specs=pl.BlockSpec((copies, 1, 2 * pairs), lambda *_: (0, 0, 0)),
+        ),
+        name="pack",
+    )(source_ids, line(holder), line(receiver), line(source))
 
 
 def pick_kernel(wanted_ref, raw_ref, taper_ref, out_ref, rows_ref, sems):
@@ -378,12 +418,11 @@
     pairs = pair_source.shape[0]
     holder = pair_holder[:, 0]
     order = jnp.arange(pairs, dtype=jnp.int32)
-    packed = (holder * channels + pair_receiver) * 256 + pair_source
-    notes = jnp.concatenate([packed, source_ids])
-    notes = jnp.broadcast_to(notes[None], (groups,) + notes.shape)
+    per = source_ids.shape[0]
+    notes = pack_notes(source_ids, holder, pair_receiver, pair_source, groups)
     notes = lax.all_to_all(notes, "gy", split_axis=0, concat_axis=0, tiled=True)
-    wanted = (notes[:, pairs:] - gx * groups * channels).reshape(-1)
-    notes = notes[:, :pairs]
+    wanted = (notes[:, 0, pairs:pairs + per] - gx * groups * channels).reshape(-1)
+    notes = notes[:, 0, :pairs]
     first = pick_rows(wanted, raw_window, taper, groups)
     first = lax.all_to_all(first, "gy", split_axis=0, concat_axis=0, tiled=True)
     tapered = (raw_window * taper[None, :]).astype(jnp.bfloat16)

time: 137 us -> 137 us (level)
  Pallas kernels: 26.2 us -> 28.3 us
    pallas_call x0 -> x1, Pallas kernels: none -> 1.97 us  [pack_notes(): pl.pallas_call(pack_kernel, out_shape=jax.ShapeDtypeStruct((copies, 1, 2...]
where the time goes in v5:
time: 137 us
  starting transfers between devices  48.8 us (36%)
  waiting for transfers between devices  46.7 us (34%)
  Pallas kernels  28.3 us (21%)
  other arithmetic  10.9 us (8%)
    ppermute x9, waiting for transfers between devices, shift(): lax.ppermute(value, 'gx', [(g, (g + 2 * step) % (2 * SIDE)) for g in rang...  16.7 us
    all_to_all x1, waiting for transfers between devices, program(): lax.all_to_all(partial, ('gx', 'gy'), split_axis=0, concat_axis=0, tiled=...  13.9 us
    ppermute x9, starting transfers between devices, shift(): lax.ppermute(value, 'gx', [(g, (g + 2 * step) % (2 * SIDE)) for g in rang...  13.2 us
    pallas_call x2, Pallas kernels, whiten(): pl.pallas_call(whiten_kernel, out_shape=(out, out), grid_spec=pltpu.Prefe...  12.4 us
    all_to_all x1, starting transfers between devices, program(): lax.all_to_all(partial, ('gx', 'gy'), split_axis=0, concat_axis=0, tiled=...  11.8 us
    pallas_call x2, Pallas kernels, correlate(): pl.pallas_call(kernel, out_shape=jax.ShapeDtypeStruct(shape, dtype), grid...  10.3 us
    all_to_all x1, waiting for transfers between devices, program(): first = lax.all_to_all(first, 'gy', split_axis=0, concat_axis=0, tiled=True)  9.67 us
    all_to_all x1, starting transfers between devices, program(): notes = lax.all_to_all(notes, 'gy', split_axis=0, concat_axis=0, tiled=True)  8.42 us
  transfers between devices with their start and end apart: 16, of which 9 were waited for; matrix products, arithmetic and copies ran while one was open for 8% of the time, Pallas kernels for 13%

profile of v5, /device:TPU:1, one launch (start us, length us, event | category | flops | bytes accessed | tf_op | source)
XLA Modules:
  0.0 136.6 jit_solution(589948669437377222)
XLA Ops:
  0.0 2.0 %pack.1 = s32[16,1,256]{2,1,0:T(1,128)} custom-call(s32[2]{0:T(128)} %ids_ref.1, s32[1,128]{1,0:T(1,128)} %bitcast.66, s32[1,128]{1,0:T(1,128)} %bitcast.69, s32[1,128]{1,0:T(1,128)} %bitcast.70), custom_call_target="tpu_custom_call" | custom-call | tf_op jit(solution)/shard_map/pack/pallas_call | solution.py:352
  2.0 8.4 %all-to-all-start = ((s32[16,1,256]{2,1,0:T(1,128)}), s32[16,1,256]{2,1,0:T(1,128)S(1)}, u32[]{:S(2)}, u32[]{:S(2)}) async-start(s32[16,1,256]{2,1,0:T(1,128)} %pack.1), calls=%async_computation | async-start | bytes 32768 | tf_op jit(solution)/shard_map/all_to_all | solution.py:423
  11.3 5.5 %all-to-all-done = s32[16,1,256]{2,1,0:T(1,128)S(1)} async-done(((s32[16,1,256]{2,1,0:T(1,128)}), s32[16,1,256]{2,1,0:T(1,128)S(1)}, u32[]{:S(2)}, u32[]{:S(2)}) %all-to-all-start) | async-done | bytes 16416 | tf_op jit(solution)/shard_map/all_to_all | solution.py:423
  17.5 3.6 %pick.1 = bf16[16,32,1024]{2,1,0:T(8,128)(2,1)} custom-call(s32[32]{0:T(128)} %sub.219.wanted_ref, f32[1024,1024]{1,0:T(8,128)} %raw_ref.1, f32[1,1024]{1,0:T(1,128)} %fusion.66.taper_ref), custom_call_target="tpu_custom_call" | custom-call | tf_op jit(solution)/shard_map/pick/pallas_call | solution.py:382
  21.1 3.7 %all-to-all-start.1 = ((bf16[16,32,1024]{2,1,0:T(8,128)(2,1)}), bf16[16,32,1024]{2,1,0:T(8,128)(2,1)S(1)}, u32[]{:S(2)}, u32[]{:S(2)}) async-start(bf16[16,32,1024]{2,1,0:T(8,128)(2,1)} %pick.1), calls=%async_computation.1 | async-start | bytes 2097152 | tf_op jit(solution)/shard_map/all_to_all | solution.py:427
  24.8 1.0 broadcast_multiply_fusion.1
  26.0 4.1 %multiply_convert_fusion = bf16[1024,1024]{1,0:T(8,128)(2,1)} fusion(f32[1024,1024]{1,0:T(8,128)} %raw_ref.1, f32[1024]{0:T(1024)S(1)} %fusion.61), kind=kLoop, calls=%fused_computation | loop fusion | flops 2097152 | bytes 6295552 | tf_op jit(solution)/shard_map/convert_element_type | solution.py:428
  30.1 9.7 %all-to-all-done.1.x_ref = bf16[16,32,1024]{2,1,0:T(8,128)(2,1)S(1)} async-done(((bf16[16,32,1024]{2,1,0:T(8,128)(2,1)}), bf16[16,32,1024]{2,1,0:T(8,128)(2,1)S(1)}, u32[]{:S(2)}, u32[]{:S(2)}) %all-to-all-start.1) | async-done | bytes 1048608 | tf_op jit(solution)/shard_map/all_to_all | solution.py:427
  39.8 4.8 %all-to-all-start.2 = ((bf16[16,64,1024]{2,1,0:T(8,128)(2,1)}), bf16[16,64,1024]{2,1,0:T(8,128)(2,1)}, u32[]{:S(2)}, u32[]{:S(2)}) async-start(bf16[16,64,1024]{2,1,0:T(8,128)(2,1)} %bitcast.55), calls=%async_computation.2 | async-start | bytes 4194304 | tf_op jit(solution)/shard_map/all_to_all | solution.py:429
  44.6 4.5 %whiten.2 = (bf16[32,64,128]{2,1,0:T(8,128)(2,1)}, bf16[32,64,128]{2,1,0:T(8,128)(2,1)S(1)}) custom-call(s32[1]{0:T(128)} %bitcast.12.core_ref, bf16[16,32,1024]{2,1,0:T(8,128)(2,1)S(1)} %all-to-all-done.1.x_ref, f32[2,16,256]{2,1,0:T(8,128)S(1)} %pad_maximum_fusion.1.tw_ref, bf16[512,512]{1,0:T(8,128)(2,1)S(1)} %fusion.11.upper_ref, ...), custom_call_target="tpu_custom_call" | custom-call | tf_op jit(solution)/shard_map/whiten/pallas_call | solution.py:196
  49.1 3.0 %collective-permute-start.4 = (bf16[32,64,128]{2,1,0:T(8,128)(2,1)S(1)}, bf16[32,64,128]{2,1,0:T(8,128)(2,1)}, u32[]{:S(2)}, u32[]{:S(2)}) collective-permute-start(bf16[32,64,128]{2,1,0:T(8,128)(2,1)S(1)} %get-tuple-element.15), channel_id=1, source_target_pairs={{0,16},{16,0},{32,48},{48,32},{64,80},{80,64},{96,112},{112,96},{1... | collective-permute-start | bytes 1572872 | tf_op jit(solution)/shard_map/ppermute | solution.py:398
  52.1 1.4 collective-permute-start
  53.5 2.6 %collective-permute-start.1 = (s32[16,128]{1,0:T(8,128)S(1)}, s32[16,128]{1,0:T(8,128)S(1)}, u32[]{:S(2)}, u32[]{:S(2)}) collective-permute-start(s32[16,128]{1,0:T(8,128)S(1)} %bitcast.59), channel_id=1, source_target_pairs={{0,64},{16,80},{32,96},{48,112},{64,0},{80,16},{96,32},{112,48},{1... | collective-permute-start | bytes 24584 | tf_op jit(solution)/shard_map/ppermute | solution.py:399
  56.1 1.1 collective-permute-start.2
  57.9 1.1 collective-permute-done.2
  59.0 1.3 collective-permute-start.3
  60.3 0.9 collective-permute-done.3
  61.2 2.3 %collective-permute-start.11 = (bf16[32,64,128]{2,1,0:T(8,128)(2,1)}, bf16[32,64,128]{2,1,0:T(8,128)(2,1)}, u32[]{:S(2)}, u32[]{:S(2)}) collective-permute-start(bf16[32,64,128]{2,1,0:T(8,128)(2,1)} %get-tuple-element.18.refs_0_), channel_id=1, source_target_pairs={{0,96},{16,112},{32,0},{48,16},{64,32},{80,48},{96,64},{112,80},{1... | collective-permute-start | bytes 1572872 | tf_op jit(solution)/shard_map/ppermute | solution.py:399
  63.9 1.1 fusion.18
  65.1 2.7 %collective-permute-start.7 = (bf16[32,64,128]{2,1,0:T(8,128)(2,1)}, bf16[32,64,128]{2,1,0:T(8,128)(2,1)}, u32[]{:S(2)}, u32[]{:S(2)}) collective-permute-start(bf16[32,64,128]{2,1,0:T(8,128)(2,1)} %collective-permute-done.4.refs_1_), channel_id=1, source_target_pairs={{0,96},{16,112},{32,0},{48,16},{64,32},{80,48},{96,64},{112,80},{1... | collective-permute-start | bytes 1572872 | tf_op jit(solution)/shard_map/ppermute | solution.py:399
  67.9 10.0 %collective-permute-done.5.refs_2_ = bf16[32,64,128]{2,1,0:T(8,128)(2,1)} collective-permute-done((bf16[32,64,128]{2,1,0:T(8,128)(2,1)}, bf16[32,64,128]{2,1,0:T(8,128)(2,1)}, u32[]{:S(2)}, u32[]{:S(2)}) %collective-permute-start.5) | collective-permute-done | bytes 524320 | tf_op jit(solution)/shard_map/ppermute | solution.py:399
  78.3 0.8 multiply_convert_fusion.2
  79.3 7.8 %whiten.3 = (bf16[64,64,128]{2,1,0:T(8,128)(2,1)S(1)}, bf16[64,64,128]{2,1,0:T(8,128)(2,1)S(1)}) custom-call(s32[1]{0:T(128)} %bitcast.12.core_ref, bf16[16,64,1024]{2,1,0:T(8,128)(2,1)} %all-to-all-done.2.x_ref, f32[2,16,256]{2,1,0:T(8,128)S(1)} %pad_maximum_fusion.1.tw_ref, bf16[512,512]{1,0:T(8,128)(2,1)S(1)} %fusion.11.upper_ref, ...), custom_call_target="tpu_custom_call" | custom-call | tf_op jit(solution)/shard_map/whiten/pallas_call | solution.py:196
  87.2 2.7 %collective-permute-start.9 = (bf16[64,64,128]{2,1,0:T(8,128)(2,1)S(1)}, bf16[64,64,128]{2,1,0:T(8,128)(2,1)S(1)}, u32[]{:S(2)}, u32[]{:S(2)}) collective-permute-start(bf16[64,64,128]{2,1,0:T(8,128)(2,1)S(1)} %get-tuple-element.20), channel_id=1, source_target_pairs={{0,16},{16,0},{32,48},{48,32},{64,80},{80,64},{96,112},{112,96},{1... | collective-permute-start | bytes 3145736 | tf_op jit(solution)/shard_map/ppermute | solution.py:398
  90.6 3.0 %collective-permute-start.8 = (bf16[32,64,128]{2,1,0:T(8,128)(2,1)}, bf16[32,64,128]{2,1,0:T(8,128)(2,1)S(1)}, u32[]{:S(2)}, u32[]{:S(2)}) collective-permute-start(bf16[32,64,128]{2,1,0:T(8,128)(2,1)} %collective-permute-done.7.refs_5_), channel_id=1, source_target_pairs={{0,96},{16,112},{32,0},{48,16},{64,32},{80,48},{96,64},{112,80},{1... | collective-permute-start | bytes 1572872 | tf_op jit(solution)/shard_map/ppermute | solution.py:399
  93.6 0.8 convert_reduce_fusion.3
  94.4 5.8 %shard_map.55.refs_5_ = f32[512,512]{1,0:T(8,128)S(1)} custom-call(s32[1]{0:T(128)} %bitcast.24.count_ref, s32[512]{0:T(512)S(1)} %get-tuple-element.50.src_ref, s32[512]{0:T(512)S(1)} %get-tuple-element.51.rcv_ref, s32[512]{0:T(512)S(1)} %get-tuple-element.49.slot_ref, bf16[32,64,128]{2,1,0:T(8,128)(2,1)} %get-tuple-element.18.refs_0_, ...), custom_call_target="tpu_custom_call" | custom-call | tf_op jit(solution)/shard_map/pallas_call | solution.py:314
  100.3 4.8 %collective-permute-done.8.refs_1_ = bf16[32,64,128]{2,1,0:T(8,128)(2,1)S(1)} collective-permute-done((bf16[32,64,128]{2,1,0:T(8,128)(2,1)}, bf16[32,64,128]{2,1,0:T(8,128)(2,1)S(1)}, u32[]{:S(2)}, u32[]{:S(2)}) %collective-permute-start.8) | collective-permute-done | bytes 524320 | tf_op jit(solution)/shard_map/ppermute | solution.py:399
  105.2 4.5 %shard_map.56 = bf16[128,4,512]{2,1,0:T(4,128)(2,1)} custom-call(s32[1]{0:T(128)} %bitcast.17.count_ref, s32[512]{0:T(512)S(1)} %get-tuple-element.53.src_ref, s32[512]{0:T(512)S(1)} %get-tuple-element.54.rcv_ref, s32[512]{0:T(512)S(1)} %get-tuple-element.52.slot_ref, bf16[32,64,128]{2,1,0:T(8,128)(2,1)} %collective-permute-done.6.refs_0_, ...), custom_call_target="tpu_custom_call" | custom-call | tf_op jit(solution)/shard_map/pallas_call | solution.py:314
  109.7 11.8 %all-to-all-start.3 = ((bf16[128,4,512]{2,1,0:T(4,128)(2,1)}), bf16[128,4,512]{2,1,0:T(4,128)(2,1)S(1)}, u32[]{:S(2)}, u32[]{:S(2)}) async-start(bf16[128,4,512]{2,1,0:T(4,128)(2,1)} %shard_map.56), calls=%async_computation.3 | async-start | bytes 1048576 | tf_op jit(solution)/shard_map/all_to_all | solution.py:498
  121.6 13.9 %all-to-all-done.3 = bf16[128,4,512]{2,1,0:T(4,128)(2,1)S(1)} async-done(((bf16[128,4,512]{2,1,0:T(4,128)(2,1)}), bf16[128,4,512]{2,1,0:T(4,128)(2,1)S(1)}, u32[]{:S(2)}, u32[]{:S(2)}) %all-to-all-start.3) | async-done | bytes 524320 | tf_op jit(solution)/shard_map/all_to_all | solution.py:498
  135.7 1.0 fusion.7
  (57 shorter events, 4.7 us)
Async XLA Ops:
  2.0 14.9 %all-to-all-start = ((s32[16,1,256]{2,1,0:T(1,128)}), s32[16,1,256]{2,1,0:T(1,128)S(1)}, u32[]{:S(2)}, u32[]{:S(2)}) async-start(s32[16,1,256]{2,1,0:T(1,128)} %pack.1), calls=%async_computation | async-start | bytes 32768 | tf_op jit(solution)/shard_map/all_to_all | solution.py:423
  21.1 18.7 %all-to-all-start.1 = ((bf16[16,32,1024]{2,1,0:T(8,128)(2,1)}), bf16[16,32,1024]{2,1,0:T(8,128)(2,1)S(1)}, u32[]{:S(2)}, u32[]{:S(2)}) async-start(bf16[16,32,1024]{2,1,0:T(8,128)(2,1)} %pick.1), calls=%async_computation.1 | async-start | bytes 2097152 | tf_op jit(solution)/shard_map/all_to_all | solution.py:427
  39.8 39.6 %all-to-all-start.2 = ((bf16[16,64,1024]{2,1,0:T(8,128)(2,1)}), bf16[16,64,1024]{2,1,0:T(8,128)(2,1)}, u32[]{:S(2)}, u32[]{:S(2)}) async-start(bf16[16,64,1024]{2,1,0:T(8,128)(2,1)} %bitcast.55), calls=%async_computation.2 | async-start | bytes 4194304 | tf_op jit(solution)/shard_map/all_to_all | solution.py:429
  49.1 14.3 %collective-permute-start.4 = (bf16[32,64,128]{2,1,0:T(8,128)(2,1)S(1)}, bf16[32,64,128]{2,1,0:T(8,128)(2,1)}, u32[]{:S(2)}, u32[]{:S(2)}) collective-permute-start(bf16[32,64,128]{2,1,0:T(8,128)(2,1)S(1)} %get-tuple-element.15), channel_id=1, source_target_pairs={{0,16},{16,0},{32,48},{48,32},{64,80},{80,64},{96,112},{112,96},{1... | collective-permute-start | bytes 1572872 | tf_op jit(solution)/shard_map/ppermute | solution.py:398
  52.1 5.1 %collective-permute-start = (s32[16,128]{1,0:T(8,128)S(1)}, s32[16,128]{1,0:T(8,128)S(1)}, u32[]{:S(2)}, u32[]{:S(2)}) collective-permute-start(s32[16,128]{1,0:T(8,128)S(1)} %bitcast.58), channel_id=1, source_target_pairs={{0,32},{16,48},{32,64},{48,80},{64,96},{80,112},{96,0},{112,16},{1... | collective-permute-start | bytes 24584 | tf_op jit(solution)/shard_map/ppermute | solution.py:399
  53.5 4.4 %collective-permute-start.1 = (s32[16,128]{1,0:T(8,128)S(1)}, s32[16,128]{1,0:T(8,128)S(1)}, u32[]{:S(2)}, u32[]{:S(2)}) collective-permute-start(s32[16,128]{1,0:T(8,128)S(1)} %bitcast.59), channel_id=1, source_target_pairs={{0,64},{16,80},{32,96},{48,112},{64,0},{80,16},{96,32},{112,48},{1... | collective-permute-start | bytes 24584 | tf_op jit(solution)/shard_map/ppermute | solution.py:399
  56.1 2.9 %collective-permute-start.2 = (s32[16,128]{1,0:T(8,128)S(1)}, s32[16,128]{1,0:T(8,128)S(1)}, u32[]{:S(2)}, u32[]{:S(2)}) collective-permute-start(s32[16,128]{1,0:T(8,128)S(1)} %bitcast.60), channel_id=1, source_target_pairs={{0,96},{16,112},{32,0},{48,16},{64,32},{80,48},{96,64},{112,80},{1... | collective-permute-start | bytes 24584 | tf_op jit(solution)/shard_map/ppermute | solution.py:399
  59.0 2.2 %collective-permute-start.3 = (s32[4,16,128]{2,1,0:T(8,128)S(1)}, s32[4,16,128]{2,1,0:T(8,128)S(1)}, u32[]{:S(2)}, u32[]{:S(2)}) collective-permute-start(s32[4,16,128]{2,1,0:T(8,128)S(1)} %get-tuple-element.44), channel_id=1, source_target_pairs={{0,16},{16,0},{32,48},{48,32},{64,80},{80,64},{96,112},{112,96},{1... | collective-permute-start | bytes 98312 | tf_op jit(solution)/shard_map/ppermute | solution.py:398
  61.2 33.2 %collective-permute-start.11 = (bf16[32,64,128]{2,1,0:T(8,128)(2,1)}, bf16[32,64,128]{2,1,0:T(8,128)(2,1)}, u32[]{:S(2)}, u32[]{:S(2)}) collective-permute-start(bf16[32,64,128]{2,1,0:T(8,128)(2,1)} %get-tuple-element.18.refs_0_), channel_id=1, source_target_pairs={{0,96},{16,112},{32,0},{48,16},{64,32},{80,48},{96,64},{112,80},{1... | collective-permute-start | bytes 1572872 | tf_op jit(solution)/shard_map/ppermute | solution.py:399
  63.5 14.4 %collective-permute-start.5 = (bf16[32,64,128]{2,1,0:T(8,128)(2,1)}, bf16[32,64,128]{2,1,0:T(8,128)(2,1)}, u32[]{:S(2)}, u32[]{:S(2)}) collective-permute-start(bf16[32,64,128]{2,1,0:T(8,128)(2,1)} %get-tuple-element.18.refs_0_), channel_id=1, source_target_pairs={{0,32},{16,48},{32,64},{48,80},{64,96},{80,112},{96,0},{112,16},{1... | collective-permute-start | bytes 1572872 | tf_op jit(solution)/shard_map/ppermute | solution.py:399
  65.0 29.3 %collective-permute-start.10 = (bf16[32,64,128]{2,1,0:T(8,128)(2,1)}, bf16[32,64,128]{2,1,0:T(8,128)(2,1)}, u32[]{:S(2)}, u32[]{:S(2)}) collective-permute-start(bf16[32,64,128]{2,1,0:T(8,128)(2,1)} %collective-permute-done.4.refs_1_), channel_id=1, source_target_pairs={{0,32},{16,48},{32,64},{48,80},{64,96},{80,112},{96,0},{112,16},{1... | collective-permute-start | bytes 1572872 | tf_op jit(solution)/shard_map/ppermute | solution.py:399
  65.1 25.4 %collective-permute-start.7 = (bf16[32,64,128]{2,1,0:T(8,128)(2,1)}, bf16[32,64,128]{2,1,0:T(8,128)(2,1)}, u32[]{:S(2)}, u32[]{:S(2)}) collective-permute-start(bf16[32,64,128]{2,1,0:T(8,128)(2,1)} %collective-permute-done.4.refs_1_), channel_id=1, source_target_pairs={{0,96},{16,112},{32,0},{48,16},{64,32},{80,48},{96,64},{112,80},{1... | collective-permute-start | bytes 1572872 | tf_op jit(solution)/shard_map/ppermute | solution.py:399
  77.9 22.5 %collective-permute-start.6 = (bf16[32,64,128]{2,1,0:T(8,128)(2,1)}, bf16[32,64,128]{2,1,0:T(8,128)(2,1)}, u32[]{:S(2)}, u32[]{:S(2)}) collective-permute-start(bf16[32,64,128]{2,1,0:T(8,128)(2,1)} %collective-permute-done.5.refs_2_), channel_id=1, source_target_pairs={{0,32},{16,48},{32,64},{48,80},{64,96},{80,112},{96,0},{112,16},{1... | collective-permute-start | bytes 1572872 | tf_op jit(solution)/shard_map/ppermute | solution.py:399
  87.2 7.2 %collective-permute-start.9 = (bf16[64,64,128]{2,1,0:T(8,128)(2,1)S(1)}, bf16[64,64,128]{2,1,0:T(8,128)(2,1)S(1)}, u32[]{:S(2)}, u32[]{:S(2)}) collective-permute-start(bf16[64,64,128]{2,1,0:T(8,128)(2,1)S(1)} %get-tuple-element.20), channel_id=1, source_target_pairs={{0,16},{16,0},{32,48},{48,32},{64,80},{80,64},{96,112},{112,96},{1... | collective-permute-start | bytes 3145736 | tf_op jit(solution)/shard_map/ppermute | solution.py:398
  90.6 14.6 %collective-permute-start.8 = (bf16[32,64,128]{2,1,0:T(8,128)(2,1)}, bf16[32,64,128]{2,1,0:T(8,128)(2,1)S(1)}, u32[]{:S(2)}, u32[]{:S(2)}) collective-permute-start(bf16[32,64,128]{2,1,0:T(8,128)(2,1)} %collective-permute-done.7.refs_5_), channel_id=1, source_target_pairs={{0,96},{16,112},{32,0},{48,16},{64,32},{80,48},{96,64},{112,80},{1... | collective-permute-start | bytes 1572872 | tf_op jit(solution)/shard_map/ppermute | solution.py:399
  105.2 16.3 %copy-start = (s32[128,1]{0,1:T(1,128)S(1)}, s32[128,1]{0,1:T(1,128)}, u32[]{:S(2)}) copy-start(s32[128,1]{0,1:T(1,128)} %param.8) | copy-start | bytes 1540
  109.7 25.9 %all-to-all-start.3 = ((bf16[128,4,512]{2,1,0:T(4,128)(2,1)}), bf16[128,4,512]{2,1,0:T(4,128)(2,1)S(1)}, u32[]{:S(2)}, u32[]{:S(2)}) async-start(bf16[128,4,512]{2,1,0:T(4,128)(2,1)} %shard_map.56), calls=%async_computation.3 | async-start | bytes 1048576 | tf_op jit(solution)/shard_map/all_to_all | solution.py:498

commit v6 on v5

--- a/solution.py
+++ b/solution.py
@@ -208,7 +208,7 @@
             out_specs=(spec, spec),
             scratch_shapes=[pltpu.VMEM((count * rows, 2 * INNER), jnp.bfloat16)] * (2 * per),
         ),
-        compiler_params=pltpu.CompilerParams(vmem_limit_bytes=48 << 20),
+        compiler_params=pltpu.CompilerParams(vmem_limit_bytes=24 << 20),
         name="whiten",
     )(core, samples, twiddle, upper, lower)
 
@@ -231,12 +231,15 @@
     return copies
 
 
-def cross_slots(count, src_ref, rcv_ref, row_of, sources_ref, receivers_ref, cross_ref):
+def cross_slots(start, stop, src_ref, rcv_ref, row_of, sources_ref, receivers_ref, cross_ref):
+    last = src_ref.shape[0] - 1
+
     def group(g, carry):
         for u in range(GROUP):
-            i = g * GROUP + u
-            a = sources_ref[src_ref[i]].astype(jnp.float32)
-            b = receivers_ref[rcv_ref[i]].astype(jnp.float32)
+            i = start + g * GROUP + u
+            entry = jnp.minimum(i, last)
+            a = sources_ref[src_ref[entry]].astype(jnp.float32)
+            b = receivers_ref[rcv_ref[entry]].astype(jnp.float32)
             re = im = None
             for s in range(NSEG):
                 ar, ai = a[s * 16:s * 16 + 8], a[s * 16 + 8:s * 16 + 16]
@@ -245,13 +248,12 @@
                 m = ai * br - ar * bi
                 re = r if re is None else re + r
                 im = m if im is None else im + m
-            row = row_of(i)
-            at = pl.multiple_of(row * HALF_ROWS, HALF_ROWS)
+            at = pl.multiple_of(row_of(i, entry) * HALF_ROWS, HALF_ROWS)
             cross_ref[pl.ds(at, 8), :] = re
             cross_ref[pl.ds(at + 8, 8), :] = im
         return carry
 
-    lax.fori_loop(0, (count + GROUP - 1) // GROUP, group, 0)
+    lax.fori_loop(0, (stop - start + GROUP - 1) // GROUP, group, 0)
 
 
 def lags_of(cross_ref, first, count, table_ref):
@@ -263,33 +265,30 @@
 
 
 def near_kernel(count_ref, src_ref, rcv_ref, slot_ref, *refs):
-    pieces = refs[:8]
-    table_hbm, out_ref, sources_ref, receivers_ref, cross_ref, table_ref, sems = refs[8:]
-    *copies, table_copy = load_pieces(
-        (pieces[:6], pieces[6:], (table_hbm,)), (sources_ref, receivers_ref, table_ref), sems
-    )
+    pieces = refs[:6]
+    mine_ref, sister_ref, table_ref, out_ref, sources_ref, cross_ref, sems = refs[6:]
+    copies = load_pieces((pieces,), (sources_ref,), sems)
     cross_ref[...] = jnp.zeros_like(cross_ref)
     for copy in copies:
         copy.wait()
-    cross_slots(count_ref[0], src_ref, rcv_ref, lambda i: slot_ref[i], sources_ref, receivers_ref, cross_ref)
-    table_copy.wait()
+    slot_of = lambda i, entry: slot_ref[entry]
+    cross_slots(0, count_ref[0], src_ref, rcv_ref, slot_of, sources_ref, mine_ref, cross_ref)
+    cross_slots(count_ref[0], count_ref[1], src_ref, rcv_ref, slot_of, sources_ref, sister_ref, cross_ref)
     out_ref[...] = lags_of(cross_ref, 0, out_ref.shape[0], table_ref)
 
 
 def far_kernel(count_ref, src_ref, rcv_ref, slot_ref, *refs):
-    pieces = refs[:4]
-    table_hbm, near_hbm, out_ref, sources_ref, receivers_ref, cross_ref, table_ref, rows_ref, product_ref, sems = refs[4:]
-    slots = near_hbm.shape[0]
-    *copies, table_copy, near_copy = load_pieces(
-        (pieces[:2], pieces[2:], (table_hbm,), (near_hbm,)), (sources_ref, receivers_ref, table_ref, rows_ref), sems
-    )
+    pieces = refs[:2]
+    mine_ref, sister_ref, table_ref, near_ref, out_ref, sources_ref, cross_ref, rows_ref, product_ref, sems = refs[2:]
+    slots = near_ref.shape[0]
+    copies = load_pieces((pieces,), (sources_ref,), sems)
+    rows_ref[0:slots, :] = near_ref[...]
     for copy in copies:
         copy.wait()
-    count = count_ref[0]
-    cross_slots(count, src_ref, rcv_ref, lambda i: i, sources_ref, receivers_ref, cross_ref)
-
-    table_copy.wait()
-    near_copy.wait()
+    count = count_ref[1]
+    row_of = lambda i, entry: i
+    cross_slots(0, count_ref[0], src_ref, rcv_ref, row_of, sources_ref, mine_ref, cross_ref)
+    cross_slots(count_ref[0], count, src_ref, rcv_ref, row_of, sources_ref, sister_ref, cross_ref)
 
     def chunk(c, carry):
         first = pl.multiple_of(c * CHUNK, CHUNK)
@@ -310,26 +309,24 @@
 def correlate(kernel, lists, pieces, receivers, blocks, shape, dtype, extra):
     slots = lists[1].shape[0]
     row = pieces[0].shape[1:]
-    inputs = len(pieces) + len(receivers) + len(blocks)
+    direct = (*receivers, *blocks)
     return pl.pallas_call(
         kernel,
         out_shape=jax.ShapeDtypeStruct(shape, dtype),
         grid_spec=pltpu.PrefetchScalarGridSpec(
             num_scalar_prefetch=4,
             grid=(1,),
-            in_specs=[pl.BlockSpec(memory_space=pl.ANY)] * inputs,
+            in_specs=[pl.BlockSpec(memory_space=pl.ANY)] * len(pieces) + [pl.BlockSpec(memory_space=pltpu.VMEM)] * len(direct),
             out_specs=pl.BlockSpec(shape, lambda *_: (0,) * len(shape)),
             scratch_shapes=[
                 pltpu.VMEM((sum(p.shape[0] for p in pieces),) + row, jnp.bfloat16),
-                pltpu.VMEM((sum(p.shape[0] for p in receivers),) + row, jnp.bfloat16),
                 pltpu.VMEM(((slots + GROUP) * HALF_ROWS, LANES), jnp.float32),
-                pltpu.VMEM(blocks[0].shape, blocks[0].dtype),
                 *extra,
-                pltpu.SemaphoreType.DMA((inputs,)),
+                pltpu.SemaphoreType.DMA((len(pieces),)),
             ],
         ),
-        compiler_params=pltpu.CompilerParams(vmem_limit_bytes=40 << 20),
-    )(*lists, *pieces, *receivers, *blocks)
+        compiler_params=pltpu.CompilerParams(vmem_limit_bytes=24 << 20),
+    )(*lists, *pieces, *direct)
 
 
 def pack_kernel(ids_ref, holder_ref, receiver_ref, source_ref, out_ref):
@@ -475,7 +472,7 @@
     source_at = (piece * 2 + (source_gx % 2 ^ core)) * (2 * groups) + source_no % (2 * groups)
     kind = jnp.arange(4, dtype=jnp.int32)[:, None]
     slot_no = dev[None, :] * 4 + kind
-    receiver_at = asked // 256 + kind // 2 * channels
+    receiver_at = asked // 256
     entry = ((slot_no - slots) * 256 + receiver_at) * 256 + source_at
     index = jnp.arange(slots, dtype=jnp.int32)
 
@@ -484,7 +481,9 @@
         spot = jnp.sum((chosen[None, :] & (index[None, :] < index[:, None])).astype(jnp.int32), axis=1)
         hit = chosen[None, :] & (spot[None, :] == index[:, None])
         line = jnp.sum(jnp.where(hit, entry.reshape(1, -1), 0), axis=1) + slots * 65536
-        return jnp.sum(chosen.astype(jnp.int32)).reshape(1), line % 256, line // 256 % 256, line // 65536
+        ends = (jnp.arange(2, dtype=jnp.int32) + 1) * (slots // 2)
+        counts = jnp.sum((chosen[None, :] & (index[None, :] < ends[:, None])).astype(jnp.int32), axis=1)
+        return counts, line % 256, line // 256 % 256, line // 65536
 
     near_lists = compact(valid & ~far)
     far_lists = compact(valid & far)

time: 137 us -> 134 us (0.978)
  Pallas kernels: 28.3 us -> 25.6 us
  starting transfers between devices: 48.8 us -> 46.4 us
    all_to_all x1, starting transfers between devices: 11.8 us -> 5.22 us  [program(): lax.all_to_all(partial, ('gx', 'gy'), split_axis=0, concat_axis=0, tiled=...]
    ppermute x3, starting transfers between devices: 6.94 us -> 9.76 us  [shift(): return lax.ppermute(value, 'gx', [(g, g ^ 1) for g in range(2 * SIDE)])]
    pallas_call x2, Pallas kernels: 10.3 us -> 7.52 us  [correlate(): pl.pallas_call(kernel, out_shape=jax.ShapeDtypeStruct(shape, dtype), grid...]
  transfers between devices with their start and end apart: 16 -> 16, of which waited for: 9 -> 8; matrix products, arithmetic and copies ran while one was open for 8% -> 9% of each run, Pallas kernels for 13% -> 13%
where the time goes in v6:
time: 134 us; the launch traced here: 133 us
  waiting for transfers between devices  47.9 us (36%)
  starting transfers between devices  46.4 us (35%)
  Pallas kernels  25.6 us (19%)
  other arithmetic  11.5 us (9%)
    ppermute x9, waiting for transfers between devices, shift(): lax.ppermute(value, 'gx', [(g, (g + 2 * step) % (2 * SIDE)) for g in rang...  17.9 us
    ppermute x9, starting transfers between devices, shift(): lax.ppermute(value, 'gx', [(g, (g + 2 * step) % (2 * SIDE)) for g in rang...  14.5 us
    all_to_all x1, waiting for transfers between devices, program(): lax.all_to_all(partial, ('gx', 'gy'), split_axis=0, concat_axis=0, tiled=...  13.9 us
    pallas_call x2, Pallas kernels, whiten(): pl.pallas_call(whiten_kernel, out_shape=(out, out), grid_spec=pltpu.Prefe...  12.5 us
    ppermute x3, starting transfers between devices, shift(): return lax.ppermute(value, 'gx', [(g, g ^ 1) for g in range(2 * SIDE)])  9.76 us
    all_to_all x1, waiting for transfers between devices, program(): first = lax.all_to_all(first, 'gy', split_axis=0, concat_axis=0, tiled=True)  9.72 us
    all_to_all x1, starting transfers between devices, program(): notes = lax.all_to_all(notes, 'gy', split_axis=0, concat_axis=0, tiled=True)  8.42 us
    pallas_call x2, Pallas kernels, correlate(): pl.pallas_call(kernel, out_shape=jax.ShapeDtypeStruct(shape, dtype), grid...  7.52 us
  transfers between devices with their start and end apart: 16, of which 8 were waited for; matrix products, arithmetic and copies ran while one was open for 9% of the time, Pallas kernels for 13%

profile of v6, /device:TPU:1, one launch (start us, length us, event | category | flops | bytes accessed | tf_op | source)
XLA Modules:
  0.0 133.4 jit_solution(849927082306558296)
XLA Ops:
  0.0 2.0 %pack.1 = s32[16,1,256]{2,1,0:T(1,128)} custom-call(s32[2]{0:T(128)} %ids_ref.1, s32[1,128]{1,0:T(1,128)} %bitcast.61, s32[1,128]{1,0:T(1,128)} %bitcast.64, s32[1,128]{1,0:T(1,128)} %bitcast.65), custom_call_target="tpu_custom_call" | custom-call | tf_op jit(solution)/shard_map/pack/pallas_call | solution.py:349
  2.0 8.4 %all-to-all-start = ((s32[16,1,256]{2,1,0:T(1,128)}), s32[16,1,256]{2,1,0:T(1,128)S(1)}, u32[]{:S(2)}, u32[]{:S(2)}) async-start(s32[16,1,256]{2,1,0:T(1,128)} %pack.1), calls=%async_computation | async-start | bytes 32768 | tf_op jit(solution)/shard_map/all_to_all | solution.py:420
  11.3 5.5 %all-to-all-done = s32[16,1,256]{2,1,0:T(1,128)S(1)} async-done(((s32[16,1,256]{2,1,0:T(1,128)}), s32[16,1,256]{2,1,0:T(1,128)S(1)}, u32[]{:S(2)}, u32[]{:S(2)}) %all-to-all-start) | async-done | bytes 16416 | tf_op jit(solution)/shard_map/all_to_all | solution.py:420
  17.5 3.6 %pick.1 = bf16[16,32,1024]{2,1,0:T(8,128)(2,1)} custom-call(s32[32]{0:T(128)} %sub.203.wanted_ref, f32[1024,1024]{1,0:T(8,128)} %raw_ref.1, f32[1,1024]{1,0:T(1,128)} %fusion.68.taper_ref), custom_call_target="tpu_custom_call" | custom-call | tf_op jit(solution)/shard_map/pick/pallas_call | solution.py:379
  21.1 3.7 %all-to-all-start.1 = ((bf16[16,32,1024]{2,1,0:T(8,128)(2,1)}), bf16[16,32,1024]{2,1,0:T(8,128)(2,1)S(1)}, u32[]{:S(2)}, u32[]{:S(2)}) async-start(bf16[16,32,1024]{2,1,0:T(8,128)(2,1)} %pick.1), calls=%async_computation.1 | async-start | bytes 2097152 | tf_op jit(solution)/shard_map/all_to_all | solution.py:424
  24.8 1.0 broadcast_multiply_fusion.1
  25.9 4.1 %multiply_convert_fusion = bf16[1024,1024]{1,0:T(8,128)(2,1)} fusion(f32[1024,1024]{1,0:T(8,128)} %raw_ref.1, f32[1024]{0:T(1024)S(1)} %fusion.61), kind=kLoop, calls=%fused_computation | loop fusion | flops 2097152 | bytes 6295552 | tf_op jit(solution)/shard_map/convert_element_type | solution.py:425
  30.0 9.7 %all-to-all-done.1.x_ref = bf16[16,32,1024]{2,1,0:T(8,128)(2,1)S(1)} async-done(((bf16[16,32,1024]{2,1,0:T(8,128)(2,1)}), bf16[16,32,1024]{2,1,0:T(8,128)(2,1)S(1)}, u32[]{:S(2)}, u32[]{:S(2)}) %all-to-all-start.1) | async-done | bytes 1048608 | tf_op jit(solution)/shard_map/all_to_all | solution.py:424
  39.7 4.8 %all-to-all-start.2 = ((bf16[16,64,1024]{2,1,0:T(8,128)(2,1)}), bf16[16,64,1024]{2,1,0:T(8,128)(2,1)}, u32[]{:S(2)}, u32[]{:S(2)}) async-start(bf16[16,64,1024]{2,1,0:T(8,128)(2,1)} %bitcast.50), calls=%async_computation.2 | async-start | bytes 4194304 | tf_op jit(solution)/shard_map/all_to_all | solution.py:426
  44.6 4.5 %whiten.2 = (bf16[32,64,128]{2,1,0:T(8,128)(2,1)S(1)}, bf16[32,64,128]{2,1,0:T(8,128)(2,1)}) custom-call(s32[1]{0:T(128)} %bitcast.12.core_ref, bf16[16,32,1024]{2,1,0:T(8,128)(2,1)S(1)} %all-to-all-done.1.x_ref, f32[2,16,256]{2,1,0:T(8,128)S(1)} %pad_maximum_fusion.1.tw_ref, bf16[512,512]{1,0:T(8,128)(2,1)S(1)} %fusion.11.upper_ref, ...), custom_call_target="tpu_custom_call" | custom-call | tf_op jit(solution)/shard_map/whiten/pallas_call | solution.py:196
  49.1 3.0 %collective-permute-start.4 = (bf16[32,64,128]{2,1,0:T(8,128)(2,1)}, bf16[32,64,128]{2,1,0:T(8,128)(2,1)S(1)}, u32[]{:S(2)}, u32[]{:S(2)}) collective-permute-start(bf16[32,64,128]{2,1,0:T(8,128)(2,1)} %get-tuple-element.15), channel_id=1, source_target_pairs={{0,16},{16,0},{32,48},{48,32},{64,80},{80,64},{96,112},{112,96},{1... | collective-permute-start | bytes 1572872 | tf_op jit(solution)/shard_map/ppermute | solution.py:395
  52.1 1.4 %collective-permute-start = (s32[16,128]{1,0:T(8,128)S(1)}, s32[16,128]{1,0:T(8,128)S(1)}, u32[]{:S(2)}, u32[]{:S(2)}) collective-permute-start(s32[16,128]{1,0:T(8,128)S(1)} %bitcast.53), channel_id=1, source_target_pairs={{0,32},{16,48},{32,64},{48,80},{64,96},{80,112},{96,0},{112,16},{1... | collective-permute-start | bytes 24584 | tf_op jit(solution)/shard_map/ppermute | solution.py:396
  53.5 2.6 %collective-permute-start.1 = (s32[16,128]{1,0:T(8,128)S(1)}, s32[16,128]{1,0:T(8,128)S(1)}, u32[]{:S(2)}, u32[]{:S(2)}) collective-permute-start(s32[16,128]{1,0:T(8,128)S(1)} %bitcast.54), channel_id=1, source_target_pairs={{0,64},{16,80},{32,96},{48,112},{64,0},{80,16},{96,32},{112,48},{1... | collective-permute-start | bytes 24584 | tf_op jit(solution)/shard_map/ppermute | solution.py:396
  56.1 1.1 collective-permute-start.2
  57.9 1.1 collective-permute-done.2
  59.0 1.3 collective-permute-start.3
  61.2 2.3 %collective-permute-start.11 = (bf16[32,64,128]{2,1,0:T(8,128)(2,1)S(1)}, bf16[32,64,128]{2,1,0:T(8,128)(2,1)S(1)}, u32[]{:S(2)}, u32[]{:S(2)}) collective-permute-start(bf16[32,64,128]{2,1,0:T(8,128)(2,1)S(1)} %get-tuple-element.18.refs_0_), channel_id=1, source_target_pairs={{0,96},{16,112},{32,0},{48,16},{64,32},{80,48},{96,64},{112,80},{1... | collective-permute-start | bytes 1572872 | tf_op jit(solution)/shard_map/ppermute | solution.py:396
  64.3 1.1 fusion.18
  65.4 2.9 %collective-permute-start.7 = (bf16[32,64,128]{2,1,0:T(8,128)(2,1)S(1)}, bf16[32,64,128]{2,1,0:T(8,128)(2,1)}, u32[]{:S(2)}, u32[]{:S(2)}) collective-permute-start(bf16[32,64,128]{2,1,0:T(8,128)(2,1)S(1)} %collective-permute-done.4.refs_1_), channel_id=1, source_target_pairs={{0,96},{16,112},{32,0},{48,16},{64,32},{80,48},{96,64},{112,80},{1... | collective-permute-start | bytes 1572872 | tf_op jit(solution)/shard_map/ppermute | solution.py:396
  68.3 2.1 %multiply_convert_fusion.2 = (bf16[1,8,128,512]{3,2,1,0:T(8,128)(2,1)}, bf16[1,8,128,512]{3,2,1,0:T(8,128)(2,1)}) fusion(f32[128,512]{1,0:T(8,128)S(1)} %get-tuple-element.24, f32[8,512]{1,0:T(8,128)S(1)} %get-tuple-element.23, f32[128,512]{1,0:T(8,128)S(1)} %get-tuple-element.22, f32[8,512]{1,0:T(8,128)S(1)} %get-tuple-element.21, ...), kind=kLoop, calls=%fused_computation.3 | loop fusion | flops 5242880 | bytes 2662400 | tf_op jit(solution)/shard_map/convert
  70.4 8.0 %whiten.3 = (bf16[64,64,128]{2,1,0:T(8,128)(2,1)S(1)}, bf16[64,64,128]{2,1,0:T(8,128)(2,1)S(1)}) custom-call(s32[1]{0:T(128)} %bitcast.12.core_ref, bf16[16,64,1024]{2,1,0:T(8,128)(2,1)} %all-to-all-done.2.x_ref, f32[2,16,256]{2,1,0:T(8,128)S(1)} %pad_maximum_fusion.1.tw_ref, bf16[512,512]{1,0:T(8,128)(2,1)S(1)} %fusion.11.upper_ref, ...), custom_call_target="tpu_custom_call" | custom-call | tf_op jit(solution)/shard_map/whiten/pallas_call | solution.py:196
  78.4 5.5 %collective-permute-start.9 = (bf16[64,64,128]{2,1,0:T(8,128)(2,1)S(1)}, bf16[64,64,128]{2,1,0:T(8,128)(2,1)S(1)}, u32[]{:S(2)}, u32[]{:S(2)}) collective-permute-start(bf16[64,64,128]{2,1,0:T(8,128)(2,1)S(1)} %get-tuple-element.20), channel_id=1, source_target_pairs={{0,16},{16,0},{32,48},{48,32},{64,80},{80,64},{96,112},{112,96},{1... | collective-permute-start | bytes 3145736 | tf_op jit(solution)/shard_map/ppermute | solution.py:395
  84.0 1.4 %collective-permute-start.10 = (bf16[32,64,128]{2,1,0:T(8,128)(2,1)S(1)}, bf16[32,64,128]{2,1,0:T(8,128)(2,1)S(1)}, u32[]{:S(2)}, u32[]{:S(2)}) collective-permute-start(bf16[32,64,128]{2,1,0:T(8,128)(2,1)S(1)} %collective-permute-done.4.refs_1_), channel_id=1, source_target_pairs={{0,32},{16,48},{32,64},{48,80},{64,96},{80,112},{96,0},{112,16},{1... | collective-permute-start | bytes 1572872 | tf_op jit(solution)/shard_map/ppermute | solution.py:396
  85.3 1.3 collective-permute-start.6
  87.5 1.6 %collective-permute-start.8 = (bf16[32,64,128]{2,1,0:T(8,128)(2,1)}, bf16[32,64,128]{2,1,0:T(8,128)(2,1)S(1)}, u32[]{:S(2)}, u32[]{:S(2)}) collective-permute-start(bf16[32,64,128]{2,1,0:T(8,128)(2,1)} %collective-permute-done.7.refs_5_), channel_id=1, source_target_pairs={{0,96},{16,112},{32,0},{48,16},{64,32},{80,48},{96,64},{112,80},{1... | collective-permute-start | bytes 1572872 | tf_op jit(solution)/shard_map/ppermute | solution.py:396
  89.4 9.5 %collective-permute-done.10.refs_3_ = bf16[32,64,128]{2,1,0:T(8,128)(2,1)S(1)} collective-permute-done((bf16[32,64,128]{2,1,0:T(8,128)(2,1)S(1)}, bf16[32,64,128]{2,1,0:T(8,128)(2,1)S(1)}, u32[]{:S(2)}, u32[]{:S(2)}) %collective-permute-start.10) | collective-permute-done | bytes 524320 | tf_op jit(solution)/shard_map/ppermute | solution.py:396
  98.9 4.6 %shard_map.55.refs_5_ = f32[512,512]{1,0:T(8,128)S(1)} custom-call(s32[2]{0:T(128)S(1)} %get-tuple-element.33.count_ref, s32[512]{0:T(512)S(1)} %get-tuple-element.50.src_ref, s32[512]{0:T(512)S(1)} %get-tuple-element.51.rcv_ref, s32[512]{0:T(512)S(1)} %get-tuple-element.49.slot_ref, bf16[32,64,128]{2,1,0:T(8,128)(2,1)S(1)} %get-tuple-element.18.refs_0_, ...), custom_call_target="tpu_custom_call" | custom-call | tf_op jit(solution)/shard_map/pallas_call | solution.py:313
  103.5 6.6 %collective-permute-done.6.refs_0_ = bf16[32,64,128]{2,1,0:T(8,128)(2,1)S(1)} collective-permute-done((bf16[32,64,128]{2,1,0:T(8,128)(2,1)S(1)}, bf16[32,64,128]{2,1,0:T(8,128)(2,1)S(1)}, u32[]{:S(2)}, u32[]{:S(2)}) %collective-permute-start.6) | collective-permute-done | bytes 524320 | tf_op jit(solution)/shard_map/ppermute | solution.py:396
  110.1 2.9 %shard_map.56 = bf16[128,4,512]{2,1,0:T(4,128)(2,1)} custom-call(s32[2]{0:T(128)S(1)} %get-tuple-element.34.count_ref, s32[512]{0:T(512)S(1)} %get-tuple-element.53.src_ref, s32[512]{0:T(512)S(1)} %get-tuple-element.54.rcv_ref, s32[512]{0:T(512)S(1)} %get-tuple-element.52.slot_ref, bf16[32,64,128]{2,1,0:T(8,128)(2,1)S(1)} %collective-permute-done.6.refs_0_, ...), custom_call_target="tpu_custom_call" | custom-call | tf_op jit(solution)/shard_map/pallas_call | solution.py:313
  113.0 5.2 %all-to-all-start.3 = ((bf16[128,4,512]{2,1,0:T(4,128)(2,1)}), bf16[128,4,512]{2,1,0:T(4,128)(2,1)S(1)}, u32[]{:S(2)}, u32[]{:S(2)}) async-start(bf16[128,4,512]{2,1,0:T(4,128)(2,1)} %shard_map.56), calls=%async_computation.3 | async-start | bytes 1048576 | tf_op jit(solution)/shard_map/all_to_all | solution.py:497
  118.4 13.9 %all-to-all-done.3 = bf16[128,4,512]{2,1,0:T(4,128)(2,1)S(1)} async-done(((bf16[128,4,512]{2,1,0:T(4,128)(2,1)}), bf16[128,4,512]{2,1,0:T(4,128)(2,1)S(1)}, u32[]{:S(2)}, u32[]{:S(2)}) %all-to-all-start.3) | async-done | bytes 524320 | tf_op jit(solution)/shard_map/all_to_all | solution.py:497
  132.5 1.0 fusion.7
  (61 shorter events, 5.5 us)
Async XLA Ops:
  2.0 14.9 %all-to-all-start = ((s32[16,1,256]{2,1,0:T(1,128)}), s32[16,1,256]{2,1,0:T(1,128)S(1)}, u32[]{:S(2)}, u32[]{:S(2)}) async-start(s32[16,1,256]{2,1,0:T(1,128)} %pack.1), calls=%async_computation | async-start | bytes 32768 | tf_op jit(solution)/shard_map/all_to_all | solution.py:420
  21.1 18.7 %all-to-all-start.1 = ((bf16[16,32,1024]{2,1,0:T(8,128)(2,1)}), bf16[16,32,1024]{2,1,0:T(8,128)(2,1)S(1)}, u32[]{:S(2)}, u32[]{:S(2)}) async-start(bf16[16,32,1024]{2,1,0:T(8,128)(2,1)} %pick.1), calls=%async_computation.1 | async-start | bytes 2097152 | tf_op jit(solution)/shard_map/all_to_all | solution.py:424
  39.7 30.6 %all-to-all-start.2 = ((bf16[16,64,1024]{2,1,0:T(8,128)(2,1)}), bf16[16,64,1024]{2,1,0:T(8,128)(2,1)}, u32[]{:S(2)}, u32[]{:S(2)}) async-start(bf16[16,64,1024]{2,1,0:T(8,128)(2,1)} %bitcast.50), calls=%async_computation.2 | async-start | bytes 4194304 | tf_op jit(solution)/shard_map/all_to_all | solution.py:426
  49.1 14.3 %collective-permute-start.4 = (bf16[32,64,128]{2,1,0:T(8,128)(2,1)}, bf16[32,64,128]{2,1,0:T(8,128)(2,1)S(1)}, u32[]{:S(2)}, u32[]{:S(2)}) collective-permute-start(bf16[32,64,128]{2,1,0:T(8,128)(2,1)} %get-tuple-element.15), channel_id=1, source_target_pairs={{0,16},{16,0},{32,48},{48,32},{64,80},{80,64},{96,112},{112,96},{1... | collective-permute-start | bytes 1572872 | tf_op jit(solution)/shard_map/ppermute | solution.py:395
  52.1 5.1 %collective-permute-start = (s32[16,128]{1,0:T(8,128)S(1)}, s32[16,128]{1,0:T(8,128)S(1)}, u32[]{:S(2)}, u32[]{:S(2)}) collective-permute-start(s32[16,128]{1,0:T(8,128)S(1)} %bitcast.53), channel_id=1, source_target_pairs={{0,32},{16,48},{32,64},{48,80},{64,96},{80,112},{96,0},{112,16},{1... | collective-permute-start | bytes 24584 | tf_op jit(solution)/shard_map/ppermute | solution.py:396
  53.5 4.4 %collective-permute-start.1 = (s32[16,128]{1,0:T(8,128)S(1)}, s32[16,128]{1,0:T(8,128)S(1)}, u32[]{:S(2)}, u32[]{:S(2)}) collective-permute-start(s32[16,128]{1,0:T(8,128)S(1)} %bitcast.54), channel_id=1, source_target_pairs={{0,64},{16,80},{32,96},{48,112},{64,0},{80,16},{96,32},{112,48},{1... | collective-permute-start | bytes 24584 | tf_op jit(solution)/shard_map/ppermute | solution.py:396
  56.1 2.9 %collective-permute-start.2 = (s32[16,128]{1,0:T(8,128)S(1)}, s32[16,128]{1,0:T(8,128)S(1)}, u32[]{:S(2)}, u32[]{:S(2)}) collective-permute-start(s32[16,128]{1,0:T(8,128)S(1)} %bitcast.55), channel_id=1, source_target_pairs={{0,96},{16,112},{32,0},{48,16},{64,32},{80,48},{96,64},{112,80},{1... | collective-permute-start | bytes 24584 | tf_op jit(solution)/shard_map/ppermute | solution.py:396
  59.0 2.2 %collective-permute-start.3 = (s32[4,16,128]{2,1,0:T(8,128)S(1)}, s32[4,16,128]{2,1,0:T(8,128)S(1)}, u32[]{:S(2)}, u32[]{:S(2)}) collective-permute-start(s32[4,16,128]{2,1,0:T(8,128)S(1)} %get-tuple-element.44), channel_id=1, source_target_pairs={{0,16},{16,0},{32,48},{48,32},{64,80},{80,64},{96,112},{112,96},{1... | collective-permute-start | bytes 98312 | tf_op jit(solution)/shard_map/ppermute | solution.py:395
  61.2 28.2 %collective-permute-start.11 = (bf16[32,64,128]{2,1,0:T(8,128)(2,1)S(1)}, bf16[32,64,128]{2,1,0:T(8,128)(2,1)S(1)}, u32[]{:S(2)}, u32[]{:S(2)}) collective-permute-start(bf16[32,64,128]{2,1,0:T(8,128)(2,1)S(1)} %get-tuple-element.18.refs_0_), channel_id=1, source_target_pairs={{0,96},{16,112},{32,0},{48,16},{64,32},{80,48},{96,64},{112,80},{1... | collective-permute-start | bytes 1572872 | tf_op jit(solution)/shard_map/ppermute | solution.py:396
  63.4 21.9 %collective-permute-start.5 = (bf16[32,64,128]{2,1,0:T(8,128)(2,1)S(1)}, bf16[32,64,128]{2,1,0:T(8,128)(2,1)S(1)}, u32[]{:S(2)}, u32[]{:S(2)}) collective-permute-start(bf16[32,64,128]{2,1,0:T(8,128)(2,1)S(1)} %get-tuple-element.18.refs_0_), channel_id=1, source_target_pairs={{0,32},{16,48},{32,64},{48,80},{64,96},{80,112},{96,0},{112,16},{1... | collective-permute-start | bytes 1572872 | tf_op jit(solution)/shard_map/ppermute | solution.py:396
  65.4 22.2 %collective-permute-start.7 = (bf16[32,64,128]{2,1,0:T(8,128)(2,1)S(1)}, bf16[32,64,128]{2,1,0:T(8,128)(2,1)}, u32[]{:S(2)}, u32[]{:S(2)}) collective-permute-start(bf16[32,64,128]{2,1,0:T(8,128)(2,1)S(1)} %collective-permute-done.4.refs_1_), channel_id=1, source_target_pairs={{0,96},{16,112},{32,0},{48,16},{64,32},{80,48},{96,64},{112,80},{1... | collective-permute-start | bytes 1572872 | tf_op jit(solution)/shard_map/ppermute | solution.py:396
  70.4 16.4 %copy-start = (bf16[1,8,128,512]{3,2,1,0:T(8,128)(2,1)S(1)}, bf16[1,8,128,512]{3,2,1,0:T(8,128)(2,1)}, u32[]{:S(2)}) copy-start(bf16[1,8,128,512]{3,2,1,0:T(8,128)(2,1)} %get-tuple-element.39) | copy-start | bytes 3145732
  70.4 16.5 %copy-start.1 = (bf16[1,8,128,512]{3,2,1,0:T(8,128)(2,1)S(1)}, bf16[1,8,128,512]{3,2,1,0:T(8,128)(2,1)}, u32[]{:S(2)}) copy-start(bf16[1,8,128,512]{3,2,1,0:T(8,128)(2,1)} %get-tuple-element.40) | copy-start | bytes 3145732
  78.4 20.5 %collective-permute-start.9 = (bf16[64,64,128]{2,1,0:T(8,128)(2,1)S(1)}, bf16[64,64,128]{2,1,0:T(8,128)(2,1)S(1)}, u32[]{:S(2)}, u32[]{:S(2)}) collective-permute-start(bf16[64,64,128]{2,1,0:T(8,128)(2,1)S(1)} %get-tuple-element.20), channel_id=1, source_target_pairs={{0,16},{16,0},{32,48},{48,32},{64,80},{80,64},{96,112},{112,96},{1... | collective-permute-start | bytes 3145736 | tf_op jit(solution)/shard_map/ppermute | solution.py:395
  84.0 14.9 %collective-permute-start.10 = (bf16[32,64,128]{2,1,0:T(8,128)(2,1)S(1)}, bf16[32,64,128]{2,1,0:T(8,128)(2,1)S(1)}, u32[]{:S(2)}, u32[]{:S(2)}) collective-permute-start(bf16[32,64,128]{2,1,0:T(8,128)(2,1)S(1)} %collective-permute-done.4.refs_1_), channel_id=1, source_target_pairs={{0,32},{16,48},{32,64},{48,80},{64,96},{80,112},{96,0},{112,16},{1... | collective-permute-start | bytes 1572872 | tf_op jit(solution)/shard_map/ppermute | solution.py:396
  85.3 24.7 %collective-permute-start.6 = (bf16[32,64,128]{2,1,0:T(8,128)(2,1)S(1)}, bf16[32,64,128]{2,1,0:T(8,128)(2,1)S(1)}, u32[]{:S(2)}, u32[]{:S(2)}) collective-permute-start(bf16[32,64,128]{2,1,0:T(8,128)(2,1)S(1)} %collective-permute-done.5.refs_2_), channel_id=1, source_target_pairs={{0,32},{16,48},{32,64},{48,80},{64,96},{80,112},{96,0},{112,16},{1... | collective-permute-start | bytes 1572872 | tf_op jit(solution)/shard_map/ppermute | solution.py:396
  87.5 22.5 %collective-permute-start.8 = (bf16[32,64,128]{2,1,0:T(8,128)(2,1)}, bf16[32,64,128]{2,1,0:T(8,128)(2,1)S(1)}, u32[]{:S(2)}, u32[]{:S(2)}) collective-permute-start(bf16[32,64,128]{2,1,0:T(8,128)(2,1)} %collective-permute-done.7.refs_5_), channel_id=1, source_target_pairs={{0,96},{16,112},{32,0},{48,16},{64,32},{80,48},{96,64},{112,80},{1... | collective-permute-start | bytes 1572872 | tf_op jit(solution)/shard_map/ppermute | solution.py:396
  110.1 8.2 %copy-start.2 = (s32[128,1]{0,1:T(1,128)S(1)}, s32[128,1]{0,1:T(1,128)}, u32[]{:S(2)}) copy-start(s32[128,1]{0,1:T(1,128)} %param.8) | copy-start | bytes 1540
  113.0 19.3 %all-to-all-start.3 = ((bf16[128,4,512]{2,1,0:T(4,128)(2,1)}), bf16[128,4,512]{2,1,0:T(4,128)(2,1)S(1)}, u32[]{:S(2)}, u32[]{:S(2)}) async-start(bf16[128,4,512]{2,1,0:T(4,128)(2,1)} %shard_map.56), calls=%async_computation.3 | async-start | bytes 1048576 | tf_op jit(solution)/shard_map/all_to_all | solution.py:497

commit v7 on v6

--- a/solution.py
+++ b/solution.py
@@ -191,7 +191,12 @@
 def whiten(core, samples, twiddle, upper, lower, per):
     rows = samples.shape[1]
     out = jax.ShapeDtypeStruct((rows, NSEG * HALF_ROWS, LANES), jnp.bfloat16)
-    spec = pl.BlockSpec((rows, per * HALF_ROWS, LANES), lambda s, c: (0, s, 0))
+    resident = pl.BlockSpec(memory_space=pltpu.VMEM)
+    if per == NSEG:
+        spec = samples_spec = resident
+    else:
+        spec = pl.BlockSpec((rows, per * HALF_ROWS, LANES), lambda s, c: (0, s, 0))
+        samples_spec = pl.BlockSpec((per * SIDE, rows, SEGLEN // SIDE), lambda s, c: (s, 0, 0))
     count = RADIX // 2 + 1
     return pl.pallas_call(
         whiten_kernel,
@@ -200,10 +205,10 @@
             num_scalar_prefetch=1,
             grid=(NSEG // per,),
             in_specs=[
-                pl.BlockSpec((per * SIDE, rows, SEGLEN // SIDE), lambda s, c: (s, 0, 0)),
-                pl.BlockSpec((2, RADIX, INNER), lambda s, c: (0, 0, 0)),
-                pl.BlockSpec((2 * INNER, 4 * LANES), lambda s, c: (0, 0)),
-                pl.BlockSpec((2 * INNER, 4 * LANES), lambda s, c: (0, 0)),
+                samples_spec,
+                resident,
+                resident,
+                resident,
             ],
             out_specs=(spec, spec),
             scratch_shapes=[pltpu.VMEM((count * rows, 2 * INNER), jnp.bfloat16)] * (2 * per),

time: 134 us -> 134 us (level)
  no operation moved by 1% of the time
where the time goes in v7:
time: 134 us; the launch traced here: 133 us
  waiting for transfers between devices  47.9 us (36%)
  starting transfers between devices  46.4 us (35%)
  Pallas kernels  25.6 us (19%)
  other arithmetic  11.5 us (9%)
    ppermute x9, waiting for transfers between devices, shift(): lax.ppermute(value, 'gx', [(g, (g + 2 * step) % (2 * SIDE)) for g in rang...  17.9 us
    ppermute x9, starting transfers between devices, shift(): lax.ppermute(value, 'gx', [(g, (g + 2 * step) % (2 * SIDE)) for g in rang...  14.5 us
    all_to_all x1, waiting for transfers between devices, program(): lax.all_to_all(partial, ('gx', 'gy'), split_axis=0, concat_axis=0, tiled=...  13.9 us
    pallas_call x2, Pallas kernels, whiten(): pl.pallas_call(whiten_kernel, out_shape=(out, out), grid_spec=pltpu.Prefe...  12.5 us
    ppermute x3, starting transfers between devices, shift(): return lax.ppermute(value, 'gx', [(g, g ^ 1) for g in range(2 * SIDE)])  9.76 us
    all_to_all x1, waiting for transfers between devices, program(): first = lax.all_to_all(first, 'gy', split_axis=0, concat_axis=0, tiled=True)  9.72 us
    all_to_all x1, starting transfers between devices, program(): notes = lax.all_to_all(notes, 'gy', split_axis=0, concat_axis=0, tiled=True)  8.42 us
    pallas_call x2, Pallas kernels, correlate(): pl.pallas_call(kernel, out_shape=jax.ShapeDtypeStruct(shape, dtype), grid...  7.52 us
  transfers between devices with their start and end apart: 16, of which 8 were waited for; matrix products, arithmetic and copies ran while one was open for 9% of the time, Pallas kernels for 13%

profile of v7, /device:TPU:1, one launch (start us, length us, event | category | flops | bytes accessed | tf_op | source)
XLA Modules:
  0.0 133.4 jit_solution(849927082306558296)
XLA Ops:
  0.0 2.0 %pack.1 = s32[16,1,256]{2,1,0:T(1,128)} custom-call(s32[2]{0:T(128)} %ids_ref.1, s32[1,128]{1,0:T(1,128)} %bitcast.61, s32[1,128]{1,0:T(1,128)} %bitcast.64, s32[1,128]{1,0:T(1,128)} %bitcast.65), custom_call_target="tpu_custom_call" | custom-call | tf_op jit(solution)/shard_map/pack/pallas_call | solution.py:354
  2.0 8.4 %all-to-all-start = ((s32[16,1,256]{2,1,0:T(1,128)}), s32[16,1,256]{2,1,0:T(1,128)S(1)}, u32[]{:S(2)}, u32[]{:S(2)}) async-start(s32[16,1,256]{2,1,0:T(1,128)} %pack.1), calls=%async_computation | async-start | bytes 32768 | tf_op jit(solution)/shard_map/all_to_all | solution.py:425
  11.3 5.5 %all-to-all-done = s32[16,1,256]{2,1,0:T(1,128)S(1)} async-done(((s32[16,1,256]{2,1,0:T(1,128)}), s32[16,1,256]{2,1,0:T(1,128)S(1)}, u32[]{:S(2)}, u32[]{:S(2)}) %all-to-all-start) | async-done | bytes 16416 | tf_op jit(solution)/shard_map/all_to_all | solution.py:425
  17.5 3.6 %pick.1 = bf16[16,32,1024]{2,1,0:T(8,128)(2,1)} custom-call(s32[32]{0:T(128)} %sub.203.wanted_ref, f32[1024,1024]{1,0:T(8,128)} %raw_ref.1, f32[1,1024]{1,0:T(1,128)} %fusion.68.taper_ref), custom_call_target="tpu_custom_call" | custom-call | tf_op jit(solution)/shard_map/pick/pallas_call | solution.py:384
  21.1 3.7 %all-to-all-start.1 = ((bf16[16,32,1024]{2,1,0:T(8,128)(2,1)}), bf16[16,32,1024]{2,1,0:T(8,128)(2,1)S(1)}, u32[]{:S(2)}, u32[]{:S(2)}) async-start(bf16[16,32,1024]{2,1,0:T(8,128)(2,1)} %pick.1), calls=%async_computation.1 | async-start | bytes 2097152 | tf_op jit(solution)/shard_map/all_to_all | solution.py:429
  24.8 1.0 broadcast_multiply_fusion.1
  25.9 4.1 %multiply_convert_fusion = bf16[1024,1024]{1,0:T(8,128)(2,1)} fusion(f32[1024,1024]{1,0:T(8,128)} %raw_ref.1, f32[1024]{0:T(1024)S(1)} %fusion.61), kind=kLoop, calls=%fused_computation | loop fusion | flops 2097152 | bytes 6295552 | tf_op jit(solution)/shard_map/convert_element_type | solution.py:430
  30.0 9.7 %all-to-all-done.1.x_ref = bf16[16,32,1024]{2,1,0:T(8,128)(2,1)S(1)} async-done(((bf16[16,32,1024]{2,1,0:T(8,128)(2,1)}), bf16[16,32,1024]{2,1,0:T(8,128)(2,1)S(1)}, u32[]{:S(2)}, u32[]{:S(2)}) %all-to-all-start.1) | async-done | bytes 1048608 | tf_op jit(solution)/shard_map/all_to_all | solution.py:429
  39.7 4.8 %all-to-all-start.2 = ((bf16[16,64,1024]{2,1,0:T(8,128)(2,1)}), bf16[16,64,1024]{2,1,0:T(8,128)(2,1)}, u32[]{:S(2)}, u32[]{:S(2)}) async-start(bf16[16,64,1024]{2,1,0:T(8,128)(2,1)} %bitcast.50), calls=%async_computation.2 | async-start | bytes 4194304 | tf_op jit(solution)/shard_map/all_to_all | solution.py:431
  44.6 4.5 %whiten.2 = (bf16[32,64,128]{2,1,0:T(8,128)(2,1)S(1)}, bf16[32,64,128]{2,1,0:T(8,128)(2,1)}) custom-call(s32[1]{0:T(128)} %bitcast.12.core_ref, bf16[16,32,1024]{2,1,0:T(8,128)(2,1)S(1)} %all-to-all-done.1.x_ref, f32[2,16,256]{2,1,0:T(8,128)S(1)} %pad_maximum_fusion.1.tw_ref, bf16[512,512]{1,0:T(8,128)(2,1)S(1)} %fusion.11.upper_ref, ...), custom_call_target="tpu_custom_call" | custom-call | tf_op jit(solution)/shard_map/whiten/pallas_call | solution.py:201
  49.1 3.0 %collective-permute-start.4 = (bf16[32,64,128]{2,1,0:T(8,128)(2,1)}, bf16[32,64,128]{2,1,0:T(8,128)(2,1)S(1)}, u32[]{:S(2)}, u32[]{:S(2)}) collective-permute-start(bf16[32,64,128]{2,1,0:T(8,128)(2,1)} %get-tuple-element.15), channel_id=1, source_target_pairs={{0,16},{16,0},{32,48},{48,32},{64,80},{80,64},{96,112},{112,96},{1... | collective-permute-start | bytes 1572872 | tf_op jit(solution)/shard_map/ppermute | solution.py:400
  52.1 1.4 %collective-permute-start = (s32[16,128]{1,0:T(8,128)S(1)}, s32[16,128]{1,0:T(8,128)S(1)}, u32[]{:S(2)}, u32[]{:S(2)}) collective-permute-start(s32[16,128]{1,0:T(8,128)S(1)} %bitcast.53), channel_id=1, source_target_pairs={{0,32},{16,48},{32,64},{48,80},{64,96},{80,112},{96,0},{112,16},{1... | collective-permute-start | bytes 24584 | tf_op jit(solution)/shard_map/ppermute | solution.py:401
  53.5 2.6 %collective-permute-start.1 = (s32[16,128]{1,0:T(8,128)S(1)}, s32[16,128]{1,0:T(8,128)S(1)}, u32[]{:S(2)}, u32[]{:S(2)}) collective-permute-start(s32[16,128]{1,0:T(8,128)S(1)} %bitcast.54), channel_id=1, source_target_pairs={{0,64},{16,80},{32,96},{48,112},{64,0},{80,16},{96,32},{112,48},{1... | collective-permute-start | bytes 24584 | tf_op jit(solution)/shard_map/ppermute | solution.py:401
  56.1 1.1 collective-permute-start.2
  57.9 1.1 collective-permute-done.2
  59.0 1.3 collective-permute-start.3
  61.2 2.3 %collective-permute-start.11 = (bf16[32,64,128]{2,1,0:T(8,128)(2,1)S(1)}, bf16[32,64,128]{2,1,0:T(8,128)(2,1)S(1)}, u32[]{:S(2)}, u32[]{:S(2)}) collective-permute-start(bf16[32,64,128]{2,1,0:T(8,128)(2,1)S(1)} %get-tuple-element.18.refs_0_), channel_id=1, source_target_pairs={{0,96},{16,112},{32,0},{48,16},{64,32},{80,48},{96,64},{112,80},{1... | collective-permute-start | bytes 1572872 | tf_op jit(solution)/shard_map/ppermute | solution.py:401
  64.3 1.1 fusion.18
  65.4 2.9 %collective-permute-start.7 = (bf16[32,64,128]{2,1,0:T(8,128)(2,1)S(1)}, bf16[32,64,128]{2,1,0:T(8,128)(2,1)}, u32[]{:S(2)}, u32[]{:S(2)}) collective-permute-start(bf16[32,64,128]{2,1,0:T(8,128)(2,1)S(1)} %collective-permute-done.4.refs_1_), channel_id=1, source_target_pairs={{0,96},{16,112},{32,0},{48,16},{64,32},{80,48},{96,64},{112,80},{1... | collective-permute-start | bytes 1572872 | tf_op jit(solution)/shard_map/ppermute | solution.py:401
  68.3 2.1 %multiply_convert_fusion.2 = (bf16[1,8,128,512]{3,2,1,0:T(8,128)(2,1)}, bf16[1,8,128,512]{3,2,1,0:T(8,128)(2,1)}) fusion(f32[128,512]{1,0:T(8,128)S(1)} %get-tuple-element.24, f32[8,512]{1,0:T(8,128)S(1)} %get-tuple-element.23, f32[128,512]{1,0:T(8,128)S(1)} %get-tuple-element.22, f32[8,512]{1,0:T(8,128)S(1)} %get-tuple-element.21, ...), kind=kLoop, calls=%fused_computation.3 | loop fusion | flops 5242880 | bytes 2662400 | tf_op jit(solution)/shard_map/convert
  70.4 8.0 %whiten.3 = (bf16[64,64,128]{2,1,0:T(8,128)(2,1)S(1)}, bf16[64,64,128]{2,1,0:T(8,128)(2,1)S(1)}) custom-call(s32[1]{0:T(128)} %bitcast.12.core_ref, bf16[16,64,1024]{2,1,0:T(8,128)(2,1)} %all-to-all-done.2.x_ref, f32[2,16,256]{2,1,0:T(8,128)S(1)} %pad_maximum_fusion.1.tw_ref, bf16[512,512]{1,0:T(8,128)(2,1)S(1)} %fusion.11.upper_ref, ...), custom_call_target="tpu_custom_call" | custom-call | tf_op jit(solution)/shard_map/whiten/pallas_call | solution.py:201
  78.4 5.5 %collective-permute-start.9 = (bf16[64,64,128]{2,1,0:T(8,128)(2,1)S(1)}, bf16[64,64,128]{2,1,0:T(8,128)(2,1)S(1)}, u32[]{:S(2)}, u32[]{:S(2)}) collective-permute-start(bf16[64,64,128]{2,1,0:T(8,128)(2,1)S(1)} %get-tuple-element.20), channel_id=1, source_target_pairs={{0,16},{16,0},{32,48},{48,32},{64,80},{80,64},{96,112},{112,96},{1... | collective-permute-start | bytes 3145736 | tf_op jit(solution)/shard_map/ppermute | solution.py:400
  84.0 1.4 %collective-permute-start.10 = (bf16[32,64,128]{2,1,0:T(8,128)(2,1)S(1)}, bf16[32,64,128]{2,1,0:T(8,128)(2,1)S(1)}, u32[]{:S(2)}, u32[]{:S(2)}) collective-permute-start(bf16[32,64,128]{2,1,0:T(8,128)(2,1)S(1)} %collective-permute-done.4.refs_1_), channel_id=1, source_target_pairs={{0,32},{16,48},{32,64},{48,80},{64,96},{80,112},{96,0},{112,16},{1... | collective-permute-start | bytes 1572872 | tf_op jit(solution)/shard_map/ppermute | solution.py:401
  85.3 1.3 collective-permute-start.6
  87.5 1.6 %collective-permute-start.8 = (bf16[32,64,128]{2,1,0:T(8,128)(2,1)}, bf16[32,64,128]{2,1,0:T(8,128)(2,1)S(1)}, u32[]{:S(2)}, u32[]{:S(2)}) collective-permute-start(bf16[32,64,128]{2,1,0:T(8,128)(2,1)} %collective-permute-done.7.refs_5_), channel_id=1, source_target_pairs={{0,96},{16,112},{32,0},{48,16},{64,32},{80,48},{96,64},{112,80},{1... | collective-permute-start | bytes 1572872 | tf_op jit(solution)/shard_map/ppermute | solution.py:401
  89.4 9.5 %collective-permute-done.10.refs_3_ = bf16[32,64,128]{2,1,0:T(8,128)(2,1)S(1)} collective-permute-done((bf16[32,64,128]{2,1,0:T(8,128)(2,1)S(1)}, bf16[32,64,128]{2,1,0:T(8,128)(2,1)S(1)}, u32[]{:S(2)}, u32[]{:S(2)}) %collective-permute-start.10) | collective-permute-done | bytes 524320 | tf_op jit(solution)/shard_map/ppermute | solution.py:401
  98.9 4.6 %shard_map.55.refs_5_ = f32[512,512]{1,0:T(8,128)S(1)} custom-call(s32[2]{0:T(128)S(1)} %get-tuple-element.33.count_ref, s32[512]{0:T(512)S(1)} %get-tuple-element.50.src_ref, s32[512]{0:T(512)S(1)} %get-tuple-element.51.rcv_ref, s32[512]{0:T(512)S(1)} %get-tuple-element.49.slot_ref, bf16[32,64,128]{2,1,0:T(8,128)(2,1)S(1)} %get-tuple-element.18.refs_0_, ...), custom_call_target="tpu_custom_call" | custom-call | tf_op jit(solution)/shard_map/pallas_call | solution.py:318
  103.5 6.6 %collective-permute-done.6.refs_0_ = bf16[32,64,128]{2,1,0:T(8,128)(2,1)S(1)} collective-permute-done((bf16[32,64,128]{2,1,0:T(8,128)(2,1)S(1)}, bf16[32,64,128]{2,1,0:T(8,128)(2,1)S(1)}, u32[]{:S(2)}, u32[]{:S(2)}) %collective-permute-start.6) | collective-permute-done | bytes 524320 | tf_op jit(solution)/shard_map/ppermute | solution.py:401
  110.1 2.9 %shard_map.56 = bf16[128,4,512]{2,1,0:T(4,128)(2,1)} custom-call(s32[2]{0:T(128)S(1)} %get-tuple-element.34.count_ref, s32[512]{0:T(512)S(1)} %get-tuple-element.53.src_ref, s32[512]{0:T(512)S(1)} %get-tuple-element.54.rcv_ref, s32[512]{0:T(512)S(1)} %get-tuple-element.52.slot_ref, bf16[32,64,128]{2,1,0:T(8,128)(2,1)S(1)} %collective-permute-done.6.refs_0_, ...), custom_call_target="tpu_custom_call" | custom-call | tf_op jit(solution)/shard_map/pallas_call | solution.py:318
  113.0 5.2 %all-to-all-start.3 = ((bf16[128,4,512]{2,1,0:T(4,128)(2,1)}), bf16[128,4,512]{2,1,0:T(4,128)(2,1)S(1)}, u32[]{:S(2)}, u32[]{:S(2)}) async-start(bf16[128,4,512]{2,1,0:T(4,128)(2,1)} %shard_map.56), calls=%async_computation.3 | async-start | bytes 1048576 | tf_op jit(solution)/shard_map/all_to_all | solution.py:502
  118.4 13.9 %all-to-all-done.3 = bf16[128,4,512]{2,1,0:T(4,128)(2,1)S(1)} async-done(((bf16[128,4,512]{2,1,0:T(4,128)(2,1)}), bf16[128,4,512]{2,1,0:T(4,128)(2,1)S(1)}, u32[]{:S(2)}, u32[]{:S(2)}) %all-to-all-start.3) | async-done | bytes 524320 | tf_op jit(solution)/shard_map/all_to_all | solution.py:502
  132.5 1.0 fusion.7
  (61 shorter events, 5.5 us)
Async XLA Ops:
  2.0 14.9 %all-to-all-start = ((s32[16,1,256]{2,1,0:T(1,128)}), s32[16,1,256]{2,1,0:T(1,128)S(1)}, u32[]{:S(2)}, u32[]{:S(2)}) async-start(s32[16,1,256]{2,1,0:T(1,128)} %pack.1), calls=%async_computation | async-start | bytes 32768 | tf_op jit(solution)/shard_map/all_to_all | solution.py:425
  21.1 18.7 %all-to-all-start.1 = ((bf16[16,32,1024]{2,1,0:T(8,128)(2,1)}), bf16[16,32,1024]{2,1,0:T(8,128)(2,1)S(1)}, u32[]{:S(2)}, u32[]{:S(2)}) async-start(bf16[16,32,1024]{2,1,0:T(8,128)(2,1)} %pick.1), calls=%async_computation.1 | async-start | bytes 2097152 | tf_op jit(solution)/shard_map/all_to_all | solution.py:429
  39.7 30.6 %all-to-all-start.2 = ((bf16[16,64,1024]{2,1,0:T(8,128)(2,1)}), bf16[16,64,1024]{2,1,0:T(8,128)(2,1)}, u32[]{:S(2)}, u32[]{:S(2)}) async-start(bf16[16,64,1024]{2,1,0:T(8,128)(2,1)} %bitcast.50), calls=%async_computation.2 | async-start | bytes 4194304 | tf_op jit(solution)/shard_map/all_to_all | solution.py:431
  49.1 14.3 %collective-permute-start.4 = (bf16[32,64,128]{2,1,0:T(8,128)(2,1)}, bf16[32,64,128]{2,1,0:T(8,128)(2,1)S(1)}, u32[]{:S(2)}, u32[]{:S(2)}) collective-permute-start(bf16[32,64,128]{2,1,0:T(8,128)(2,1)} %get-tuple-element.15), channel_id=1, source_target_pairs={{0,16},{16,0},{32,48},{48,32},{64,80},{80,64},{96,112},{112,96},{1... | collective-permute-start | bytes 1572872 | tf_op jit(solution)/shard_map/ppermute | solution.py:400
  52.1 5.1 %collective-permute-start = (s32[16,128]{1,0:T(8,128)S(1)}, s32[16,128]{1,0:T(8,128)S(1)}, u32[]{:S(2)}, u32[]{:S(2)}) collective-permute-start(s32[16,128]{1,0:T(8,128)S(1)} %bitcast.53), channel_id=1, source_target_pairs={{0,32},{16,48},{32,64},{48,80},{64,96},{80,112},{96,0},{112,16},{1... | collective-permute-start | bytes 24584 | tf_op jit(solution)/shard_map/ppermute | solution.py:401
  53.5 4.4 %collective-permute-start.1 = (s32[16,128]{1,0:T(8,128)S(1)}, s32[16,128]{1,0:T(8,128)S(1)}, u32[]{:S(2)}, u32[]{:S(2)}) collective-permute-start(s32[16,128]{1,0:T(8,128)S(1)} %bitcast.54), channel_id=1, source_target_pairs={{0,64},{16,80},{32,96},{48,112},{64,0},{80,16},{96,32},{112,48},{1... | collective-permute-start | bytes 24584 | tf_op jit(solution)/shard_map/ppermute | solution.py:401
  56.1 2.9 %collective-permute-start.2 = (s32[16,128]{1,0:T(8,128)S(1)}, s32[16,128]{1,0:T(8,128)S(1)}, u32[]{:S(2)}, u32[]{:S(2)}) collective-permute-start(s32[16,128]{1,0:T(8,128)S(1)} %bitcast.55), channel_id=1, source_target_pairs={{0,96},{16,112},{32,0},{48,16},{64,32},{80,48},{96,64},{112,80},{1... | collective-permute-start | bytes 24584 | tf_op jit(solution)/shard_map/ppermute | solution.py:401
  59.0 2.2 %collective-permute-start.3 = (s32[4,16,128]{2,1,0:T(8,128)S(1)}, s32[4,16,128]{2,1,0:T(8,128)S(1)}, u32[]{:S(2)}, u32[]{:S(2)}) collective-permute-start(s32[4,16,128]{2,1,0:T(8,128)S(1)} %get-tuple-element.44), channel_id=1, source_target_pairs={{0,16},{16,0},{32,48},{48,32},{64,80},{80,64},{96,112},{112,96},{1... | collective-permute-start | bytes 98312 | tf_op jit(solution)/shard_map/ppermute | solution.py:400
  61.2 28.2 %collective-permute-start.11 = (bf16[32,64,128]{2,1,0:T(8,128)(2,1)S(1)}, bf16[32,64,128]{2,1,0:T(8,128)(2,1)S(1)}, u32[]{:S(2)}, u32[]{:S(2)}) collective-permute-start(bf16[32,64,128]{2,1,0:T(8,128)(2,1)S(1)} %get-tuple-element.18.refs_0_), channel_id=1, source_target_pairs={{0,96},{16,112},{32,0},{48,16},{64,32},{80,48},{96,64},{112,80},{1... | collective-permute-start | bytes 1572872 | tf_op jit(solution)/shard_map/ppermute | solution.py:401
  63.4 21.9 %collective-permute-start.5 = (bf16[32,64,128]{2,1,0:T(8,128)(2,1)S(1)}, bf16[32,64,128]{2,1,0:T(8,128)(2,1)S(1)}, u32[]{:S(2)}, u32[]{:S(2)}) collective-permute-start(bf16[32,64,128]{2,1,0:T(8,128)(2,1)S(1)} %get-tuple-element.18.refs_0_), channel_id=1, source_target_pairs={{0,32},{16,48},{32,64},{48,80},{64,96},{80,112},{96,0},{112,16},{1... | collective-permute-start | bytes 1572872 | tf_op jit(solution)/shard_map/ppermute | solution.py:401
  65.4 22.2 %collective-permute-start.7 = (bf16[32,64,128]{2,1,0:T(8,128)(2,1)S(1)}, bf16[32,64,128]{2,1,0:T(8,128)(2,1)}, u32[]{:S(2)}, u32[]{:S(2)}) collective-permute-start(bf16[32,64,128]{2,1,0:T(8,128)(2,1)S(1)} %collective-permute-done.4.refs_1_), channel_id=1, source_target_pairs={{0,96},{16,112},{32,0},{48,16},{64,32},{80,48},{96,64},{112,80},{1... | collective-permute-start | bytes 1572872 | tf_op jit(solution)/shard_map/ppermute | solution.py:401
  70.4 16.4 %copy-start = (bf16[1,8,128,512]{3,2,1,0:T(8,128)(2,1)S(1)}, bf16[1,8,128,512]{3,2,1,0:T(8,128)(2,1)}, u32[]{:S(2)}) copy-start(bf16[1,8,128,512]{3,2,1,0:T(8,128)(2,1)} %get-tuple-element.39) | copy-start | bytes 3145732
  70.4 16.5 %copy-start.1 = (bf16[1,8,128,512]{3,2,1,0:T(8,128)(2,1)S(1)}, bf16[1,8,128,512]{3,2,1,0:T(8,128)(2,1)}, u32[]{:S(2)}) copy-start(bf16[1,8,128,512]{3,2,1,0:T(8,128)(2,1)} %get-tuple-element.40) | copy-start | bytes 3145732
  78.4 20.5 %collective-permute-start.9 = (bf16[64,64,128]{2,1,0:T(8,128)(2,1)S(1)}, bf16[64,64,128]{2,1,0:T(8,128)(2,1)S(1)}, u32[]{:S(2)}, u32[]{:S(2)}) collective-permute-start(bf16[64,64,128]{2,1,0:T(8,128)(2,1)S(1)} %get-tuple-element.20), channel_id=1, source_target_pairs={{0,16},{16,0},{32,48},{48,32},{64,80},{80,64},{96,112},{112,96},{1... | collective-permute-start | bytes 3145736 | tf_op jit(solution)/shard_map/ppermute | solution.py:400
  84.0 14.9 %collective-permute-start.10 = (bf16[32,64,128]{2,1,0:T(8,128)(2,1)S(1)}, bf16[32,64,128]{2,1,0:T(8,128)(2,1)S(1)}, u32[]{:S(2)}, u32[]{:S(2)}) collective-permute-start(bf16[32,64,128]{2,1,0:T(8,128)(2,1)S(1)} %collective-permute-done.4.refs_1_), channel_id=1, source_target_pairs={{0,32},{16,48},{32,64},{48,80},{64,96},{80,112},{96,0},{112,16},{1... | collective-permute-start | bytes 1572872 | tf_op jit(solution)/shard_map/ppermute | solution.py:401
  85.3 24.7 %collective-permute-start.6 = (bf16[32,64,128]{2,1,0:T(8,128)(2,1)S(1)}, bf16[32,64,128]{2,1,0:T(8,128)(2,1)S(1)}, u32[]{:S(2)}, u32[]{:S(2)}) collective-permute-start(bf16[32,64,128]{2,1,0:T(8,128)(2,1)S(1)} %collective-permute-done.5.refs_2_), channel_id=1, source_target_pairs={{0,32},{16,48},{32,64},{48,80},{64,96},{80,112},{96,0},{112,16},{1... | collective-permute-start | bytes 1572872 | tf_op jit(solution)/shard_map/ppermute | solution.py:401
  87.5 22.5 %collective-permute-start.8 = (bf16[32,64,128]{2,1,0:T(8,128)(2,1)}, bf16[32,64,128]{2,1,0:T(8,128)(2,1)S(1)}, u32[]{:S(2)}, u32[]{:S(2)}) collective-permute-start(bf16[32,64,128]{2,1,0:T(8,128)(2,1)} %collective-permute-done.7.refs_5_), channel_id=1, source_target_pairs={{0,96},{16,112},{32,0},{48,16},{64,32},{80,48},{96,64},{112,80},{1... | collective-permute-start | bytes 1572872 | tf_op jit(solution)/shard_map/ppermute | solution.py:401
  110.1 8.2 %copy-start.2 = (s32[128,1]{0,1:T(1,128)S(1)}, s32[128,1]{0,1:T(1,128)}, u32[]{:S(2)}) copy-start(s32[128,1]{0,1:T(1,128)} %param.8) | copy-start | bytes 1540
  113.0 19.3 %all-to-all-start.3 = ((bf16[128,4,512]{2,1,0:T(4,128)(2,1)}), bf16[128,4,512]{2,1,0:T(4,128)(2,1)S(1)}, u32[]{:S(2)}, u32[]{:S(2)}) async-start(bf16[128,4,512]{2,1,0:T(4,128)(2,1)} %shard_map.56), calls=%async_computation.3 | async-start | bytes 1048576 | tf_op jit(solution)/shard_map/all_to_all | solution.py:502
